TPU v7x, 256 devices: a whole 4x4x8 slice. The times are simulated.
256 devices in a mesh: layer: 32 (over y, z), xs: 8 (over x, core).
Axes of the slice: x: 4, y: 4, z: 8, core: 2. Of those that a mesh axis runs over, the one named last changes fastest.
Arguments:
- probes: float32 [64, 32, 16, 640], P('layer', None, 'xs'), may hold values from -6 to 6
- potential: float32 [64, 16, 640], P('layer', 'xs'), may hold values from -1 to 1
- projector: bfloat16 [64, 512, 1280], P('layer', 'xs'), may hold values from -0.15625 to 0.15625
- intersection_ids: int32 [64, 512], P('layer', 'xs'), may hold values from 0 to 255
- strength: float32 [64, 256], P('layer'), may hold values from -2 to 2
- decay_rates: float32 [64, 32], P('layer'), may hold values from 0.3 to 1
- contour_nodes: float32 [4], replicated, may hold values from -1 to 3
- node_weights: float32 [4], replicated, may hold values from 0.5 to 1.5
Outputs:
- moments: float32 [2, 64, 32, 16, 640], P(None, 'layer', None, 'xs')
All inputs are finite; a program needn't handle non-finite values.
Results may differ from a plain program's by a relative error of at most 0.00059.
Values sent between devices are 32-bit elements; how exact they have to be, the bound alone decides.
A program may use at most 64 MiB of HBM per device.

v0:
```python
import jax
import jax.numpy as jnp
from jax import lax
from jax.sharding import PartitionSpec as P

NPROJ = 256


FAR = -1.0 / 12.0
NEAR = 4.0 / 3.0
CENTER = -2.5


def carried_in(part, axis, combine, identity, reverse):
    count = lax.axis_size(axis)
    place = lax.axis_index(axis)
    ahead = count - 1 - place if reverse else place
    gathered = jax.tree.map(lambda a: lax.all_gather(a, axis), part)
    state = jax.tree.map(lambda a, e: jnp.zeros_like(a) + jnp.asarray(e, a.dtype), part, identity)

    def one(lap, state):
        source = count - 1 - lap if reverse else lap
        return combine(
            state, jax.tree.map(lambda a: lax.dynamic_index_in_dim(a, source, 0, False), gathered)
        )

    return lax.fori_loop(0, ahead, one, state)


def with_halo(cells, sides, width):
    for axis, dim in sides:
        count = lax.axis_size(axis)
        ends = count - 1
        head = lax.slice_in_dim(cells, 0, width, axis=dim)
        tail = lax.slice_in_dim(cells, cells.shape[dim] - width, cells.shape[dim], axis=dim)
        cells = jnp.concatenate(
            [
                lax.ppermute(tail, axis, [(i, (i + 1) % count) for i in range(ends)]),
                cells,
                lax.ppermute(head, axis, [((i + 1) % count, i) for i in range(ends)]),
            ],
            axis=dim,
        )
    return cells


def second_along(padded, axis, count):

    def piece(offset):
        return lax.slice_in_dim(padded, 2 + offset, 2 + offset + count, axis=axis)

    return FAR * (piece(-2) + piece(2)) + NEAR * (piece(-1) + piece(1)) + CENTER * piece(0)


def combine(earlier, later):
    return (earlier[0] * later[0], later[0][:, None, None] * earlier[1] + later[1])


def scan_sweeps(forcing, decay_rates):
    count = forcing.shape[1]
    zero = jnp.zeros_like(forcing[:, 0])
    through = jnp.prod(decay_rates, axis=0)
    state = zero
    ahead_list = []
    for index in range(count):
        rate = decay_rates[index][:, None, None]
        state = rate * state + (1.0 - rate) * forcing[:, index]
        ahead_list.append(state)
    ahead_zero = jnp.stack(ahead_list, axis=1)
    entering = carried_in(
        (through, ahead_zero[:, -1]), "layer", combine, (jnp.ones_like(through), zero), False
    )[1]
    lower_prod = jnp.cumprod(decay_rates, axis=0)
    ahead = ahead_zero + lower_prod[None, :, :, None, None] * entering[:, None]
    state = zero
    back_list = []
    for index in reversed(range(count)):
        rate = decay_rates[index][:, None, None]
        state = rate * state + (1.0 - rate) * ahead[:, index]
        back_list.append(state)
    back_zero = jnp.stack(back_list[::-1], axis=1)
    from_above = carried_in(
        (through, back_zero[:, 0]), "layer", combine, (jnp.ones_like(through), zero), True
    )[1]
    upper_prod = jnp.cumprod(decay_rates[::-1], axis=0)[::-1]
    return back_zero + upper_prod[None, :, :, None, None] * from_above[:, None]


def run_sweeps(forcing, decay_rates):
    return scan_sweeps(forcing, decay_rates)


def shards(
    probes,
    potential,
    projector,
    intersection_ids,
    strength,
    decay_rates,
    contour_nodes,
    node_weights,
):
    layers, columns, rows, depth = probes.shape
    padded = with_halo(probes, (("layer", 0), ("xs", 2)), 2)
    across = jnp.pad(probes, ((0, 0), (0, 0), (0, 0), (2, 2)))
    laplace = second_along(padded[:, :, 2:-2, :], 0, layers)
    laplace = laplace + second_along(padded[2:-2], 2, rows)
    laplace = laplace + second_along(across, 3, depth)
    rounded = probes.astype(jnp.bfloat16).reshape(layers, columns, rows * depth)
    slot_coef = jnp.einsum("lsp,lcp->lsc", projector, rounded, preferred_element_type=jnp.float32)
    onehot = (intersection_ids[:, :, None] == jnp.arange(NPROJ, dtype=jnp.int32)).astype(
        jnp.float32
    )
    partial_coef = jnp.einsum("lsq,lsc->lqc", onehot, slot_coef, precision=lax.Precision.HIGHEST)
    coef = lax.psum(partial_coef, "xs")
    scaled = (strength[:, :, None] * coef).astype(jnp.bfloat16)
    slot_back = jnp.einsum(
        "lsq,lqc->lsc", onehot.astype(jnp.bfloat16), scaled, preferred_element_type=jnp.float32
    ).astype(jnp.bfloat16)
    projected = jnp.einsum(
        "lsp,lsc->lcp", projector, slot_back, preferred_element_type=jnp.float32
    ).reshape(layers, columns, rows, depth)
    hamil = -0.5 * laplace + potential[:, None] * probes + projected
    forcing = hamil[None] - contour_nodes[:, None, None, None, None] * probes[None]
    swept = run_sweeps(forcing, decay_rates)
    first = jnp.sum(node_weights[:, None, None, None, None] * swept, axis=0)
    second = jnp.sum((node_weights * contour_nodes)[:, None, None, None, None] * swept, axis=0)
    return jnp.stack([first, second])


def solution(mesh):
    in_specs = (
        P("layer", None, "xs", None),
        P("layer", "xs", None),
        P("layer", "xs", None),
        P("layer", "xs"),
        P("layer", None),
        P("layer", None),
        P(),
        P(),
    )
    out_specs = P(None, "layer", None, "xs", None)
    return jax.shard_map(shards, mesh=mesh, in_specs=in_specs, out_specs=out_specs, check_vma=False)
```

profile of v0, /device:TPU:32, one launch (start us, length us, event | category | flops | bytes accessed | tf_op | source)
XLA Modules:
  0.0 553.8 jit_solution(769351655144849599)
XLA Ops:
  6.5 3.9 collective-permute-start
  10.5 2.0 collective-permute-start.1
  12.5 5.7 %collective-permute-done = f32[2,32,2,640]{3,2,1,0:T(2,128)S(1)} collective-permute-done((f32[2,32,2,640]{3,2,1,0:T(2,128)}, f32[2,32,2,640]{3,2,1,0:T(2,128)S(1)}, u32[]{:S(2)}, u32[]{:S(2)}) %collective-permute-start) | collective-permute-done | bytes 327712 | tf_op jit(solution)/shard_map/ppermute | solution.py:38
  18.3 2.0 constant_dynamic-update-slice_fusion.1
  20.3 1.7 collective-permute-done.1
  22.0 1.3 collective-permute-start.3
  23.3 4.0 collective-permute-start.2
  27.3 1.0 reshape.100
  28.6 0.9 fusion.21
  30.3 64.9 %all-reduce.4.cloned.1.call-done = f32[2,256,32]{1,2,0:T(8,128)} async-done(((f32[2,256,32]{1,2,0:T(8,128)}), f32[2,256,32]{1,2,0:T(8,128)}) %all-reduce.4.cloned.1.call-update) | async-done | bytes 65552 | tf_op jit(solution)/shard_map/psum | solution.py:115
  95.2 1.9 fusion.2
  97.2 1.9 reshape.101
  99.1 3.2 add_add_fusion
  102.5 1.0 fusion.6
  105.3 72.3 %all-reduce.1 = f32[1024]{0:T(1024)S(1)} all-reduce(f32[1024]{0:T(1024)S(1)} %dynamic-update-slice), channel_id=2, replica_groups=mesh['layer'=32,'xs'=8] {'layer'}, use_global_device_ids=true, to_apply=%add.1 | all-reduce | flops 1024 | bytes 8192
  177.9 84.7 %all-gather.4.cloned.1.call-done = f32[32,4,32,2,640]{4,2,3,1,0:T(8,128)} async-done(((f32[1,4,32,2,640]{4,2,3,1,0:T(8,128)}), f32[32,4,32,2,640]{4,2,3,1,0:T(8,128)}) %all-gather.4.cloned.1.call-update) | async-done | bytes 20971536 | tf_op jit(solution)/shard_map/all_gather | solution.py:18
  262.7 2.1 while.26
  262.8 1.1 constant_dynamic-slice_fusion.4
  263.9 0.9 fusion.34
  265.1 1.0 fusion.3
  266.5 217.5 %all-gather.6.cloned.1.call-done = f32[32,4,32,2,640]{4,2,3,1,0:T(8,128)} async-done(((f32[1,4,32,2,640]{4,2,3,1,0:T(8,128)}), f32[32,4,32,2,640]{4,2,3,1,0:T(8,128)}) %all-gather.6.cloned.1.call-update) | async-done | bytes 20971536 | tf_op jit(solution)/shard_map/all_gather | solution.py:18
  484.1 61.4 %while.27 = (s32[]{:T(128)}, f32[4,32,2,640]{3,2,1,0:T(2,128)S(1)}, s32[]{:T(128)}, f32[32,32]{1,0:T(8,128)S(1)}, f32[32,4,32,2,640]{4,2,3,1,0:T(8,128)}, /*index=5*/s32[]{:T(128)}, s32[]{:T(128)}, s32[]{:T(128)}, s32[]{:T(128)}) while((s32[]{:T(128)}, f32[4,32,2,640]{3,2,1,0:T(2,128)S(1)}, s32[]{:T(128)}, f32[32,32]{1,0:T(8,128)S(1)}, ...), condition=%wide.region_7.8_spmd, body=%wide.region_6.7_spmd.sunk | while | flops 327686 | bytes 3277339 | solution.py:27
  484.1 1.1 constant_dynamic-slice_fusion.5
  485.3 0.9 fusion.35
  486.2 1.1 constant_dynamic-slice_fusion.5
  487.3 0.9 fusion.35
  488.2 1.1 constant_dynamic-slice_fusion.5
  489.4 0.9 fusion.35
  490.3 1.1 constant_dynamic-slice_fusion.5
  491.4 0.9 fusion.35
  492.3 1.1 constant_dynamic-slice_fusion.5
  493.5 0.9 fusion.35
  494.3 1.1 constant_dynamic-slice_fusion.5
  495.5 0.9 fusion.35
  496.4 1.1 constant_dynamic-slice_fusion.5
  497.6 0.9 fusion.35
  498.4 1.1 constant_dynamic-slice_fusion.5
  499.6 0.9 fusion.35
  500.5 1.1 constant_dynamic-slice_fusion.5
  501.6 0.9 fusion.35
  502.5 1.1 constant_dynamic-slice_fusion.5
  503.7 0.9 fusion.35
  504.6 1.1 constant_dynamic-slice_fusion.5
  505.7 0.9 fusion.35
  506.6 1.1 constant_dynamic-slice_fusion.5
  508.7 1.1 constant_dynamic-slice_fusion.5
  510.7 1.1 constant_dynamic-slice_fusion.5
  512.8 1.1 constant_dynamic-slice_fusion.5
  514.8 1.1 constant_dynamic-slice_fusion.5
  516.8 1.1 constant_dynamic-slice_fusion.5
  518.9 1.1 constant_dynamic-slice_fusion.5
  520.9 1.1 constant_dynamic-slice_fusion.5
  523.0 1.1 constant_dynamic-slice_fusion.5
  525.0 1.1 constant_dynamic-slice_fusion.5
  527.1 1.1 constant_dynamic-slice_fusion.5
  529.1 1.1 constant_dynamic-slice_fusion.5
  531.2 1.1 constant_dynamic-slice_fusion.5
  533.2 1.1 constant_dynamic-slice_fusion.5
  535.3 1.1 constant_dynamic-slice_fusion.5
  537.3 1.1 constant_dynamic-slice_fusion.5
  539.4 1.1 constant_dynamic-slice_fusion.5
  541.4 1.1 constant_dynamic-slice_fusion.5
  543.4 1.1 constant_dynamic-slice_fusion.5
  545.9 1.3 copy.21
  (105 shorter events, 20.8 us)
Async XLA Ops:
  6.5 21.8 %copy-start = (bf16[2,64,1280]{2,1,0:T(8,128)(2,1)S(1)}, bf16[2,64,1280]{2,1,0:T(8,128)(2,1)}, u32[]{:S(2)}) copy-start(bf16[2,64,1280]{2,1,0:T(8,128)(2,1)} %param.14) | copy-start | bytes 983044
  6.5 20.8 %copy-start.3 = (f32[2,32]{1,0:T(2,128)S(1)}, f32[2,32]{1,0:T(2,128)}, u32[]{:S(2)}) copy-start(f32[2,32]{1,0:T(2,128)} %param.17) | copy-start | bytes 772
  6.5 88.7 %all-reduce.4.cloned.1.call-start = ((), (), s32[]{:S(2)}) async-start(), calls=%async_computation | async-start | bytes 131072 | tf_op jit(solution)/shard_map/psum | solution.py:115
  6.5 11.7 %collective-permute-start = (f32[2,32,2,640]{3,2,1,0:T(2,128)}, f32[2,32,2,640]{3,2,1,0:T(2,128)S(1)}, u32[]{:S(2)}, u32[]{:S(2)}) collective-permute-start(f32[2,32,2,640]{3,2,1,0:T(2,128)} %param.12), channel_id=1, source_target_pairs={{0,8},{8,16},{16,24},{24,32},{32,40},{40,48},{48,56},{56,64},{64,7... | collective-permute-start | bytes 983048 | tf_op jit(solution)/shard_map/ppermute | solution.py:38
  10.5 11.5 %collective-permute-start.1 = (f32[2,32,2,640]{3,2,1,0:T(2,128)}, f32[2,32,2,640]{3,2,1,0:T(2,128)S(1)}, u32[]{:S(2)}, u32[]{:S(2)}) collective-permute-start(f32[2,32,2,640]{3,2,1,0:T(2,128)} %param.12), channel_id=1, source_target_pairs={{8,0},{16,8},{24,16},{32,24},{40,32},{48,40},{56,48},{64,56},{72,6... | collective-permute-start | bytes 983048 | tf_op jit(solution)/shard_map/ppermute | solution.py:40
  18.3 10.3 %copy-start.5 = (s32[2,64]{1,0:T(2,128)S(1)}, s32[2,64]{1,0:T(2,128)}, u32[]{:S(2)}) copy-start(s32[2,64]{1,0:T(2,128)} %param.15) | copy-start | bytes 1540
  18.3 11.3 %copy-start.1 = (f32[2,32,2,640]{3,2,1,0:T(2,128)S(1)}, f32[2,32,2,640]{3,2,1,0:T(2,128)}, u32[]{:S(2)}) copy-start(f32[2,32,2,640]{3,2,1,0:T(2,128)} %param.12) | copy-start | bytes 983044
  20.3 74.9 %copy-start.6 = (f32[2,256]{1,0:T(2,128)S(1)}, f32[2,256]{1,0:T(2,128)}, u32[]{:S(2)}) copy-start(f32[2,256]{1,0:T(2,128)} %param.16) | copy-start | bytes 6148
  22.0 77.0 %collective-permute-start.3 = (f32[6,32,2,640]{3,2,1,0:T(2,128)S(1)}, f32[6,32,2,640]{3,2,1,0:T(2,128)S(1)}, u32[]{:S(2)}, u32[]{:S(2)}) collective-permute-start(f32[6,32,2,640]{3,2,1,0:T(2,128)S(1)} %constant_dynamic-update-slice_fusion), channel_id=1, source_target_pairs={{1,0},{2,1},{3,2},{4,3},{5,4},{6,5},{7,6},{9,8},{10,9},{11,10},{12... | collective-permute-start | bytes 2949128 | tf_op jit(solution)/shard_map/ppermute | solution.py:40
  23.3 75.7 %collective-permute-start.2 = (f32[6,32,2,640]{3,2,1,0:T(2,128)S(1)}, f32[6,32,2,640]{3,2,1,0:T(2,128)}, u32[]{:S(2)}, u32[]{:S(2)}) collective-permute-start(f32[6,32,2,640]{3,2,1,0:T(2,128)S(1)} %constant_dynamic-update-slice_fusion), channel_id=1, source_target_pairs={{0,1},{1,2},{2,3},{3,4},{4,5},{5,6},{6,7},{8,9},{9,10},{10,11},{11... | collective-permute-start | bytes 2949128 | tf_op jit(solution)/shard_map/ppermute | solution.py:38
  28.4 70.7 %copy-start.4 = (f32[2,2,640]{2,1,0:T(2,128)S(1)}, f32[2,2,640]{2,1,0:T(2,128)}, u32[]{:S(2)}) copy-start(f32[2,2,640]{2,1,0:T(2,128)} %param.13) | copy-start | bytes 30724
  29.5 233.1 %all-gather.4.cloned.1.call-start = ((), (), s32[]{:S(2)}) async-start(), calls=%async_computation.1 | async-start | bytes 21626880 | tf_op jit(solution)/shard_map/all_gather | solution.py:18
  99.1 3.2 copy-start.2
  99.1 3.2 copy-start.7
  102.5 1.2 copy-start.9
  103.6 380.3 %all-gather.6.cloned.1.call-start = ((), (), s32[]{:S(2)}) async-start(), calls=%async_computation.2 | async-start | bytes 21626880 | tf_op jit(solution)/shard_map/all_gather | solution.py:18
  265.1 1.2 copy-start.8
Sparse Core Ops, SparseCore 0:
  29.6 65.5 all-reduce.3
  103.7 158.8 all-gather.3
  266.3 217.6 all-gather.5
where the time goes:
time: 560 us; the launch traced here: 554 us
  waiting for transfers between devices  374 us (67%)
  blocking collectives  72.3 us (13%)
  local copies, waits for them, and re-layouts  42.2 us (8%)
  other arithmetic  35.2 us (6%)
  between operations  14 us (2%)
  starting transfers between devices  11.3 us (2%)
    all_gather x2, waiting for transfers between devices, carried_in(): gathered = jax.tree.map(lambda a: lax.all_gather(a, axis), part)  302 us
    unnamed x1, blocking collectives  72.3 us
    psum x1, waiting for transfers between devices, shards(): coef = lax.psum(partial_coef, 'xs')  64.9 us
    dynamic_slice x31, local copies, waits for them, and re-layouts, one(): lax.dynamic_index_in_dim(a, source, 0, False)  35.2 us
    add x31, other arithmetic, combine(): later[0][:, None, None] * earlier[1] + later[1]  26.7 us
  transfers between devices with their start and end apart: 7, of which 5 were waited for; matrix products, arithmetic and copies ran while one was open for 2% of the time, Pallas kernels for 0%

commit v1 on v0

v1 whole, which is shorter than its diff:
```python
import jax
import jax.numpy as jnp
from jax import lax
from jax.sharding import PartitionSpec as P

NPROJ = 256


FAR = -1.0 / 12.0
NEAR = 4.0 / 3.0
CENTER = -2.5


def with_halo(cells, sides, width):
    for axis, dim in sides:
        count = lax.axis_size(axis)
        ends = count - 1
        head = lax.slice_in_dim(cells, 0, width, axis=dim)
        tail = lax.slice_in_dim(cells, cells.shape[dim] - width, cells.shape[dim], axis=dim)
        cells = jnp.concatenate(
            [
                lax.ppermute(tail, axis, [(i, (i + 1) % count) for i in range(ends)]),
                cells,
                lax.ppermute(head, axis, [((i + 1) % count, i) for i in range(ends)]),
            ],
            axis=dim,
        )
    return cells


def second_along(padded, axis, count):

    def piece(offset):
        return lax.slice_in_dim(padded, 2 + offset, 2 + offset + count, axis=axis)

    return FAR * (piece(-2) + piece(2)) + NEAR * (piece(-1) + piece(1)) + CENTER * piece(0)


def shifted(tree, axis, step, reverse):
    count = lax.axis_size(axis)
    if reverse:
        pairs = [(i + step, i) for i in range(count - step)]
    else:
        pairs = [(i, i + step) for i in range(count - step)]
    return lax.ppermute(tree, axis, pairs)


def carried(through, end, axis, reverse):
    count = lax.axis_size(axis)
    span = 1
    t, a = through, end
    while 2 * span < count:
        tr, ar = shifted((t, a), axis, span, reverse)
        a = a + t[None, :, None, None] * ar
        t = t * tr
        span *= 2
    near_t, near_a = shifted((t, a), axis, 1, reverse)
    if span + 1 < count:
        far_a = shifted(a, axis, span + 1, reverse)
        return near_a + near_t[None, :, None, None] * far_a
    return near_a


def sweeps(forcing, decay_rates):
    count = forcing.shape[1]
    rates = decay_rates[None, :, :, None, None]
    keep = 1.0 - rates
    state = jnp.zeros_like(forcing[:, 0])
    ahead_list = []
    for index in range(count):
        state = rates[:, index] * state + keep[:, index] * forcing[:, index]
        ahead_list.append(state)
    through = jnp.prod(decay_rates, axis=0)
    entering = carried(through, state, "layer", False)
    lower = jnp.cumprod(decay_rates, axis=0)
    ahead = [ahead_list[i] + lower[i][None, :, None, None] * entering for i in range(count)]
    state = jnp.zeros_like(forcing[:, 0])
    back_list = [None] * count
    for index in reversed(range(count)):
        state = rates[:, index] * state + keep[:, index] * ahead[index]
        back_list[index] = state
    from_above = carried(through, state, "layer", True)
    upper = jnp.cumprod(decay_rates[::-1], axis=0)[::-1]
    return jnp.stack(
        [back_list[i] + upper[i][None, :, None, None] * from_above for i in range(count)], axis=1
    )


def plane_sum(x, axis):
    count = lax.axis_size(axis)
    step = 1
    while step < count:
        x = x + lax.ppermute(x, axis, [(i, i ^ step) for i in range(count)])
        step *= 2
    return x


def shards(
    probes,
    potential,
    projector,
    intersection_ids,
    strength,
    decay_rates,
    contour_nodes,
    node_weights,
):
    layers, columns, rows, depth = probes.shape
    padded = with_halo(probes, (("layer", 0), ("xs", 2)), 2)
    across = jnp.pad(probes, ((0, 0), (0, 0), (0, 0), (2, 2)))
    laplace = second_along(padded[:, :, 2:-2, :], 0, layers)
    laplace = laplace + second_along(padded[2:-2], 2, rows)
    laplace = laplace + second_along(across, 3, depth)
    rounded = probes.astype(jnp.bfloat16).reshape(layers, columns, rows * depth)
    slot_coef = jnp.einsum("lsp,lcp->lsc", projector, rounded, preferred_element_type=jnp.float32)
    onehot = (intersection_ids[:, :, None] == jnp.arange(NPROJ, dtype=jnp.int32)).astype(
        jnp.float32
    )
    partial_coef = jnp.einsum("lsq,lsc->lqc", onehot, slot_coef, precision=lax.Precision.HIGHEST)
    coef = plane_sum(partial_coef, "xs")
    scaled = (strength[:, :, None] * coef).astype(jnp.bfloat16)
    slot_back = jnp.einsum(
        "lsq,lqc->lsc", onehot.astype(jnp.bfloat16), scaled, preferred_element_type=jnp.float32
    ).astype(jnp.bfloat16)
    projected = jnp.einsum(
        "lsp,lsc->lcp", projector, slot_back, preferred_element_type=jnp.float32
    ).reshape(layers, columns, rows, depth)
    hamil = -0.5 * laplace + potential[:, None] * probes + projected
    w0 = jnp.sum(node_weights)
    w1 = jnp.sum(node_weights * contour_nodes)
    w2 = jnp.sum(node_weights * contour_nodes * contour_nodes)
    forcing = jnp.stack([w0 * hamil - w1 * probes, w1 * hamil - w2 * probes])
    return sweeps(forcing, decay_rates)


def solution(mesh):
    in_specs = (
        P("layer", None, "xs", None),
        P("layer", "xs", None),
        P("layer", "xs", None),
        P("layer", "xs"),
        P("layer", None),
        P("layer", None),
        P(),
        P(),
    )
    out_specs = P(None, "layer", None, "xs", None)
    return jax.shard_map(shards, mesh=mesh, in_specs=in_specs, out_specs=out_specs, check_vma=False)
```

time: 560 us -> 215 us (0.38)
  the two profiles are of different devices: /device:TPU:32 before, /device:TPU:20 now
where the time goes in v1:
time: 215 us; the launch traced here: 214 us
  waiting for transfers between devices  109 us (51%)
  starting transfers between devices  87.8 us (41%)
  other arithmetic  12.2 us (6%)
  local copies, waits for them, and re-layouts  3.58 us (2%)
    ppermute x22, waiting for transfers between devices, shifted(): return lax.ppermute(tree, axis, pairs)  86.3 us
    ppermute x22, starting transfers between devices, shifted(): return lax.ppermute(tree, axis, pairs)  70.6 us
    ppermute x3, waiting for transfers between devices, plane_sum(): x = x + lax.ppermute(x, axis, [(i, i ^ step) for i in range(count)])  16 us
    ppermute x2, starting transfers between devices, with_halo(): lax.ppermute(head, axis, [((i + 1) % count, i) for i in range(ends)])  9.39 us
    another operation x2, other arithmetic, shards(): forcing = jnp.stack([w0 * hamil - w1 * probes, w1 * hamil - w2 * probes])  6.09 us
    ppermute x2, waiting for transfers between devices, with_halo(): lax.ppermute(tail, axis, [(i, (i + 1) % count) for i in range(ends)])  5.93 us
    ppermute x2, starting transfers between devices, with_halo(): lax.ppermute(tail, axis, [(i, (i + 1) % count) for i in range(ends)])  5.87 us
  transfers between devices with their start and end apart: 29, of which 20 were waited for; matrix products, arithmetic and copies ran while one was open for 3% of the time, Pallas kernels for 0%

profile of v1, /device:TPU:20, one launch (start us, length us, event | category | flops | bytes accessed | tf_op | source)
XLA Modules:
  0.0 214.3 jit_solution(1177613473676727116)
XLA Ops:
  0.0 3.9 %collective-permute-start = (f32[2,32,2,640]{3,2,1,0:T(2,128)}, f32[2,32,2,640]{3,2,1,0:T(2,128)S(1)}, u32[]{:S(2)}, u32[]{:S(2)}) collective-permute-start(f32[2,32,2,640]{3,2,1,0:T(2,128)} %param.8), channel_id=1, source_target_pairs={{0,8},{8,16},{16,24},{24,32},{32,40},{40,48},{48,56},{56,64},{64,7... | collective-permute-start | bytes 983048 | tf_op jit(solution)/shard_map/ppermute | solution.py:22
  4.0 5.7 %collective-permute-start.1 = (f32[2,32,2,640]{3,2,1,0:T(2,128)}, f32[2,32,2,640]{3,2,1,0:T(2,128)S(1)}, u32[]{:S(2)}, u32[]{:S(2)}) collective-permute-start(f32[2,32,2,640]{3,2,1,0:T(2,128)} %param.8), channel_id=1, source_target_pairs={{8,0},{16,8},{24,16},{32,24},{40,32},{48,40},{56,48},{64,56},{72,6... | collective-permute-start | bytes 983048 | tf_op jit(solution)/shard_map/ppermute | solution.py:24
  9.8 5.9 %collective-permute-done = f32[2,32,2,640]{3,2,1,0:T(2,128)S(1)} collective-permute-done((f32[2,32,2,640]{3,2,1,0:T(2,128)}, f32[2,32,2,640]{3,2,1,0:T(2,128)S(1)}, u32[]{:S(2)}, u32[]{:S(2)}) %collective-permute-start) | collective-permute-done | bytes 327712 | tf_op jit(solution)/shard_map/ppermute | solution.py:22
  15.7 0.8 constant_dynamic-update-slice_fusion.1
  16.6 0.4 collective-permute-done.1
  17.1 1.9 collective-permute-start.2
  19.0 3.6 %collective-permute-start.3 = (f32[6,32,2,640]{3,2,1,0:T(2,128)S(1)}, f32[6,32,2,640]{3,2,1,0:T(2,128)}, u32[]{:S(2)}, u32[]{:S(2)}) collective-permute-start(f32[6,32,2,640]{3,2,1,0:T(2,128)S(1)} %constant_dynamic-update-slice_fusion), channel_id=1, source_target_pairs={{1,0},{2,1},{3,2},{4,3},{5,4},{6,5},{7,6},{9,8},{10,9},{11,10},{12... | collective-permute-start | bytes 2949128 | tf_op jit(solution)/shard_map/ppermute | solution.py:24
  22.6 1.0 reshape.27
  23.9 0.5 copy-done.4
  24.4 0.2 fusion.20
  24.7 1.2 collective-permute-done.4
  26.0 1.3 collective-permute-start.5
  27.3 10.3 %collective-permute-done.5 = f32[2,256,32]{1,2,0:T(8,128)S(1)} collective-permute-done((f32[2,256,32]{1,2,0:T(8,128)S(1)}, f32[2,256,32]{1,2,0:T(8,128)S(1)}, u32[]{:S(2)}, u32[]{:S(2)}) %collective-permute-start.5) | collective-permute-done | bytes 65568 | tf_op jit(solution)/shard_map/ppermute | solution.py:93
  37.6 0.7 collective-permute-start.6
  38.2 0.7 multiply_reduce_fusion.1
  38.9 4.5 %collective-permute-done.6 = f32[2,256,32]{1,2,0:T(8,128)S(1)} collective-permute-done((f32[2,256,32]{1,2,0:T(8,128)S(1)}, f32[2,256,32]{1,2,0:T(8,128)S(1)}, u32[]{:S(2)}, u32[]{:S(2)}) %collective-permute-start.6) | collective-permute-done | bytes 65568 | tf_op jit(solution)/shard_map/ppermute | solution.py:93
  43.4 1.1 fusion
  44.5 1.9 reshape.28
  46.4 4.5 %subtract_bitcast_fusion.1 = (f32[1,2,32,2,640]{4,3,2,0,1:T(2,128)S(1)}, f32[2,32,2,640]{3,2,1,0:T(2,128)S(1)}) fusion(f32[2,32,2,640]{3,2,1,0:T(2,128)S(1)} %copy-done.1, f32[]{:T(128)} %get-tuple-element.5, f32[]{:T(128)} %get-tuple-element.7, f32[2,32,2,640]{3,2,1,0:T(2,128)} %reshape.28, f32[2,2,640]{2,1,0:T(2,128)S(1)} %copy-done.3, ...), kind=kLoop, calls=%fused_computation.42 | loop fusion | flops 2621440 | bytes 5581824 | tf_op jit(solution)/shard_map/stack | solution.py:132
  51.0 1.5 subtract_bitcast_fusion
  52.5 0.4 fusion.6
  52.9 2.3 %collective-permute-start.7 = (f32[2,32,2,640]{3,2,1,0:T(2,128)S(1)}, f32[2,32,2,640]{3,2,1,0:T(2,128)S(1)}, u32[]{:S(2)}, u32[]{:S(2)}) collective-permute-start(f32[2,32,2,640]{3,2,1,0:T(2,128)S(1)} %get-tuple-element.10), channel_id=1, source_target_pairs={{0,8},{8,16},{16,24},{24,32},{32,40},{40,48},{48,56},{56,64},{64,7... | collective-permute-start | bytes 983048 | tf_op jit(solution)/shard_map/ppermute | solution.py:45
  55.2 11.5 %collective-permute-done.7 = f32[2,32,2,640]{3,2,1,0:T(2,128)S(1)} collective-permute-done((f32[2,32,2,640]{3,2,1,0:T(2,128)S(1)}, f32[2,32,2,640]{3,2,1,0:T(2,128)S(1)}, u32[]{:S(2)}, u32[]{:S(2)}) %collective-permute-start.7) | collective-permute-done | bytes 327712 | tf_op jit(solution)/shard_map/ppermute | solution.py:45
  66.9 2.7 %collective-permute-start.9 = (f32[2,32,2,640]{3,2,1,0:T(2,128)S(1)}, f32[2,32,2,640]{3,2,1,0:T(2,128)S(1)}, u32[]{:S(2)}, u32[]{:S(2)}) collective-permute-start(f32[2,32,2,640]{3,2,1,0:T(2,128)S(1)} %multiply_add_fusion.11), channel_id=1, source_target_pairs={{0,16},{8,24},{16,32},{24,40},{32,48},{40,56},{48,64},{56,72},{64,... | collective-permute-start | bytes 983048 | tf_op jit(solution)/shard_map/ppermute | solution.py:45
  69.6 3.4 %collective-permute-start.19 = (f32[32]{0:T(128)S(1)}, f32[32]{0:T(128)S(1)}, u32[]{:S(2)}, u32[]{:S(2)}) collective-permute-start(f32[32]{0:T(128)S(1)} %get-tuple-element.24), channel_id=1, source_target_pairs={{8,0},{16,8},{24,16},{32,24},{40,32},{48,40},{56,48},{64,56},{72,6... | collective-permute-start | bytes 392 | tf_op jit(solution)/shard_map/ppermute | solution.py:45
  73.0 3.3 %collective-permute-start.8 = (f32[32]{0:T(128)S(1)}, f32[32]{0:T(128)S(1)}, u32[]{:S(2)}, u32[]{:S(2)}) collective-permute-start(f32[32]{0:T(128)S(1)} %get-tuple-element.24), channel_id=1, source_target_pairs={{0,8},{8,16},{16,24},{24,32},{32,40},{40,48},{48,56},{56,64},{64,7... | collective-permute-start | bytes 392 | tf_op jit(solution)/shard_map/ppermute | solution.py:45
  76.3 4.3 %collective-permute-done.8 = f32[32]{0:T(128)S(1)} collective-permute-done((f32[32]{0:T(128)S(1)}, f32[32]{0:T(128)S(1)}, u32[]{:S(2)}, u32[]{:S(2)}) %collective-permute-start.8) | collective-permute-done | bytes 160 | tf_op jit(solution)/shard_map/ppermute | solution.py:45
  80.6 8.0 %collective-permute-done.9 = f32[2,32,2,640]{3,2,1,0:T(2,128)S(1)} collective-permute-done((f32[2,32,2,640]{3,2,1,0:T(2,128)S(1)}, f32[2,32,2,640]{3,2,1,0:T(2,128)S(1)}, u32[]{:S(2)}, u32[]{:S(2)}) %collective-permute-start.9) | collective-permute-done | bytes 327712 | tf_op jit(solution)/shard_map/ppermute | solution.py:45
  88.8 5.3 %collective-permute-start.11 = (f32[2,32,2,640]{3,2,1,0:T(2,128)S(1)}, f32[2,32,2,640]{3,2,1,0:T(2,128)S(1)}, u32[]{:S(2)}, u32[]{:S(2)}) collective-permute-start(f32[2,32,2,640]{3,2,1,0:T(2,128)S(1)} %multiply_add_fusion.10), channel_id=1, source_target_pairs={{0,32},{8,40},{16,48},{24,56},{32,64},{40,72},{48,80},{56,88},{64,... | collective-permute-start | bytes 983048 | tf_op jit(solution)/shard_map/ppermute | solution.py:45
  94.1 1.9 collective-permute-start.10
  96.1 6.5 %collective-permute-done.10 = f32[32]{0:T(128)S(1)} collective-permute-done((f32[32]{0:T(128)S(1)}, f32[32]{0:T(128)S(1)}, u32[]{:S(2)}, u32[]{:S(2)}) %collective-permute-start.10) | collective-permute-done | bytes 160 | tf_op jit(solution)/shard_map/ppermute | solution.py:45
  102.6 1.7 collective-permute-done.11
  104.3 0.2 multiply_add_fusion.9
  104.5 3.0 %collective-permute-start.13 = (f32[2,32,2,640]{3,2,1,0:T(2,128)S(1)}, f32[2,32,2,640]{3,2,1,0:T(2,128)S(1)}, u32[]{:S(2)}, u32[]{:S(2)}) collective-permute-start(f32[2,32,2,640]{3,2,1,0:T(2,128)S(1)} %multiply_add_fusion.9), channel_id=1, source_target_pairs={{0,64},{8,72},{16,80},{24,88},{32,96},{40,104},{48,112},{56,120},{... | collective-permute-start | bytes 983048 | tf_op jit(solution)/shard_map/ppermute | solution.py:45
  107.5 4.5 %collective-permute-start.12 = (f32[32]{0:T(128)S(1)}, f32[32]{0:T(128)S(1)}, u32[]{:S(2)}, u32[]{:S(2)}) collective-permute-start(f32[32]{0:T(128)S(1)} %mul.333), channel_id=1, source_target_pairs={{0,32},{8,40},{16,48},{24,56},{32,64},{40,72},{48,80},{56,88},{64,... | collective-permute-start | bytes 392 | tf_op jit(solution)/shard_map/ppermute | solution.py:45
  112.0 5.8 %collective-permute-done.12 = f32[32]{0:T(128)S(1)} collective-permute-done((f32[32]{0:T(128)S(1)}, f32[32]{0:T(128)S(1)}, u32[]{:S(2)}, u32[]{:S(2)}) %collective-permute-start.12) | collective-permute-done | bytes 160 | tf_op jit(solution)/shard_map/ppermute | solution.py:45
  117.8 0.2 multiply_add_fusion.8
  118.0 1.9 collective-permute-start.14
  119.9 0.7 collective-permute-start.17
  120.6 1.9 collective-permute-start.15
  122.6 3.5 %collective-permute-done.15 = f32[32]{0:T(128)S(1)} collective-permute-done((f32[32]{0:T(128)S(1)}, f32[32]{0:T(128)S(1)}, u32[]{:S(2)}, u32[]{:S(2)}) %collective-permute-start.15) | collective-permute-done | bytes 160 | tf_op jit(solution)/shard_map/ppermute | solution.py:45
  126.1 2.8 %collective-permute-start.16 = (f32[32]{0:T(128)S(1)}, f32[32]{0:T(128)S(1)}, u32[]{:S(2)}, u32[]{:S(2)}) collective-permute-start(f32[32]{0:T(128)S(1)} %mul.339), channel_id=1, source_target_pairs={{0,8},{8,16},{16,24},{24,32},{32,40},{40,48},{48,56},{56,64},{64,7... | collective-permute-start | bytes 392 | tf_op jit(solution)/shard_map/ppermute | solution.py:45
  129.0 4.7 %collective-permute-done.16 = f32[32]{0:T(128)S(1)} collective-permute-done((f32[32]{0:T(128)S(1)}, f32[32]{0:T(128)S(1)}, u32[]{:S(2)}, u32[]{:S(2)}) %collective-permute-start.16) | collective-permute-done | bytes 160 | tf_op jit(solution)/shard_map/ppermute | solution.py:45
  133.7 0.6 multiply_add_fusion.5
  134.3 3.9 %collective-permute-start.18 = (f32[2,32,2,640]{3,2,1,0:T(2,128)S(1)}, f32[2,32,2,640]{3,2,1,0:T(2,128)S(1)}, u32[]{:S(2)}, u32[]{:S(2)}) collective-permute-start(f32[2,32,2,640]{3,2,1,0:T(2,128)S(1)} %get-tuple-element.8), channel_id=1, source_target_pairs={{8,0},{16,8},{24,16},{32,24},{40,32},{48,40},{56,48},{64,56},{72,6... | collective-permute-start | bytes 983048 | tf_op jit(solution)/shard_map/ppermute | solution.py:45
  138.2 6.8 %collective-permute-done.18 = f32[2,32,2,640]{3,2,1,0:T(2,128)S(1)} collective-permute-done((f32[2,32,2,640]{3,2,1,0:T(2,128)S(1)}, f32[2,32,2,640]{3,2,1,0:T(2,128)S(1)}, u32[]{:S(2)}, u32[]{:S(2)}) %collective-permute-start.18) | collective-permute-done | bytes 327712 | tf_op jit(solution)/shard_map/ppermute | solution.py:45
  145.2 3.1 %collective-permute-start.20 = (f32[2,32,2,640]{3,2,1,0:T(2,128)S(1)}, f32[2,32,2,640]{3,2,1,0:T(2,128)S(1)}, u32[]{:S(2)}, u32[]{:S(2)}) collective-permute-start(f32[2,32,2,640]{3,2,1,0:T(2,128)S(1)} %multiply_add_fusion.4), channel_id=1, source_target_pairs={{16,0},{24,8},{32,16},{40,24},{48,32},{56,40},{64,48},{72,56},{80,... | collective-permute-start | bytes 983048 | tf_op jit(solution)/shard_map/ppermute | solution.py:45
  148.3 15.9 %collective-permute-done.20 = f32[2,32,2,640]{3,2,1,0:T(2,128)S(1)} collective-permute-done((f32[2,32,2,640]{3,2,1,0:T(2,128)S(1)}, f32[2,32,2,640]{3,2,1,0:T(2,128)S(1)}, u32[]{:S(2)}, u32[]{:S(2)}) %collective-permute-start.20) | collective-permute-done | bytes 327712 | tf_op jit(solution)/shard_map/ppermute | solution.py:45
  164.5 1.9 collective-permute-start.22
  166.4 4.8 %collective-permute-start.21 = (f32[32]{0:T(128)S(1)}, f32[32]{0:T(128)S(1)}, u32[]{:S(2)}, u32[]{:S(2)}) collective-permute-start(f32[32]{0:T(128)S(1)} %get-tuple-element.30), channel_id=1, source_target_pairs={{16,0},{24,8},{32,16},{40,24},{48,32},{56,40},{64,48},{72,56},{80,... | collective-permute-start | bytes 392 | tf_op jit(solution)/shard_map/ppermute | solution.py:45
  171.2 3.9 %collective-permute-done.21 = f32[32]{0:T(128)S(1)} collective-permute-done((f32[32]{0:T(128)S(1)}, f32[32]{0:T(128)S(1)}, u32[]{:S(2)}, u32[]{:S(2)}) %collective-permute-start.21) | collective-permute-done | bytes 160 | tf_op jit(solution)/shard_map/ppermute | solution.py:45
  175.1 2.3 %collective-permute-done.22 = f32[2,32,2,640]{3,2,1,0:T(2,128)S(1)} collective-permute-done((f32[2,32,2,640]{3,2,1,0:T(2,128)S(1)}, f32[2,32,2,640]{3,2,1,0:T(2,128)S(1)}, u32[]{:S(2)}, u32[]{:S(2)}) %collective-permute-start.22) | collective-permute-done | bytes 327712 | tf_op jit(solution)/shard_map/ppermute | solution.py:45
  177.7 1.9 collective-permute-start.24
  179.6 4.8 %collective-permute-start.23 = (f32[32]{0:T(128)S(1)}, f32[32]{0:T(128)S(1)}, u32[]{:S(2)}, u32[]{:S(2)}) collective-permute-start(f32[32]{0:T(128)S(1)} %mul.355), channel_id=1, source_target_pairs={{32,0},{40,8},{48,16},{56,24},{64,32},{72,40},{80,48},{88,56},{96,... | collective-permute-start | bytes 392 | tf_op jit(solution)/shard_map/ppermute | solution.py:45
  184.4 4.5 %collective-permute-done.23 = f32[32]{0:T(128)S(1)} collective-permute-done((f32[32]{0:T(128)S(1)}, f32[32]{0:T(128)S(1)}, u32[]{:S(2)}, u32[]{:S(2)}) %collective-permute-start.23) | collective-permute-done | bytes 160 | tf_op jit(solution)/shard_map/ppermute | solution.py:45
  189.0 0.2 multiply_add_fusion.1
  189.2 11.9 %collective-permute-start.25 = (f32[2,32,2,640]{3,2,1,0:T(2,128)S(1)}, f32[2,32,2,640]{3,2,1,0:T(2,128)S(1)}, u32[]{:S(2)}, u32[]{:S(2)}) collective-permute-start(f32[2,32,2,640]{3,2,1,0:T(2,128)S(1)} %multiply_add_fusion.1), channel_id=1, source_target_pairs={{8,0},{16,8},{24,16},{32,24},{40,32},{48,40},{56,48},{64,56},{72,6... | collective-permute-start | bytes 983048 | tf_op jit(solution)/shard_map/ppermute | solution.py:45
  201.1 0.7 collective-permute-start.28
  201.8 1.9 collective-permute-start.26
  203.8 3.5 %collective-permute-done.26 = f32[32]{0:T(128)S(1)} collective-permute-done((f32[32]{0:T(128)S(1)}, f32[32]{0:T(128)S(1)}, u32[]{:S(2)}, u32[]{:S(2)}) %collective-permute-start.26) | collective-permute-done | bytes 160 | tf_op jit(solution)/shard_map/ppermute | solution.py:45
  207.3 1.9 collective-permute-start.27
  209.2 3.5 %collective-permute-done.27 = f32[32]{0:T(128)S(1)} collective-permute-done((f32[32]{0:T(128)S(1)}, f32[32]{0:T(128)S(1)}, u32[]{:S(2)}, u32[]{:S(2)}) %collective-permute-start.27) | collective-permute-done | bytes 160 | tf_op jit(solution)/shard_map/ppermute | solution.py:45
  212.7 0.4 add_bitcast_fusion.1
  213.1 1.1 pad_maximum_fusion
  (51 shorter events, 1.8 us)
Async XLA Ops:
  0.0 23.7 %copy-start = (bf16[2,64,1280]{2,1,0:T(8,128)(2,1)S(1)}, bf16[2,64,1280]{2,1,0:T(8,128)(2,1)}, u32[]{:S(2)}) copy-start(bf16[2,64,1280]{2,1,0:T(8,128)(2,1)} %param.10) | copy-start | bytes 983044
  0.0 9.7 %copy-start.2 = (f32[2,32]{1,0:T(2,128)S(1)}, f32[2,32]{1,0:T(2,128)}, u32[]{:S(2)}) copy-start(f32[2,32]{1,0:T(2,128)} %param.13) | copy-start | bytes 772
  0.0 15.7 %collective-permute-start = (f32[2,32,2,640]{3,2,1,0:T(2,128)}, f32[2,32,2,640]{3,2,1,0:T(2,128)S(1)}, u32[]{:S(2)}, u32[]{:S(2)}) collective-permute-start(f32[2,32,2,640]{3,2,1,0:T(2,128)} %param.8), channel_id=1, source_target_pairs={{0,8},{8,16},{16,24},{24,32},{32,40},{40,48},{48,56},{56,64},{64,7... | collective-permute-start | bytes 983048 | tf_op jit(solution)/shard_map/ppermute | solution.py:22
  4.0 13.0 %collective-permute-start.1 = (f32[2,32,2,640]{3,2,1,0:T(2,128)}, f32[2,32,2,640]{3,2,1,0:T(2,128)S(1)}, u32[]{:S(2)}, u32[]{:S(2)}) collective-permute-start(f32[2,32,2,640]{3,2,1,0:T(2,128)} %param.8), channel_id=1, source_target_pairs={{8,0},{16,8},{24,16},{32,24},{40,32},{48,40},{56,48},{64,56},{72,6... | collective-permute-start | bytes 983048 | tf_op jit(solution)/shard_map/ppermute | solution.py:24
  9.8 6.0 %copy-start.1 = (f32[2,32,2,640]{3,2,1,0:T(2,128)S(1)}, f32[2,32,2,640]{3,2,1,0:T(2,128)}, u32[]{:S(2)}) copy-start(f32[2,32,2,640]{3,2,1,0:T(2,128)} %param.8) | copy-start | bytes 983044
  17.1 29.3 %collective-permute-start.2 = (f32[6,32,2,640]{3,2,1,0:T(2,128)S(1)}, f32[6,32,2,640]{3,2,1,0:T(2,128)S(1)}, u32[]{:S(2)}, u32[]{:S(2)}) collective-permute-start(f32[6,32,2,640]{3,2,1,0:T(2,128)S(1)} %constant_dynamic-update-slice_fusion), channel_id=1, source_target_pairs={{0,1},{1,2},{2,3},{3,4},{4,5},{5,6},{6,7},{8,9},{9,10},{10,11},{11... | collective-permute-start | bytes 2949128 | tf_op jit(solution)/shard_map/ppermute | solution.py:22
  19.0 27.4 %collective-permute-start.3 = (f32[6,32,2,640]{3,2,1,0:T(2,128)S(1)}, f32[6,32,2,640]{3,2,1,0:T(2,128)}, u32[]{:S(2)}, u32[]{:S(2)}) collective-permute-start(f32[6,32,2,640]{3,2,1,0:T(2,128)S(1)} %constant_dynamic-update-slice_fusion), channel_id=1, source_target_pairs={{1,0},{2,1},{3,2},{4,3},{5,4},{6,5},{7,6},{9,8},{10,9},{11,10},{12... | collective-permute-start | bytes 2949128 | tf_op jit(solution)/shard_map/ppermute | solution.py:24
  23.7 0.7 copy-start.4
  24.6 1.3 collective-permute-start.4
  26.0 11.6 %collective-permute-start.5 = (f32[2,256,32]{1,2,0:T(8,128)S(1)}, f32[2,256,32]{1,2,0:T(8,128)S(1)}, u32[]{:S(2)}, u32[]{:S(2)}) collective-permute-start(f32[2,256,32]{1,2,0:T(8,128)S(1)} %add.128), channel_id=1, source_target_pairs={{0,2},{1,3},{2,0},{3,1},{4,6},{5,7},{6,4},{7,5},{8,10},{9,11},{10,... | collective-permute-start | bytes 196616 | tf_op jit(solution)/shard_map/ppermute | solution.py:93
  27.2 11.0 %copy-start.6 = (f32[4]{0:T(128)S(1)}, f32[4]{0:T(128)}, u32[]{:S(2)}) copy-start(f32[4]{0:T(128)} %param.15) | copy-start | bytes 52
  27.3 11.0 %copy-start.7 = (f32[4]{0:T(128)S(1)}, f32[4]{0:T(128)}, u32[]{:S(2)}) copy-start(f32[4]{0:T(128)} %param.14) | copy-start | bytes 52
  37.5 5.9 %copy-start.5 = (f32[2,256]{1,0:T(2,128)S(1)}, f32[2,256]{1,0:T(2,128)}, u32[]{:S(2)}) copy-start(f32[2,256]{1,0:T(2,128)} %param.12) | copy-start | bytes 6148
  37.6 5.9 %collective-permute-start.6 = (f32[2,256,32]{1,2,0:T(8,128)S(1)}, f32[2,256,32]{1,2,0:T(8,128)S(1)}, u32[]{:S(2)}, u32[]{:S(2)}) collective-permute-start(f32[2,256,32]{1,2,0:T(8,128)S(1)} %add.129), channel_id=1, source_target_pairs={{0,4},{1,5},{2,6},{3,7},{4,0},{5,1},{6,2},{7,3},{8,12},{9,13},{10,... | collective-permute-start | bytes 196616 | tf_op jit(solution)/shard_map/ppermute | solution.py:93
  44.5 1.9 copy-start.3
  52.9 13.8 %collective-permute-start.7 = (f32[2,32,2,640]{3,2,1,0:T(2,128)S(1)}, f32[2,32,2,640]{3,2,1,0:T(2,128)S(1)}, u32[]{:S(2)}, u32[]{:S(2)}) collective-permute-start(f32[2,32,2,640]{3,2,1,0:T(2,128)S(1)} %get-tuple-element.10), channel_id=1, source_target_pairs={{0,8},{8,16},{16,24},{24,32},{32,40},{40,48},{48,56},{56,64},{64,7... | collective-permute-start | bytes 983048 | tf_op jit(solution)/shard_map/ppermute | solution.py:45
  66.9 21.6 %collective-permute-start.9 = (f32[2,32,2,640]{3,2,1,0:T(2,128)S(1)}, f32[2,32,2,640]{3,2,1,0:T(2,128)S(1)}, u32[]{:S(2)}, u32[]{:S(2)}) collective-permute-start(f32[2,32,2,640]{3,2,1,0:T(2,128)S(1)} %multiply_add_fusion.11), channel_id=1, source_target_pairs={{0,16},{8,24},{16,32},{24,40},{32,48},{40,56},{48,64},{56,72},{64,... | collective-permute-start | bytes 983048 | tf_op jit(solution)/shard_map/ppermute | solution.py:45
  69.6 6.7 %collective-permute-start.19 = (f32[32]{0:T(128)S(1)}, f32[32]{0:T(128)S(1)}, u32[]{:S(2)}, u32[]{:S(2)}) collective-permute-start(f32[32]{0:T(128)S(1)} %get-tuple-element.24), channel_id=1, source_target_pairs={{8,0},{16,8},{24,16},{32,24},{40,32},{48,40},{56,48},{64,56},{72,6... | collective-permute-start | bytes 392 | tf_op jit(solution)/shard_map/ppermute | solution.py:45
  73.0 7.6 %collective-permute-start.8 = (f32[32]{0:T(128)S(1)}, f32[32]{0:T(128)S(1)}, u32[]{:S(2)}, u32[]{:S(2)}) collective-permute-start(f32[32]{0:T(128)S(1)} %get-tuple-element.24), channel_id=1, source_target_pairs={{0,8},{8,16},{16,24},{24,32},{32,40},{40,48},{48,56},{56,64},{64,7... | collective-permute-start | bytes 392 | tf_op jit(solution)/shard_map/ppermute | solution.py:45
  88.8 15.4 %collective-permute-start.11 = (f32[2,32,2,640]{3,2,1,0:T(2,128)S(1)}, f32[2,32,2,640]{3,2,1,0:T(2,128)S(1)}, u32[]{:S(2)}, u32[]{:S(2)}) collective-permute-start(f32[2,32,2,640]{3,2,1,0:T(2,128)S(1)} %multiply_add_fusion.10), channel_id=1, source_target_pairs={{0,32},{8,40},{16,48},{24,56},{32,64},{40,72},{48,80},{56,88},{64,... | collective-permute-start | bytes 983048 | tf_op jit(solution)/shard_map/ppermute | solution.py:45
  94.1 8.4 %collective-permute-start.10 = (f32[32]{0:T(128)S(1)}, f32[32]{0:T(128)S(1)}, u32[]{:S(2)}, u32[]{:S(2)}) collective-permute-start(f32[32]{0:T(128)S(1)} %get-tuple-element.31), channel_id=1, source_target_pairs={{0,16},{8,24},{16,32},{24,40},{32,48},{40,56},{48,64},{56,72},{64,... | collective-permute-start | bytes 392 | tf_op jit(solution)/shard_map/ppermute | solution.py:45
  104.5 13.3 %collective-permute-start.13 = (f32[2,32,2,640]{3,2,1,0:T(2,128)S(1)}, f32[2,32,2,640]{3,2,1,0:T(2,128)S(1)}, u32[]{:S(2)}, u32[]{:S(2)}) collective-permute-start(f32[2,32,2,640]{3,2,1,0:T(2,128)S(1)} %multiply_add_fusion.9), channel_id=1, source_target_pairs={{0,64},{8,72},{16,80},{24,88},{32,96},{40,104},{48,112},{56,120},{... | collective-permute-start | bytes 983048 | tf_op jit(solution)/shard_map/ppermute | solution.py:45
  107.5 10.2 %collective-permute-start.12 = (f32[32]{0:T(128)S(1)}, f32[32]{0:T(128)S(1)}, u32[]{:S(2)}, u32[]{:S(2)}) collective-permute-start(f32[32]{0:T(128)S(1)} %mul.333), channel_id=1, source_target_pairs={{0,32},{8,40},{16,48},{24,56},{32,64},{40,72},{48,80},{56,88},{64,... | collective-permute-start | bytes 392 | tf_op jit(solution)/shard_map/ppermute | solution.py:45
  118.0 15.6 %collective-permute-start.14 = (f32[2,32,2,640]{3,2,1,0:T(2,128)S(1)}, f32[2,32,2,640]{3,2,1,0:T(2,128)S(1)}, u32[]{:S(2)}, u32[]{:S(2)}) collective-permute-start(f32[2,32,2,640]{3,2,1,0:T(2,128)S(1)} %multiply_add_fusion.8), channel_id=1, source_target_pairs={{0,8},{8,16},{16,24},{24,32},{32,40},{40,48},{48,56},{56,64},{64,7... | collective-permute-start | bytes 983048 | tf_op jit(solution)/shard_map/ppermute | solution.py:45
  119.9 13.7 %collective-permute-start.17 = (f32[2,32,2,640]{3,2,1,0:T(2,128)S(1)}, f32[2,32,2,640]{3,2,1,0:T(2,128)S(1)}, u32[]{:S(2)}, u32[]{:S(2)}) collective-permute-start(f32[2,32,2,640]{3,2,1,0:T(2,128)S(1)} %multiply_add_fusion.8), channel_id=1, source_target_pairs={{0,136},{8,144},{16,152},{24,160},{32,168},{40,176},{48,184},{56,1... | collective-permute-start | bytes 983048 | tf_op jit(solution)/shard_map/ppermute | solution.py:45
  120.6 5.5 %collective-permute-start.15 = (f32[32]{0:T(128)S(1)}, f32[32]{0:T(128)S(1)}, u32[]{:S(2)}, u32[]{:S(2)}) collective-permute-start(f32[32]{0:T(128)S(1)} %mul.336), channel_id=1, source_target_pairs={{0,64},{8,72},{16,80},{24,88},{32,96},{40,104},{48,112},{56,120},{... | collective-permute-start | bytes 392 | tf_op jit(solution)/shard_map/ppermute | solution.py:45
  126.1 7.5 %collective-permute-start.16 = (f32[32]{0:T(128)S(1)}, f32[32]{0:T(128)S(1)}, u32[]{:S(2)}, u32[]{:S(2)}) collective-permute-start(f32[32]{0:T(128)S(1)} %mul.339), channel_id=1, source_target_pairs={{0,8},{8,16},{16,24},{24,32},{32,40},{40,48},{48,56},{56,64},{64,7... | collective-permute-start | bytes 392 | tf_op jit(solution)/shard_map/ppermute | solution.py:45
  134.3 10.7 %collective-permute-start.18 = (f32[2,32,2,640]{3,2,1,0:T(2,128)S(1)}, f32[2,32,2,640]{3,2,1,0:T(2,128)S(1)}, u32[]{:S(2)}, u32[]{:S(2)}) collective-permute-start(f32[2,32,2,640]{3,2,1,0:T(2,128)S(1)} %get-tuple-element.8), channel_id=1, source_target_pairs={{8,0},{16,8},{24,16},{32,24},{40,32},{48,40},{56,48},{64,56},{72,6... | collective-permute-start | bytes 983048 | tf_op jit(solution)/shard_map/ppermute | solution.py:45
  145.2 19.0 %collective-permute-start.20 = (f32[2,32,2,640]{3,2,1,0:T(2,128)S(1)}, f32[2,32,2,640]{3,2,1,0:T(2,128)S(1)}, u32[]{:S(2)}, u32[]{:S(2)}) collective-permute-start(f32[2,32,2,640]{3,2,1,0:T(2,128)S(1)} %multiply_add_fusion.4), channel_id=1, source_target_pairs={{16,0},{24,8},{32,16},{40,24},{48,32},{56,40},{64,48},{72,56},{80,... | collective-permute-start | bytes 983048 | tf_op jit(solution)/shard_map/ppermute | solution.py:45
  164.5 13.0 %collective-permute-start.22 = (f32[2,32,2,640]{3,2,1,0:T(2,128)S(1)}, f32[2,32,2,640]{3,2,1,0:T(2,128)S(1)}, u32[]{:S(2)}, u32[]{:S(2)}) collective-permute-start(f32[2,32,2,640]{3,2,1,0:T(2,128)S(1)} %multiply_add_fusion.3), channel_id=1, source_target_pairs={{32,0},{40,8},{48,16},{56,24},{64,32},{72,40},{80,48},{88,56},{96,... | collective-permute-start | bytes 983048 | tf_op jit(solution)/shard_map/ppermute | solution.py:45
  166.4 8.7 %collective-permute-start.21 = (f32[32]{0:T(128)S(1)}, f32[32]{0:T(128)S(1)}, u32[]{:S(2)}, u32[]{:S(2)}) collective-permute-start(f32[32]{0:T(128)S(1)} %get-tuple-element.30), channel_id=1, source_target_pairs={{16,0},{24,8},{32,16},{40,24},{48,32},{56,40},{64,48},{72,56},{80,... | collective-permute-start | bytes 392 | tf_op jit(solution)/shard_map/ppermute | solution.py:45
  177.7 11.3 %collective-permute-start.24 = (f32[2,32,2,640]{3,2,1,0:T(2,128)S(1)}, f32[2,32,2,640]{3,2,1,0:T(2,128)S(1)}, u32[]{:S(2)}, u32[]{:S(2)}) collective-permute-start(f32[2,32,2,640]{3,2,1,0:T(2,128)S(1)} %multiply_add_fusion.2), channel_id=1, source_target_pairs={{64,0},{72,8},{80,16},{88,24},{96,32},{104,40},{112,48},{120,56},{... | collective-permute-start | bytes 983048 | tf_op jit(solution)/shard_map/ppermute | solution.py:45
  179.6 9.3 %collective-permute-start.23 = (f32[32]{0:T(128)S(1)}, f32[32]{0:T(128)S(1)}, u32[]{:S(2)}, u32[]{:S(2)}) collective-permute-start(f32[32]{0:T(128)S(1)} %mul.355), channel_id=1, source_target_pairs={{32,0},{40,8},{48,16},{56,24},{64,32},{72,40},{80,48},{88,56},{96,... | collective-permute-start | bytes 392 | tf_op jit(solution)/shard_map/ppermute | solution.py:45
  189.2 23.5 %collective-permute-start.25 = (f32[2,32,2,640]{3,2,1,0:T(2,128)S(1)}, f32[2,32,2,640]{3,2,1,0:T(2,128)S(1)}, u32[]{:S(2)}, u32[]{:S(2)}) collective-permute-start(f32[2,32,2,640]{3,2,1,0:T(2,128)S(1)} %multiply_add_fusion.1), channel_id=1, source_target_pairs={{8,0},{16,8},{24,16},{32,24},{40,32},{48,40},{56,48},{64,56},{72,6... | collective-permute-start | bytes 983048 | tf_op jit(solution)/shard_map/ppermute | solution.py:45
  201.1 11.6 %collective-permute-start.28 = (f32[2,32,2,640]{3,2,1,0:T(2,128)S(1)}, f32[2,32,2,640]{3,2,1,0:T(2,128)S(1)}, u32[]{:S(2)}, u32[]{:S(2)}) collective-permute-start(f32[2,32,2,640]{3,2,1,0:T(2,128)S(1)} %multiply_add_fusion.1), channel_id=1, source_target_pairs={{136,0},{144,8},{152,16},{160,24},{168,32},{176,40},{184,48},{192,... | collective-permute-start | bytes 983048 | tf_op jit(solution)/shard_map/ppermute | solution.py:45
  201.8 5.5 %collective-permute-start.26 = (f32[32]{0:T(128)S(1)}, f32[32]{0:T(128)S(1)}, u32[]{:S(2)}, u32[]{:S(2)}) collective-permute-start(f32[32]{0:T(128)S(1)} %mul.358), channel_id=1, source_target_pairs={{64,0},{72,8},{80,16},{88,24},{96,32},{104,40},{112,48},{120,56},{... | collective-permute-start | bytes 392 | tf_op jit(solution)/shard_map/ppermute | solution.py:45
  207.3 5.4 %collective-permute-start.27 = (f32[32]{0:T(128)S(1)}, f32[32]{0:T(128)S(1)}, u32[]{:S(2)}, u32[]{:S(2)}) collective-permute-start(f32[32]{0:T(128)S(1)} %mul.361), channel_id=1, source_target_pairs={{8,0},{16,8},{24,16},{32,24},{40,32},{48,40},{56,48},{64,56},{72,6... | collective-permute-start | bytes 392 | tf_op jit(solution)/shard_map/ppermute | solution.py:45

commit v2 on v1

--- a/solution.py
+++ b/solution.py
@@ -1,6 +1,10 @@
+import functools
+
 import jax
 import jax.numpy as jnp
 from jax import lax
+from jax.experimental import pallas as pl
+from jax.experimental.pallas import tpu as pltpu
 from jax.sharding import PartitionSpec as P
 
 NPROJ = 256
@@ -36,54 +40,136 @@
     return FAR * (piece(-2) + piece(2)) + NEAR * (piece(-1) + piece(1)) + CENTER * piece(0)
 
 
-def shifted(tree, axis, step, reverse):
-    count = lax.axis_size(axis)
-    if reverse:
-        pairs = [(i + step, i) for i in range(count - step)]
-    else:
-        pairs = [(i, i + step) for i in range(count - step)]
-    return lax.ppermute(tree, axis, pairs)
-
-
-def carried(through, end, axis, reverse):
-    count = lax.axis_size(axis)
+MESH = pl.DeviceIdType.MESH
+
+
+def spans_of(count):
+    spans = []
     span = 1
-    t, a = through, end
     while 2 * span < count:
-        tr, ar = shifted((t, a), axis, span, reverse)
-        a = a + t[None, :, None, None] * ar
-        t = t * tr
+        spans.append(span)
         span *= 2
-    near_t, near_a = shifted((t, a), axis, 1, reverse)
-    if span + 1 < count:
-        far_a = shifted(a, axis, span + 1, reverse)
-        return near_a + near_t[None, :, None, None] * far_a
-    return near_a
+    return spans, span + 1
+
+
+def sweep_kernel(count, f_ref, d_ref, o_ref, state, landed, send_sem, recv_sem):
+    me = lax.axis_index("layer")
+    row = lax.axis_index("xs")
+    layers = f_ref.shape[1]
+    width = f_ref.shape[3]
+    spans, far = spans_of(count)
+    hops = spans + [1, far]
+    barrier = pltpu.get_barrier_semaphore()
+    for hop in hops:
+        for sign in (1, -1):
+            pl.semaphore_signal(
+                barrier, inc=1, device_id=(lax.rem(me + sign * hop + count, count), row),
+                device_id_type=MESH,
+            )
+    pl.semaphore_wait(barrier, 2 * len(hops))
+
+    rates = [d_ref[index] for index in range(layers)]
+    through = rates[0]
+    for index in range(1, layers):
+        through = through * rates[index]
+
+    def put(direction, slot, ends, keep):
+        state[direction, slot, :, :, :width] = ends
+        state[direction, slot, :, :, width:] = jnp.broadcast_to(keep[None], (2,) + keep.shape[:1] + (128,))
+
+    def send(direction, slot, target_slot, hop, sign):
+        copy = pltpu.make_async_remote_copy(
+            src_ref=state.at[direction, slot],
+            dst_ref=landed.at[direction, target_slot],
+            send_sem=send_sem.at[direction, target_slot],
+            recv_sem=recv_sem.at[direction, target_slot],
+            device_id=(lax.rem(me + sign * hop + count, count), row),
+            device_id_type=MESH,
+        )
+        copy.start()
+        return copy
+
+    def scan(direction, ends, sign):
+        put(direction, 0, ends, through)
+        for slot, hop in enumerate(spans):
+            send(direction, slot, slot, hop, sign).wait()
+            source = me - hop if sign == 1 else me + hop
+            valid = ((source >= 0) & (source < count)).astype(jnp.float32)
+            mine = state[direction, slot]
+            got = landed[direction, slot]
+            keep = mine[0, :, width:width + 1]
+            put(
+                direction, slot + 1,
+                mine[:, :, :width] + (valid * keep)[None] * got[:, :, :width],
+                keep * (valid * got[0, :, width:width + 1]),
+            )
+        last = len(spans)
+        near = send(direction, last, last, 1, sign)
+        distant = send(direction, last, last + 1, far, sign)
+        near.wait()
+        distant.wait()
+        near_source = me - 1 if sign == 1 else me + 1
+        far_source = me - far if sign == 1 else me + far
+        near_valid = ((near_source >= 0) & (near_source < count)).astype(jnp.float32)
+        far_valid = ((far_source >= 0) & (far_source < count)).astype(jnp.float32)
+        got = landed[direction, last]
+        result = got[:, :, :width]
+        if far < count:
+            result = result + (far_valid * got[0, :, width:width + 1])[None] * landed[direction, last + 1, :, :, :width]
+        return near_valid * result
+
+    state_now = None
+    ahead = []
+    for index in range(layers):
+        source = f_ref[:, index]
+        if state_now is None:
+            state_now = (1.0 - rates[index])[None] * source
+        else:
+            state_now = rates[index][None] * state_now + (1.0 - rates[index])[None] * source
+        ahead.append(state_now)
+    entering = scan(0, state_now, 1)
+    lower = rates[0]
+    for index in range(layers):
+        if index > 0:
+            lower = lower * rates[index]
+        ahead[index] = ahead[index] + lower[None] * entering
+    state_now = None
+    back = [None] * layers
+    for index in reversed(range(layers)):
+        if state_now is None:
+            state_now = (1.0 - rates[index])[None] * ahead[index]
+        else:
+            state_now = rates[index][None] * state_now + (1.0 - rates[index])[None] * ahead[index]
+        back[index] = state_now
+    from_above = scan(1, state_now, -1)
+    upper = rates[layers - 1]
+    for index in reversed(range(layers)):
+        if index < layers - 1:
+            upper = upper * rates[index]
+        o_ref[:, index] = back[index] + upper[None] * from_above
 
 
 def sweeps(forcing, decay_rates):
-    count = forcing.shape[1]
-    rates = decay_rates[None, :, :, None, None]
-    keep = 1.0 - rates
-    state = jnp.zeros_like(forcing[:, 0])
-    ahead_list = []
-    for index in range(count):
-        state = rates[:, index] * state + keep[:, index] * forcing[:, index]
-        ahead_list.append(state)
-    through = jnp.prod(decay_rates, axis=0)
-    entering = carried(through, state, "layer", False)
-    lower = jnp.cumprod(decay_rates, axis=0)
-    ahead = [ahead_list[i] + lower[i][None, :, None, None] * entering for i in range(count)]
-    state = jnp.zeros_like(forcing[:, 0])
-    back_list = [None] * count
-    for index in reversed(range(count)):
-        state = rates[:, index] * state + keep[:, index] * ahead[index]
-        back_list[index] = state
-    from_above = carried(through, state, "layer", True)
-    upper = jnp.cumprod(decay_rates[::-1], axis=0)[::-1]
-    return jnp.stack(
-        [back_list[i] + upper[i][None, :, None, None] * from_above for i in range(count)], axis=1
-    )
+    moments, layers, columns, rows, depth = forcing.shape
+    width = rows * depth
+    count = lax.axis_size("layer")
+    spans, _ = spans_of(count)
+    rounds = len(spans) + 2
+    flat = forcing.reshape(moments, layers, columns, width)
+    out = pl.pallas_call(
+        functools.partial(sweep_kernel, count),
+        out_shape=jax.ShapeDtypeStruct(flat.shape, jnp.float32),
+        in_specs=[pl.BlockSpec(memory_space=pltpu.VMEM)] * 2,
+        out_specs=pl.BlockSpec(memory_space=pltpu.VMEM),
+        scratch_shapes=[
+            pltpu.VMEM((2, rounds, moments, columns, width + 128), jnp.float32),
+            pltpu.VMEM((2, rounds, moments, columns, width + 128), jnp.float32),
+            pltpu.SemaphoreType.DMA((2, rounds)),
+            pltpu.SemaphoreType.DMA((2, rounds)),
+        ],
+        compiler_params=pltpu.CompilerParams(collective_id=0, has_side_effects=True),
+    )(flat, decay_rates[:, :, None])
+    return out.reshape(forcing.shape)
 
 
 def plane_sum(x, axis):

time: 215 us -> 226 us (1.051)
  the two profiles are of different devices: /device:TPU:20 before, /device:TPU:22 now
where the time goes in v2:
time: 226 us
  Pallas kernels  170 us (75%)
  waiting for transfers between devices  19.8 us (9%)
  starting transfers between devices  17.5 us (8%)
  other arithmetic  8.7 us (4%)
  local copies, waits for them, and re-layouts  7.75 us (3%)
    pallas_call x1, Pallas kernels, sweeps(): pl.pallas_call(functools.partial(sweep_kernel, count), out_shape=jax.Shap...  170 us
    ppermute x3, waiting for transfers between devices, plane_sum(): x = x + lax.ppermute(x, axis, [(i, i ^ step) for i in range(count)])  13.5 us
    ppermute x2, starting transfers between devices, with_halo(): lax.ppermute(head, axis, [((i + 1) % count, i) for i in range(ends)])  9.39 us
    sub x2, other arithmetic, shards(): forcing = jnp.stack([w0 * hamil - w1 * probes, w1 * hamil - w2 * probes])  6.33 us
    ppermute x2, waiting for transfers between devices, with_halo(): lax.ppermute(tail, axis, [(i, (i + 1) % count) for i in range(ends)])  5.98 us
    ppermute x2, starting transfers between devices, with_halo(): lax.ppermute(tail, axis, [(i, (i + 1) % count) for i in range(ends)])  5.87 us
  transfers between devices with their start and end apart: 7, of which 5 were waited for; matrix products, arithmetic and copies ran while one was open for 3% of the time, Pallas kernels for 0%

profile of v2, /device:TPU:22, one launch (start us, length us, event | category | flops | bytes accessed | tf_op | source)
XLA Modules:
  0.0 225.6 jit_solution(15647466471919994218)
XLA Ops:
  0.0 0.0 copy-start
  0.0 0.0 copy-start.1
  0.0 3.9 %collective-permute-start = (f32[2,32,2,640]{3,2,1,0:T(2,128)}, f32[2,32,2,640]{3,2,1,0:T(2,128)S(1)}, u32[]{:S(2)}, u32[]{:S(2)}) collective-permute-start(f32[2,32,2,640]{3,2,1,0:T(2,128)} %param.8), channel_id=1, source_target_pairs={{0,8},{8,16},{16,24},{24,32},{32,40},{40,48},{48,56},{56,64},{64,7... | collective-permute-start | bytes 983048 | tf_op jit(solution)/shard_map/ppermute | solution.py:26
  4.0 5.7 %collective-permute-start.1 = (f32[2,32,2,640]{3,2,1,0:T(2,128)}, f32[2,32,2,640]{3,2,1,0:T(2,128)S(1)}, u32[]{:S(2)}, u32[]{:S(2)}) collective-permute-start(f32[2,32,2,640]{3,2,1,0:T(2,128)} %param.8), channel_id=1, source_target_pairs={{8,0},{16,8},{24,16},{32,24},{40,32},{48,40},{56,48},{64,56},{72,6... | collective-permute-start | bytes 983048 | tf_op jit(solution)/shard_map/ppermute | solution.py:28
  9.7 6.0 %collective-permute-done = f32[2,32,2,640]{3,2,1,0:T(2,128)S(1)} collective-permute-done((f32[2,32,2,640]{3,2,1,0:T(2,128)}, f32[2,32,2,640]{3,2,1,0:T(2,128)S(1)}, u32[]{:S(2)}, u32[]{:S(2)}) %collective-permute-start) | collective-permute-done | bytes 327712 | tf_op jit(solution)/shard_map/ppermute | solution.py:26
  15.7 0.0 copy-done.1
  15.7 0.8 constant_dynamic-update-slice_fusion.1
  16.6 0.4 collective-permute-done.1
  17.0 0.1 constant_dynamic-update-slice_fusion
  17.1 1.9 collective-permute-start.2
  19.0 3.6 %collective-permute-start.3 = (f32[6,32,2,640]{3,2,1,0:T(2,128)S(1)}, f32[6,32,2,640]{3,2,1,0:T(2,128)}, u32[]{:S(2)}, u32[]{:S(2)}) collective-permute-start(f32[6,32,2,640]{3,2,1,0:T(2,128)S(1)} %constant_dynamic-update-slice_fusion), channel_id=1, source_target_pairs={{1,0},{2,1},{3,2},{4,3},{5,4},{6,5},{7,6},{9,8},{10,9},{11,10},{12... | collective-permute-start | bytes 2949128 | tf_op jit(solution)/shard_map/ppermute | solution.py:28
  22.6 1.0 reshape.17
  23.7 0.0 copy-done
  23.7 0.0 copy-start.4
  23.7 0.2 fusion.19
  23.9 0.5 copy-done.4
  24.4 0.2 fusion.13
  24.6 0.1 collective-permute-start.4
  24.7 1.2 collective-permute-done.4
  26.0 0.0 copy-start.6
  26.0 0.9 collective-permute-start.5
  26.9 0.0 copy-done.6
  26.9 0.7 copy.9.d_ref
  27.6 0.0 copy-start.7
  27.6 0.0 copy-start.8
  27.6 8.3 %collective-permute-done.5 = f32[2,256,32]{1,2,0:T(8,128)S(1)} collective-permute-done((f32[2,256,32]{1,2,0:T(8,128)S(1)}, f32[2,256,32]{1,2,0:T(8,128)S(1)}, u32[]{:S(2)}, u32[]{:S(2)}) %collective-permute-start.5) | collective-permute-done | bytes 65568 | tf_op jit(solution)/shard_map/ppermute | solution.py:179
  35.9 0.0 copy-start.5
  35.9 1.3 collective-permute-start.6
  37.2 0.0 copy-done.7
  37.2 0.0 copy-done.8
  37.2 0.6 multiply_reduce_fusion.1
  37.8 4.0 %collective-permute-done.6 = f32[2,256,32]{1,2,0:T(8,128)S(1)} collective-permute-done((f32[2,256,32]{1,2,0:T(8,128)S(1)}, f32[2,256,32]{1,2,0:T(8,128)S(1)}, u32[]{:S(2)}, u32[]{:S(2)}) %collective-permute-start.6) | collective-permute-done | bytes 65568 | tf_op jit(solution)/shard_map/ppermute | solution.py:179
  41.8 0.0 copy-done.5
  41.8 1.1 fusion
  42.9 0.0 copy-start.3
  42.9 1.9 reshape.18
  44.8 0.0 collective-permute-done.2
  44.8 0.0 collective-permute-done.3
  44.8 0.0 copy-done.3
  44.8 5.1 %multiply_subtract_fusion.1 = (f32[2,32,2,640]{3,2,1,0:T(2,128)}, f32[2,32,2,640]{3,2,1,0:T(2,128)S(1)}) fusion(f32[2,32,2,640]{3,2,1,0:T(2,128)S(1)} %copy-done.1, f32[]{:T(128)} %get-tuple-element.5, f32[]{:T(128)} %get-tuple-element.7, f32[2,32,2,640]{3,2,1,0:T(2,128)} %reshape.18, f32[2,2,640]{2,1,0:T(2,128)S(1)} %copy-done.3, ...), kind=kLoop, calls=%fused_computation.19 | loop fusion | flops 2621440 | bytes 5581824 | tf_op jit(solution)/shard_map/sub | solution.py:218
  49.8 1.2 multiply_subtract_fusion
  51.1 0.0 copy-start.2
  51.1 0.3 stack.10
  51.4 0.7 copy-done.2
  52.1 0.3 stack.9
  52.3 0.9 pad_maximum_fusion.f_ref
  53.2 170.1 %shard_map.82 = f32[2,2,32,1280]{3,2,1,0:T(8,128)} custom-call(f32[2,2,32,1280]{3,2,1,0:T(8,128)} %pad_maximum_fusion.f_ref, f32[2,32,1]{2,1,0:T(8,128)} %copy.9.d_ref), custom_call_target="tpu_custom_call" | custom-call | tf_op jit(solution)/shard_map/pallas_call | solution.py:159
  223.3 2.3 %reshape.19 = f32[2,2,32,2,640]{4,3,2,1,0:T(2,128)} reshape(f32[2,2,32,1280]{3,2,1,0:T(8,128)} %shard_map.82) | data formatting | bytes 1310720 | tf_op jit(solution)/shard_map/reshape | solution.py:172
  (3 shorter events, 0.1 us)
Async XLA Ops:
  0.0 23.7 %copy-start = (bf16[2,64,1280]{2,1,0:T(8,128)(2,1)S(1)}, bf16[2,64,1280]{2,1,0:T(8,128)(2,1)}, u32[]{:S(2)}) copy-start(bf16[2,64,1280]{2,1,0:T(8,128)(2,1)} %param.10) | copy-start | bytes 983044
  0.0 15.7 %copy-start.1 = (f32[2,32,2,640]{3,2,1,0:T(2,128)S(1)}, f32[2,32,2,640]{3,2,1,0:T(2,128)}, u32[]{:S(2)}) copy-start(f32[2,32,2,640]{3,2,1,0:T(2,128)} %param.8) | copy-start | bytes 983044
  0.0 15.7 %collective-permute-start = (f32[2,32,2,640]{3,2,1,0:T(2,128)}, f32[2,32,2,640]{3,2,1,0:T(2,128)S(1)}, u32[]{:S(2)}, u32[]{:S(2)}) collective-permute-start(f32[2,32,2,640]{3,2,1,0:T(2,128)} %param.8), channel_id=1, source_target_pairs={{0,8},{8,16},{16,24},{24,32},{32,40},{40,48},{48,56},{56,64},{64,7... | collective-permute-start | bytes 983048 | tf_op jit(solution)/shard_map/ppermute | solution.py:26
  4.0 13.0 %collective-permute-start.1 = (f32[2,32,2,640]{3,2,1,0:T(2,128)}, f32[2,32,2,640]{3,2,1,0:T(2,128)S(1)}, u32[]{:S(2)}, u32[]{:S(2)}) collective-permute-start(f32[2,32,2,640]{3,2,1,0:T(2,128)} %param.8), channel_id=1, source_target_pairs={{8,0},{16,8},{24,16},{32,24},{40,32},{48,40},{56,48},{64,56},{72,6... | collective-permute-start | bytes 983048 | tf_op jit(solution)/shard_map/ppermute | solution.py:28
  17.1 27.7 %collective-permute-start.2 = (f32[6,32,2,640]{3,2,1,0:T(2,128)S(1)}, f32[6,32,2,640]{3,2,1,0:T(2,128)S(1)}, u32[]{:S(2)}, u32[]{:S(2)}) collective-permute-start(f32[6,32,2,640]{3,2,1,0:T(2,128)S(1)} %constant_dynamic-update-slice_fusion), channel_id=1, source_target_pairs={{0,1},{1,2},{2,3},{3,4},{4,5},{5,6},{6,7},{8,9},{9,10},{10,11},{11... | collective-permute-start | bytes 2949128 | tf_op jit(solution)/shard_map/ppermute | solution.py:26
  19.0 25.8 %collective-permute-start.3 = (f32[6,32,2,640]{3,2,1,0:T(2,128)S(1)}, f32[6,32,2,640]{3,2,1,0:T(2,128)}, u32[]{:S(2)}, u32[]{:S(2)}) collective-permute-start(f32[6,32,2,640]{3,2,1,0:T(2,128)S(1)} %constant_dynamic-update-slice_fusion), channel_id=1, source_target_pairs={{1,0},{2,1},{3,2},{4,3},{5,4},{6,5},{7,6},{9,8},{10,9},{11,10},{12... | collective-permute-start | bytes 2949128 | tf_op jit(solution)/shard_map/ppermute | solution.py:28
  23.7 0.7 copy-start.4
  24.6 1.3 collective-permute-start.4
  26.0 0.9 copy-start.6
  26.0 9.9 %collective-permute-start.5 = (f32[2,256,32]{1,2,0:T(8,128)S(1)}, f32[2,256,32]{1,2,0:T(8,128)S(1)}, u32[]{:S(2)}, u32[]{:S(2)}) collective-permute-start(f32[2,256,32]{1,2,0:T(8,128)S(1)} %add.74), channel_id=1, source_target_pairs={{0,2},{1,3},{2,0},{3,1},{4,6},{5,7},{6,4},{7,5},{8,10},{9,11},{10,... | collective-permute-start | bytes 196616 | tf_op jit(solution)/shard_map/ppermute | solution.py:179
  27.6 9.6 %copy-start.7 = (f32[4]{0:T(128)S(1)}, f32[4]{0:T(128)}, u32[]{:S(2)}) copy-start(f32[4]{0:T(128)} %param.15) | copy-start | bytes 52
  27.6 9.6 %copy-start.8 = (f32[4]{0:T(128)S(1)}, f32[4]{0:T(128)}, u32[]{:S(2)}) copy-start(f32[4]{0:T(128)} %param.14) | copy-start | bytes 52
  35.9 5.9 %copy-start.5 = (f32[2,256]{1,0:T(2,128)S(1)}, f32[2,256]{1,0:T(2,128)}, u32[]{:S(2)}) copy-start(f32[2,256]{1,0:T(2,128)} %param.12) | copy-start | bytes 6148
  35.9 5.9 %collective-permute-start.6 = (f32[2,256,32]{1,2,0:T(8,128)S(1)}, f32[2,256,32]{1,2,0:T(8,128)S(1)}, u32[]{:S(2)}, u32[]{:S(2)}) collective-permute-start(f32[2,256,32]{1,2,0:T(8,128)S(1)} %add.75), channel_id=1, source_target_pairs={{0,4},{1,5},{2,6},{3,7},{4,0},{5,1},{6,2},{7,3},{8,12},{9,13},{10,... | collective-permute-start | bytes 196616 | tf_op jit(solution)/shard_map/ppermute | solution.py:179
  42.9 1.9 copy-start.3
  51.1 1.0 copy-start.2

commit v3 on v2

--- a/solution.py
+++ b/solution.py
@@ -151,25 +151,24 @@
 
 def sweeps(forcing, decay_rates):
     moments, layers, columns, rows, depth = forcing.shape
-    width = rows * depth
-    count = lax.axis_size("layer")
-    spans, _ = spans_of(count)
-    rounds = len(spans) + 2
-    flat = forcing.reshape(moments, layers, columns, width)
-    out = pl.pallas_call(
-        functools.partial(sweep_kernel, count),
-        out_shape=jax.ShapeDtypeStruct(flat.shape, jnp.float32),
-        in_specs=[pl.BlockSpec(memory_space=pltpu.VMEM)] * 2,
-        out_specs=pl.BlockSpec(memory_space=pltpu.VMEM),
-        scratch_shapes=[
-            pltpu.VMEM((2, rounds, moments, columns, width + 128), jnp.float32),
-            pltpu.VMEM((2, rounds, moments, columns, width + 128), jnp.float32),
-            pltpu.SemaphoreType.DMA((2, rounds)),
-            pltpu.SemaphoreType.DMA((2, rounds)),
-        ],
-        compiler_params=pltpu.CompilerParams(collective_id=0, has_side_effects=True),
-    )(flat, decay_rates[:, :, None])
-    return out.reshape(forcing.shape)
+    flat = forcing.reshape(moments, layers, columns, rows * depth)
+    whole = lax.all_to_all(flat, "layer", 2, 1, tiled=True)
+    rates = lax.all_to_all(decay_rates, "layer", 1, 0, tiled=True)
+    total = whole.shape[1]
+    rate = rates[:, None, :, None]
+    keep = 1.0 - rate
+    state = jnp.zeros_like(whole[:, 0])
+    ahead = []
+    for index in range(total):
+        state = rate[index] * state + keep[index] * whole[:, index]
+        ahead.append(state)
+    state = jnp.zeros_like(whole[:, 0])
+    back = [None] * total
+    for index in reversed(range(total)):
+        state = rate[index] * state + keep[index] * ahead[index]
+        back[index] = state
+    swept = jnp.stack(back, axis=1)
+    return lax.all_to_all(swept, "layer", 1, 2, tiled=True).reshape(forcing.shape)
 
 
 def plane_sum(x, axis):

time: 226 us -> 234 us (1.035)
  the two profiles are of different devices: /device:TPU:22 before, /device:TPU:32 now
where the time goes in v3:
time: 234 us; the launch traced here: 232 us
  other arithmetic  131 us (56%)
  starting transfers between devices  37.2 us (16%)
  waiting for transfers between devices  23.5 us (10%)
  blocking collectives  22.6 us (10%)
  local copies, waits for them, and re-layouts  13.9 us (6%)
    unnamed x33, other arithmetic  121 us
    all_to_all x1, blocking collectives, sweeps(): lax.all_to_all(swept, 'layer', 1, 2, tiled=True).reshape(forcing.shape)  22.6 us
    all_to_all x1, waiting for transfers between devices, sweeps(): whole = lax.all_to_all(flat, 'layer', 2, 1, tiled=True)  11.7 us
    all_to_all x1, starting transfers between devices, sweeps(): rates = lax.all_to_all(decay_rates, 'layer', 1, 0, tiled=True)  11 us
    all_to_all x1, starting transfers between devices, sweeps(): whole = lax.all_to_all(flat, 'layer', 2, 1, tiled=True)  9.79 us
    ppermute x3, starting transfers between devices, plane_sum(): x = x + lax.ppermute(x, axis, [(i, i ^ step) for i in range(count)])  7.75 us
    sub x2, other arithmetic, shards(): forcing = jnp.stack([w0 * hamil - w1 * probes, w1 * hamil - w2 * probes])  6.44 us
    ppermute x2, waiting for transfers between devices, with_halo(): lax.ppermute(tail, axis, [(i, (i + 1) % count) for i in range(ends)])  5.68 us
  transfers between devices with their start and end apart: 9, of which 5 were waited for; matrix products, arithmetic and copies ran while one was open for 9% of the time, Pallas kernels for 0%

profile of v3, /device:TPU:32, one launch (start us, length us, event | category | flops | bytes accessed | tf_op | source)
XLA Modules:
  0.0 231.5 jit_solution(8708334873851379920)
XLA Ops:
  0.0 3.9 %collective-permute-start = (f32[2,32,2,640]{3,2,1,0:T(2,128)}, f32[2,32,2,640]{3,2,1,0:T(2,128)S(1)}, u32[]{:S(2)}, u32[]{:S(2)}) collective-permute-start(f32[2,32,2,640]{3,2,1,0:T(2,128)} %param.8), channel_id=1, source_target_pairs={{0,8},{8,16},{16,24},{24,32},{32,40},{40,48},{48,56},{56,64},{64,7... | collective-permute-start | bytes 983048 | tf_op jit(solution)/shard_map/ppermute | solution.py:26
  4.0 2.0 collective-permute-start.1
  6.0 5.7 %collective-permute-done = f32[2,32,2,640]{3,2,1,0:T(2,128)S(1)} collective-permute-done((f32[2,32,2,640]{3,2,1,0:T(2,128)}, f32[2,32,2,640]{3,2,1,0:T(2,128)S(1)}, u32[]{:S(2)}, u32[]{:S(2)}) %collective-permute-start) | collective-permute-done | bytes 327712 | tf_op jit(solution)/shard_map/ppermute | solution.py:26
  11.7 0.8 constant_dynamic-update-slice_fusion.1
  12.6 2.8 %collective-permute-done.1 = f32[2,32,2,640]{3,2,1,0:T(2,128)S(1)} collective-permute-done((f32[2,32,2,640]{3,2,1,0:T(2,128)}, f32[2,32,2,640]{3,2,1,0:T(2,128)S(1)}, u32[]{:S(2)}, u32[]{:S(2)}) %collective-permute-start.1) | collective-permute-done | bytes 327712 | tf_op jit(solution)/shard_map/ppermute | solution.py:28
  15.5 1.4 collective-permute-start.2
  16.9 1.3 collective-permute-start.3
  18.2 1.0 reshape.1073
  20.1 2.9 %collective-permute-start.4 = (f32[2,256,32]{1,2,0:T(8,128)S(1)}, f32[2,256,32]{1,2,0:T(8,128)S(1)}, u32[]{:S(2)}, u32[]{:S(2)}) collective-permute-start(f32[2,256,32]{1,2,0:T(8,128)S(1)} %fusion.13), channel_id=1, source_target_pairs={{0,1},{1,0},{2,3},{3,2},{4,5},{5,4},{6,7},{7,6},{8,9},{9,8},{10,11... | collective-permute-start | bytes 196616 | tf_op jit(solution)/shard_map/ppermute | solution.py:178
  23.0 0.9 collective-permute-done.4
  23.9 2.1 collective-permute-start.5
  26.0 0.7 copy.77
  26.7 11.0 %all-to-all-start = ((f32[2,32,1]{0,2,1:T(1,128)}), f32[2,32,1]{0,2,1:T(1,128)S(1)}, u32[]{:S(2)}, u32[]{:S(2)}) async-start(f32[2,32,1]{0,2,1:T(1,128)} %copy.77), calls=%async_computation | async-start | bytes 32768 | tf_op jit(solution)/shard_map/all_to_all | solution.py:156
  37.8 2.8 %collective-permute-start.6 = (f32[2,256,32]{1,2,0:T(8,128)S(1)}, f32[2,256,32]{1,2,0:T(8,128)S(1)}, u32[]{:S(2)}, u32[]{:S(2)}) collective-permute-start(f32[2,256,32]{1,2,0:T(8,128)S(1)} %add.591), channel_id=1, source_target_pairs={{0,4},{1,5},{2,6},{3,7},{4,0},{5,1},{6,2},{7,3},{8,12},{9,13},{10,... | collective-permute-start | bytes 196616 | tf_op jit(solution)/shard_map/ppermute | solution.py:178
  41.3 2.4 %collective-permute-done.6 = f32[2,256,32]{1,2,0:T(8,128)S(1)} collective-permute-done((f32[2,256,32]{1,2,0:T(8,128)S(1)}, f32[2,256,32]{1,2,0:T(8,128)S(1)}, u32[]{:S(2)}, u32[]{:S(2)}) %collective-permute-start.6) | collective-permute-done | bytes 65568 | tf_op jit(solution)/shard_map/ppermute | solution.py:178
  43.6 1.1 fusion
  44.7 1.9 reshape.1074
  46.7 5.1 %multiply_subtract_fusion.1 = (f32[2,32,2,640]{3,2,1,0:T(2,128)}, f32[2,32,2,640]{3,2,1,0:T(2,128)S(1)}) fusion(f32[2,32,2,640]{3,2,1,0:T(2,128)S(1)} %copy-done.1, f32[]{:T(128)} %get-tuple-element.5, f32[]{:T(128)} %get-tuple-element.7, f32[2,32,2,640]{3,2,1,0:T(2,128)} %reshape.1074, f32[2,2,640]{2,1,0:T(2,128)S(1)} %copy-done.3, ...), kind=kLoop, calls=%fused_computation.19 | loop fusion | flops 2621440 | bytes 5581824 | tf_op jit(solution)/shard_map/sub | solution.py:217
  51.8 1.3 multiply_subtract_fusion
  55.0 1.4 pad_maximum_fusion
  56.4 9.8 %all-to-all-start.1 = ((f32[2,2,32,1280]{3,0,1,2:T(2,128)}), f32[2,2,32,1280]{3,0,1,2:T(2,128)S(1)}, u32[]{:S(2)}, u32[]{:S(2)}) async-start(f32[2,2,32,1280]{3,0,1,2:T(2,128)} %pad_maximum_fusion), calls=%async_computation.1 | async-start | bytes 1310720 | tf_op jit(solution)/shard_map/all_to_all | solution.py:155
  66.3 0.7 fusion.173
  69.7 0.7 fusion.174
  70.4 0.7 fusion.178
  71.1 0.7 fusion.176
  71.9 0.7 fusion.177
  72.6 0.7 fusion.175
  73.3 11.7 %all-to-all-done.1 = f32[2,2,32,1280]{3,0,1,2:T(2,128)S(1)} async-done(((f32[2,2,32,1280]{3,0,1,2:T(2,128)}), f32[2,2,32,1280]{3,0,1,2:T(2,128)S(1)}, u32[]{:S(2)}, u32[]{:S(2)}) %all-to-all-start.1) | async-done | bytes 655392 | tf_op jit(solution)/shard_map/all_to_all | solution.py:155
  85.0 80.3 %constant_dynamic-update-slice_fusion.66 = (f32[2,64,1,1280]{3,0,2,1:T(2,128)S(1)}, f32[2,1280]{1,0:T(2,128)S(1)}, f32[2,1280]{1,0:T(2,128)S(1)}, f32[2,1280]{1,...) fusion(f32[]{:T(128)} %bitcast.69, f32[]{:T(128)} %bitcast.2, ...), kind=kLoop, calls=%fused_computation.91 | loop fusion | flops 977919 | bytes 1399808
  165.3 1.2 constant_dynamic-update-slice_fusion.64
  166.5 1.3 constant_dynamic-update-slice_fusion.62
  167.8 1.3 constant_dynamic-update-slice_fusion.60
  169.1 1.2 constant_dynamic-update-slice_fusion.58
  170.3 1.3 constant_dynamic-update-slice_fusion.56
  171.6 1.1 constant_dynamic-update-slice_fusion.54
  172.8 1.3 constant_dynamic-update-slice_fusion.52
  174.1 1.3 constant_dynamic-update-slice_fusion.50
  175.4 1.4 constant_dynamic-update-slice_fusion.48
  176.8 1.3 constant_dynamic-update-slice_fusion.46
  178.1 1.3 constant_dynamic-update-slice_fusion.44
  179.4 1.1 constant_dynamic-update-slice_fusion.42
  180.5 1.3 constant_dynamic-update-slice_fusion.40
  181.8 1.3 constant_dynamic-update-slice_fusion.38
  183.1 1.2 constant_dynamic-update-slice_fusion.36
  184.3 1.4 constant_dynamic-update-slice_fusion.34
  185.7 1.3 constant_dynamic-update-slice_fusion.32
  187.0 1.2 constant_dynamic-update-slice_fusion.30
  188.2 1.1 constant_dynamic-update-slice_fusion.28
  189.4 1.3 constant_dynamic-update-slice_fusion.26
  190.7 1.3 constant_dynamic-update-slice_fusion.24
  192.0 1.2 constant_dynamic-update-slice_fusion.22
  193.2 1.2 constant_dynamic-update-slice_fusion.20
  194.4 1.3 constant_dynamic-update-slice_fusion.18
  195.7 1.3 constant_dynamic-update-slice_fusion.16
  197.0 1.4 constant_dynamic-update-slice_fusion.14
  198.4 1.3 constant_dynamic-update-slice_fusion.12
  199.7 1.3 constant_dynamic-update-slice_fusion.10
  200.9 1.2 constant_dynamic-update-slice_fusion.8
  202.2 1.3 constant_dynamic-update-slice_fusion.6
  203.5 2.5 %constant_dynamic-update-slice_fusion.4 = f32[2,64,1,1280]{3,0,2,1:T(2,128)S(1)} fusion(f32[2,64,1,1280]{3,0,2,1:T(2,128)S(1)} %constant_dynamic-update-slice_fusion.5, f32[2,1280]{1,0:T(2,128)S(1)} %get-tuple-element.40, f32[]{:T(128)} %bitcast.253, f32[]{:T(128)} %bitcast.64, f32[2,64,1,1280]{3,0,1,2:T(2,128)S(1)} %bitcast.812, f32[]{:T(128)} %bitcast.66, ...), kind=kLoop, calls=%fused_computation.29 | loop fusion | flops 20480 | bytes 33792
  205.9 1.3 constant_dynamic-update-slice_fusion.3
  207.2 22.6 %all_to_all.49 = f32[2,64,1,1280]{3,0,2,1:T(2,128)S(1)} all-to-all(f32[2,64,1,1280]{3,0,2,1:T(2,128)S(1)} %constant_dynamic-update-slice_fusion.3), channel_id=1, replica_groups=mesh['layer'=32,'xs'=8] {'layer'}, dimensions={1} | all-to-all | bytes 1310720 | tf_op jit(solution)/shard_map/all_to_all | solution.py:171
  229.9 0.7 reshape.1075
  230.6 0.9 copy.143
  (69 shorter events, 5.4 us)
Async XLA Ops:
  0.0 19.2 %copy-start = (bf16[2,64,1280]{2,1,0:T(8,128)(2,1)S(1)}, bf16[2,64,1280]{2,1,0:T(8,128)(2,1)}, u32[]{:S(2)}) copy-start(bf16[2,64,1280]{2,1,0:T(8,128)(2,1)} %param.10) | copy-start | bytes 983044
  0.0 11.7 %copy-start.1 = (f32[2,32,2,640]{3,2,1,0:T(2,128)S(1)}, f32[2,32,2,640]{3,2,1,0:T(2,128)}, u32[]{:S(2)}) copy-start(f32[2,32,2,640]{3,2,1,0:T(2,128)} %param.8) | copy-start | bytes 983044
  0.0 11.7 %collective-permute-start = (f32[2,32,2,640]{3,2,1,0:T(2,128)}, f32[2,32,2,640]{3,2,1,0:T(2,128)S(1)}, u32[]{:S(2)}, u32[]{:S(2)}) collective-permute-start(f32[2,32,2,640]{3,2,1,0:T(2,128)} %param.8), channel_id=1, source_target_pairs={{0,8},{8,16},{16,24},{24,32},{32,40},{40,48},{48,56},{56,64},{64,7... | collective-permute-start | bytes 983048 | tf_op jit(solution)/shard_map/ppermute | solution.py:26
  4.0 11.5 %collective-permute-start.1 = (f32[2,32,2,640]{3,2,1,0:T(2,128)}, f32[2,32,2,640]{3,2,1,0:T(2,128)S(1)}, u32[]{:S(2)}, u32[]{:S(2)}) collective-permute-start(f32[2,32,2,640]{3,2,1,0:T(2,128)} %param.8), channel_id=1, source_target_pairs={{8,0},{16,8},{24,16},{32,24},{40,32},{48,40},{56,48},{64,56},{72,6... | collective-permute-start | bytes 983048 | tf_op jit(solution)/shard_map/ppermute | solution.py:28
  15.5 31.1 %collective-permute-start.2 = (f32[6,32,2,640]{3,2,1,0:T(2,128)S(1)}, f32[6,32,2,640]{3,2,1,0:T(2,128)S(1)}, u32[]{:S(2)}, u32[]{:S(2)}) collective-permute-start(f32[6,32,2,640]{3,2,1,0:T(2,128)S(1)} %constant_dynamic-update-slice_fusion), channel_id=1, source_target_pairs={{0,1},{1,2},{2,3},{3,4},{4,5},{5,6},{6,7},{8,9},{9,10},{10,11},{11... | collective-permute-start | bytes 2949128 | tf_op jit(solution)/shard_map/ppermute | solution.py:26
  16.9 29.8 %collective-permute-start.3 = (f32[6,32,2,640]{3,2,1,0:T(2,128)S(1)}, f32[6,32,2,640]{3,2,1,0:T(2,128)}, u32[]{:S(2)}, u32[]{:S(2)}) collective-permute-start(f32[6,32,2,640]{3,2,1,0:T(2,128)S(1)} %constant_dynamic-update-slice_fusion), channel_id=1, source_target_pairs={{1,0},{2,1},{3,2},{4,3},{5,4},{6,5},{7,6},{9,8},{10,9},{11,10},{12... | collective-permute-start | bytes 2949128 | tf_op jit(solution)/shard_map/ppermute | solution.py:28
  19.2 0.7 copy-start.4
  20.1 3.8 %collective-permute-start.4 = (f32[2,256,32]{1,2,0:T(8,128)S(1)}, f32[2,256,32]{1,2,0:T(8,128)S(1)}, u32[]{:S(2)}, u32[]{:S(2)}) collective-permute-start(f32[2,256,32]{1,2,0:T(8,128)S(1)} %fusion.13), channel_id=1, source_target_pairs={{0,1},{1,0},{2,3},{3,2},{4,5},{5,4},{6,7},{7,6},{8,9},{9,8},{10,11... | collective-permute-start | bytes 196616 | tf_op jit(solution)/shard_map/ppermute | solution.py:178
  23.9 2.1 copy-start.6
  23.9 13.8 %collective-permute-start.5 = (f32[2,256,32]{1,2,0:T(8,128)S(1)}, f32[2,256,32]{1,2,0:T(8,128)S(1)}, u32[]{:S(2)}, u32[]{:S(2)}) collective-permute-start(f32[2,256,32]{1,2,0:T(8,128)S(1)} %add.590), channel_id=1, source_target_pairs={{0,2},{1,3},{2,0},{3,1},{4,6},{5,7},{6,4},{7,5},{8,10},{9,11},{10,... | collective-permute-start | bytes 196616 | tf_op jit(solution)/shard_map/ppermute | solution.py:178
  26.7 29.7 %all-to-all-start = ((f32[2,32,1]{0,2,1:T(1,128)}), f32[2,32,1]{0,2,1:T(1,128)S(1)}, u32[]{:S(2)}, u32[]{:S(2)}) async-start(f32[2,32,1]{0,2,1:T(1,128)} %copy.77), calls=%async_computation | async-start | bytes 32768 | tf_op jit(solution)/shard_map/all_to_all | solution.py:156
  37.7 2.9 %copy-start.7 = (f32[4]{0:T(128)S(1)}, f32[4]{0:T(128)}, u32[]{:S(2)}) copy-start(f32[4]{0:T(128)} %param.15) | copy-start | bytes 52
  37.7 2.9 %copy-start.8 = (f32[4]{0:T(128)S(1)}, f32[4]{0:T(128)}, u32[]{:S(2)}) copy-start(f32[4]{0:T(128)} %param.14) | copy-start | bytes 52
  37.8 5.9 %copy-start.5 = (f32[2,256]{1,0:T(2,128)S(1)}, f32[2,256]{1,0:T(2,128)}, u32[]{:S(2)}) copy-start(f32[2,256]{1,0:T(2,128)} %param.12) | copy-start | bytes 6148
  37.8 5.9 %collective-permute-start.6 = (f32[2,256,32]{1,2,0:T(8,128)S(1)}, f32[2,256,32]{1,2,0:T(8,128)S(1)}, u32[]{:S(2)}, u32[]{:S(2)}) collective-permute-start(f32[2,256,32]{1,2,0:T(8,128)S(1)} %add.591), channel_id=1, source_target_pairs={{0,4},{1,5},{2,6},{3,7},{4,0},{5,1},{6,2},{7,3},{8,12},{9,13},{10,... | collective-permute-start | bytes 196616 | tf_op jit(solution)/shard_map/ppermute | solution.py:178
  44.7 1.9 copy-start.3
  53.4 1.0 copy-start.2
  56.4 28.6 %all-to-all-start.1 = ((f32[2,2,32,1280]{3,0,1,2:T(2,128)}), f32[2,2,32,1280]{3,0,1,2:T(2,128)S(1)}, u32[]{:S(2)}, u32[]{:S(2)}) async-start(f32[2,2,32,1280]{3,0,1,2:T(2,128)} %pad_maximum_fusion), calls=%async_computation.1 | async-start | bytes 1310720 | tf_op jit(solution)/shard_map/all_to_all | solution.py:155

commit v4 on v3

--- a/solution.py
+++ b/solution.py
@@ -149,26 +149,44 @@
         o_ref[:, index] = back[index] + upper[None] * from_above
 
 
+def local_sweep_kernel(r_ref, f_ref, o_ref):
+    total = f_ref.shape[0]
+    here = f_ref.shape[2]
+    for column in range(here):
+
+        def forward(index, state):
+            rate = r_ref[index, column]
+            state = rate * state + (1.0 - rate) * f_ref[index, :, column]
+            o_ref[index, :, column] = state
+            return state
+
+        zero = jnp.zeros(f_ref.shape[1:2] + f_ref.shape[3:], jnp.float32)
+        lax.fori_loop(0, total, forward, zero)
+
+        def backward(step, state):
+            index = total - 1 - step
+            rate = r_ref[index, column]
+            state = rate * state + (1.0 - rate) * o_ref[index, :, column]
+            o_ref[index, :, column] = state
+            return state
+
+        lax.fori_loop(0, total, backward, zero)
+
+
 def sweeps(forcing, decay_rates):
-    moments, layers, columns, rows, depth = forcing.shape
-    flat = forcing.reshape(moments, layers, columns, rows * depth)
-    whole = lax.all_to_all(flat, "layer", 2, 1, tiled=True)
+    layers, moments, columns, width = forcing.shape
+    whole = lax.all_to_all(forcing, "layer", 2, 0, tiled=True)
     rates = lax.all_to_all(decay_rates, "layer", 1, 0, tiled=True)
-    total = whole.shape[1]
-    rate = rates[:, None, :, None]
-    keep = 1.0 - rate
-    state = jnp.zeros_like(whole[:, 0])
-    ahead = []
-    for index in range(total):
-        state = rate[index] * state + keep[index] * whole[:, index]
-        ahead.append(state)
-    state = jnp.zeros_like(whole[:, 0])
-    back = [None] * total
-    for index in reversed(range(total)):
-        state = rate[index] * state + keep[index] * ahead[index]
-        back[index] = state
-    swept = jnp.stack(back, axis=1)
-    return lax.all_to_all(swept, "layer", 1, 2, tiled=True).reshape(forcing.shape)
+    total, _, here, _ = whole.shape
+    tiles = whole.reshape(total, moments, here, width // 128, 128)
+    swept = pl.pallas_call(
+        local_sweep_kernel,
+        out_shape=jax.ShapeDtypeStruct(tiles.shape, jnp.float32),
+        in_specs=[pl.BlockSpec(memory_space=pltpu.SMEM), pl.BlockSpec(memory_space=pltpu.VMEM)],
+        out_specs=pl.BlockSpec(memory_space=pltpu.VMEM),
+    )(rates, tiles)
+    swept = swept.reshape(total, moments, here, width)
+    return lax.all_to_all(swept, "layer", 0, 2, tiled=True)
 
 
 def plane_sum(x, axis):
@@ -214,8 +232,9 @@
     w0 = jnp.sum(node_weights)
     w1 = jnp.sum(node_weights * contour_nodes)
     w2 = jnp.sum(node_weights * contour_nodes * contour_nodes)
-    forcing = jnp.stack([w0 * hamil - w1 * probes, w1 * hamil - w2 * probes])
-    return sweeps(forcing, decay_rates)
+    forcing = jnp.stack([w0 * hamil - w1 * probes, w1 * hamil - w2 * probes], axis=1)
+    swept = sweeps(forcing.reshape(layers, 2, columns, rows * depth), decay_rates)
+    return jnp.swapaxes(swept, 0, 1).reshape(2, layers, columns, rows, depth)
 
 
 def solution(mesh):

time: 234 us -> 116 us (0.50)
  other arithmetic: 131 us -> 9.25 us
  waiting for transfers between devices: 23.5 us -> 29.9 us
  Pallas kernels: 0 us -> 3.38 us
  local copies, waits for them, and re-layouts: 13.9 us -> 11.5 us
    unnamed x33 -> x1, other arithmetic: 121 us -> 0.84 us
    all_to_all x1, waiting for transfers between devices: 11.7 us -> 18.1 us  [sweeps(): whole = lax.all_to_all(forcing, 'layer', 2, 0, tiled=True)]
    slice x8 -> x0, local copies, waits for them, and re-layouts: 5.7 us -> none  [the longest x5 3.56 us: sweeps(): state = rate[index] * state + keep[index] * ahead[index]]
    pallas_call x0 -> x1, Pallas kernels: none -> 3.38 us  [sweeps(): pl.pallas_call(local_sweep_kernel, out_shape=jax.ShapeDtypeStruct(tiles.s...]
    reshape x2 -> x4, local copies, waits for them, and re-layouts: 1.67 us -> 4.74 us  [the longest x2 1.67 us: shards(): return jnp.swapaxes(swept, 0, 1).reshape(2, layers, columns, rows, depth)]
    sub x3 -> x2, other arithmetic: 6.45 us -> 6.33 us  [the longest x1 5.09 us: shards(): w0 * hamil - w1 * probes]
  transfers between devices with their start and end apart: 9 -> 9, of which waited for: 5 -> 5; matrix products, arithmetic and copies ran while one was open for 9% -> 14% of each run, Pallas kernels for 0% -> 0%
where the time goes in v4:
time: 116 us
  starting transfers between devices  37.2 us (32%)
  waiting for transfers between devices  29.9 us (26%)
  blocking collectives  22.6 us (19%)
  local copies, waits for them, and re-layouts  11.5 us (10%)
  other arithmetic  9.25 us (8%)
  Pallas kernels  3.38 us (3%)
  matrix products  1.54 us (1%)
    all_to_all x1, blocking collectives, sweeps(): return lax.all_to_all(swept, 'layer', 0, 2, tiled=True)  22.6 us
    all_to_all x1, waiting for transfers between devices, sweeps(): whole = lax.all_to_all(forcing, 'layer', 2, 0, tiled=True)  18.1 us
    all_to_all x1, starting transfers between devices, sweeps(): rates = lax.all_to_all(decay_rates, 'layer', 1, 0, tiled=True)  11 us
    all_to_all x1, starting transfers between devices, sweeps(): whole = lax.all_to_all(forcing, 'layer', 2, 0, tiled=True)  9.79 us
    ppermute x3, starting transfers between devices, plane_sum(): x = x + lax.ppermute(x, axis, [(i, i ^ step) for i in range(count)])  7.75 us
    ppermute x2, waiting for transfers between devices, with_halo(): lax.ppermute(tail, axis, [(i, (i + 1) % count) for i in range(ends)])  5.68 us
    ppermute x2, starting transfers between devices, with_halo(): lax.ppermute(tail, axis, [(i, (i + 1) % count) for i in range(ends)])  5.3 us
    sub x1, other arithmetic, shards(): w0 * hamil - w1 * probes  5.09 us
  transfers between devices with their start and end apart: 9, of which 5 were waited for; matrix products, arithmetic and copies ran while one was open for 14% of the time, Pallas kernels for 0%

profile of v4, /device:TPU:32, one launch (start us, length us, event | category | flops | bytes accessed | tf_op | source)
XLA Modules:
  0.0 115.6 jit_solution(8973022137574573874)
XLA Ops:
  0.0 0.0 copy-start
  0.0 0.0 copy-start.1
  0.0 3.9 %collective-permute-start = (f32[2,32,2,640]{3,2,1,0:T(2,128)}, f32[2,32,2,640]{3,2,1,0:T(2,128)S(1)}, u32[]{:S(2)}, u32[]{:S(2)}) collective-permute-start(f32[2,32,2,640]{3,2,1,0:T(2,128)} %param.8), channel_id=1, source_target_pairs={{0,8},{8,16},{16,24},{24,32},{32,40},{40,48},{48,56},{56,64},{64,7... | collective-permute-start | bytes 983048 | tf_op jit(solution)/shard_map/ppermute | solution.py:26
  4.0 2.0 %collective-permute-start.1 = (f32[2,32,2,640]{3,2,1,0:T(2,128)}, f32[2,32,2,640]{3,2,1,0:T(2,128)S(1)}, u32[]{:S(2)}, u32[]{:S(2)}) collective-permute-start(f32[2,32,2,640]{3,2,1,0:T(2,128)} %param.8), channel_id=1, source_target_pairs={{8,0},{16,8},{24,16},{32,24},{40,32},{48,40},{56,48},{64,56},{72,6... | collective-permute-start | bytes 983048 | tf_op jit(solution)/shard_map/ppermute | solution.py:28
  6.0 5.7 %collective-permute-done = f32[2,32,2,640]{3,2,1,0:T(2,128)S(1)} collective-permute-done((f32[2,32,2,640]{3,2,1,0:T(2,128)}, f32[2,32,2,640]{3,2,1,0:T(2,128)S(1)}, u32[]{:S(2)}, u32[]{:S(2)}) %collective-permute-start) | collective-permute-done | bytes 327712 | tf_op jit(solution)/shard_map/ppermute | solution.py:26
  11.7 0.0 copy-done.1
  11.7 0.8 constant_dynamic-update-slice_fusion.1
  12.6 2.8 %collective-permute-done.1 = f32[2,32,2,640]{3,2,1,0:T(2,128)S(1)} collective-permute-done((f32[2,32,2,640]{3,2,1,0:T(2,128)}, f32[2,32,2,640]{3,2,1,0:T(2,128)S(1)}, u32[]{:S(2)}, u32[]{:S(2)}) %collective-permute-start.1) | collective-permute-done | bytes 327712 | tf_op jit(solution)/shard_map/ppermute | solution.py:28
  15.4 0.1 constant_dynamic-update-slice_fusion
  15.5 1.4 %collective-permute-start.2 = (f32[6,32,2,640]{3,2,1,0:T(2,128)S(1)}, f32[6,32,2,640]{3,2,1,0:T(2,128)S(1)}, u32[]{:S(2)}, u32[]{:S(2)}) collective-permute-start(f32[6,32,2,640]{3,2,1,0:T(2,128)S(1)} %constant_dynamic-update-slice_fusion), channel_id=1, source_target_pairs={{0,1},{1,2},{2,3},{3,4},{4,5},{5,6},{6,7},{8,9},{9,10},{10,11},{11... | collective-permute-start | bytes 2949128 | tf_op jit(solution)/shard_map/ppermute | solution.py:26
  16.9 1.3 %collective-permute-start.3 = (f32[6,32,2,640]{3,2,1,0:T(2,128)S(1)}, f32[6,32,2,640]{3,2,1,0:T(2,128)}, u32[]{:S(2)}, u32[]{:S(2)}) collective-permute-start(f32[6,32,2,640]{3,2,1,0:T(2,128)S(1)} %constant_dynamic-update-slice_fusion), channel_id=1, source_target_pairs={{1,0},{2,1},{3,2},{4,3},{5,4},{6,5},{7,6},{9,8},{10,9},{11,10},{12... | collective-permute-start | bytes 2949128 | tf_op jit(solution)/shard_map/ppermute | solution.py:28
  18.2 1.0 reshape.27
  19.2 0.0 copy-done
  19.2 0.0 copy-start.4
  19.2 0.2 fusion.19
  19.4 0.5 copy-done.4
  19.9 0.2 fusion.13
  20.1 2.9 %collective-permute-start.4 = (f32[2,256,32]{1,2,0:T(8,128)S(1)}, f32[2,256,32]{1,2,0:T(8,128)S(1)}, u32[]{:S(2)}, u32[]{:S(2)}) collective-permute-start(f32[2,256,32]{1,2,0:T(8,128)S(1)} %fusion.13), channel_id=1, source_target_pairs={{0,1},{1,0},{2,3},{3,2},{4,5},{5,4},{6,7},{7,6},{8,9},{9,8},{10,11... | collective-permute-start | bytes 196616 | tf_op jit(solution)/shard_map/ppermute | solution.py:196
  23.0 0.9 collective-permute-done.4
  23.9 0.0 copy-start.6
  23.9 2.1 %collective-permute-start.5 = (f32[2,256,32]{1,2,0:T(8,128)S(1)}, f32[2,256,32]{1,2,0:T(8,128)S(1)}, u32[]{:S(2)}, u32[]{:S(2)}) collective-permute-start(f32[2,256,32]{1,2,0:T(8,128)S(1)} %add.74), channel_id=1, source_target_pairs={{0,2},{1,3},{2,0},{3,1},{4,6},{5,7},{6,4},{7,5},{8,10},{9,11},{10,... | collective-permute-start | bytes 196616 | tf_op jit(solution)/shard_map/ppermute | solution.py:196
  26.0 0.0 copy-done.6
  26.0 0.7 copy.21
  26.7 11.0 %all-to-all-start = ((f32[2,32,1]{0,2,1:T(1,128)}), f32[2,32,1]{0,2,1:T(1,128)S(1)}, u32[]{:S(2)}, u32[]{:S(2)}) async-start(f32[2,32,1]{0,2,1:T(1,128)} %copy.21), calls=%async_computation | async-start | bytes 32768 | tf_op jit(solution)/shard_map/all_to_all | solution.py:179
  37.7 0.0 copy-start.7
  37.7 0.0 copy-start.8
  37.7 0.0 collective-permute-done.5
  37.8 0.0 copy-start.5
  37.8 2.8 %collective-permute-start.6 = (f32[2,256,32]{1,2,0:T(8,128)S(1)}, f32[2,256,32]{1,2,0:T(8,128)S(1)}, u32[]{:S(2)}, u32[]{:S(2)}) collective-permute-start(f32[2,256,32]{1,2,0:T(8,128)S(1)} %add.75), channel_id=1, source_target_pairs={{0,4},{1,5},{2,6},{3,7},{4,0},{5,1},{6,2},{7,3},{8,12},{9,13},{10,... | collective-permute-start | bytes 196616 | tf_op jit(solution)/shard_map/ppermute | solution.py:196
  40.6 0.0 copy-done.7
  40.6 0.0 copy-done.8
  40.6 0.6 multiply_reduce_fusion.1
  41.2 2.4 %collective-permute-done.6 = f32[2,256,32]{1,2,0:T(8,128)S(1)} collective-permute-done((f32[2,256,32]{1,2,0:T(8,128)S(1)}, f32[2,256,32]{1,2,0:T(8,128)S(1)}, u32[]{:S(2)}, u32[]{:S(2)}) %collective-permute-start.6) | collective-permute-done | bytes 65568 | tf_op jit(solution)/shard_map/ppermute | solution.py:196
  43.6 0.0 copy-done.5
  43.6 1.1 fusion
  44.7 0.0 copy-start.3
  44.7 1.9 %reshape.28 = f32[2,32,2,640]{3,2,1,0:T(2,128)} reshape(f32[2,32,1280]{2,1,0:T(8,128)} %fusion) | data formatting | bytes 655360 | tf_op jit(solution)/shard_map/reshape | solution.py:230
  46.6 0.0 collective-permute-done.2
  46.6 0.0 collective-permute-done.3
  46.6 0.0 copy-done.3
  46.7 5.1 %multiply_subtract_fusion.1 = (f32[2,32,2,640]{3,2,1,0:T(2,128)}, f32[2,32,2,640]{3,2,1,0:T(2,128)S(1)}) fusion(f32[2,32,2,640]{3,2,1,0:T(2,128)S(1)} %copy-done.1, f32[]{:T(128)} %get-tuple-element.5, f32[]{:T(128)} %get-tuple-element.7, f32[2,32,2,640]{3,2,1,0:T(2,128)} %reshape.28, f32[2,2,640]{2,1,0:T(2,128)S(1)} %copy-done.3, ...), kind=kLoop, calls=%fused_computation.19 | loop fusion | flops 2621440 | bytes 5581824 | tf_op jit(solution)/shard_map/sub | solution.py:235
  51.7 1.2 %multiply_subtract_fusion = f32[2,8,8,640]{3,2,1,0:T(8,128)S(1)} fusion(f32[2,8,8,640]{3,2,1,0:T(8,128)S(1)} %bitcast.27, f32[2,8,8,640]{3,2,1,0:T(8,128)S(1)} %bitcast.31, f32[]{:T(128)} %get-tuple-element.6, f32[]{:T(128)} %get-tuple-element.5), kind=kLoop, calls=%fused_computation.18 | loop fusion | flops 245760 | bytes 983048 | tf_op jit(solution)/shard_map/sub | solution.py:235
  53.0 0.3 stack.10
  53.3 0.0 copy-start.2
  53.3 0.3 copy.23
  53.6 0.6 copy-done.2
  54.2 0.3 stack.9
  54.5 0.3 copy.22
  54.8 1.4 %pad_maximum_fusion = f32[2,2,32,1280]{3,1,0,2:T(2,128)} fusion(f32[2,1,32,1280]{3,1,0,2:T(1,128)S(1)} %copy.23, f32[2,1,32,1280]{3,1,0,2:T(1,128)S(1)} %copy.22), kind=kLoop, calls=%fused_computation.2 | loop fusion | flops 163840 | bytes 1310720 | tf_op jit(solution)/shard_map/stack | solution.py:235
  56.3 0.0 all-to-all-done
  56.3 9.8 %all-to-all-start.1 = ((f32[2,2,32,1280]{3,1,0,2:T(2,128)}), f32[2,2,32,1280]{3,1,0,2:T(2,128)S(1)}, u32[]{:S(2)}, u32[]{:S(2)}) async-start(f32[2,2,32,1280]{3,1,0,2:T(2,128)} %pad_maximum_fusion), calls=%async_computation.1 | async-start | bytes 1310720 | tf_op jit(solution)/shard_map/all_to_all | solution.py:178
  66.1 0.7 all_to_all.49.r_ref
  66.8 18.1 %all-to-all-done.1 = f32[2,2,32,1280]{3,1,0,2:T(2,128)S(1)} async-done(((f32[2,2,32,1280]{3,1,0,2:T(2,128)}), f32[2,2,32,1280]{3,1,0,2:T(2,128)S(1)}, u32[]{:S(2)}, u32[]{:S(2)}) %all-to-all-start.1) | async-done | bytes 655392 | tf_op jit(solution)/shard_map/all_to_all | solution.py:178
  84.9 1.5 %reshape.29 = f32[64,2,1,10,128]{4,3,1,0,2:T(8,128)} reshape(f32[32,2,2,1,1280]{4,2,1,0,3:T(2,128)S(1)} %bitcast.28) | data formatting | bytes 1310720 | tf_op jit(solution)/shard_map/reshape | solution.py:181
  86.4 3.4 %shard_map.82 = f32[64,2,1,10,128]{4,3,2,1,0:T(8,128)} custom-call(f32[64,1]{1,0:T(8,128)} %all_to_all.49.r_ref, f32[64,2,1,10,128]{4,3,2,1,0:T(8,128)} %bitcast.26), custom_call_target="tpu_custom_call" | custom-call | tf_op jit(solution)/shard_map/pallas_call | solution.py:182
  89.7 1.6 %reshape.32 = f32[64,2,1,1280]{3,1,0,2:T(2,128)S(1)} reshape(f32[64,2,1,10,128]{4,3,2,1,0:T(8,128)} %shard_map.82) | data formatting | bytes 1310720 | tf_op jit(solution)/shard_map/reshape | solution.py:188
  91.3 22.6 %all_to_all.53 = f32[64,2,1,1280]{3,1,2,0:T(2,128)S(1)} all-to-all(f32[64,2,1,1280]{3,1,2,0:T(2,128)S(1)} %bitcast.29), channel_id=1, replica_groups=mesh['layer'=32,'xs'=8] {'layer'}, dimensions={0} | all-to-all | bytes 1310720 | tf_op jit(solution)/shard_map/all_to_all | solution.py:189
  114.0 0.7 reshape.33
  114.7 0.9 copy.31
  (4 shorter events, 0.1 us)
Async XLA Ops:
  0.0 19.2 %copy-start = (bf16[2,64,1280]{2,1,0:T(8,128)(2,1)S(1)}, bf16[2,64,1280]{2,1,0:T(8,128)(2,1)}, u32[]{:S(2)}) copy-start(bf16[2,64,1280]{2,1,0:T(8,128)(2,1)} %param.10) | copy-start | bytes 983044
  0.0 11.7 %copy-start.1 = (f32[2,32,2,640]{3,2,1,0:T(2,128)S(1)}, f32[2,32,2,640]{3,2,1,0:T(2,128)}, u32[]{:S(2)}) copy-start(f32[2,32,2,640]{3,2,1,0:T(2,128)} %param.8) | copy-start | bytes 983044
  0.0 11.7 %collective-permute-start = (f32[2,32,2,640]{3,2,1,0:T(2,128)}, f32[2,32,2,640]{3,2,1,0:T(2,128)S(1)}, u32[]{:S(2)}, u32[]{:S(2)}) collective-permute-start(f32[2,32,2,640]{3,2,1,0:T(2,128)} %param.8), channel_id=1, source_target_pairs={{0,8},{8,16},{16,24},{24,32},{32,40},{40,48},{48,56},{56,64},{64,7... | collective-permute-start | bytes 983048 | tf_op jit(solution)/shard_map/ppermute | solution.py:26
  4.0 11.5 %collective-permute-start.1 = (f32[2,32,2,640]{3,2,1,0:T(2,128)}, f32[2,32,2,640]{3,2,1,0:T(2,128)S(1)}, u32[]{:S(2)}, u32[]{:S(2)}) collective-permute-start(f32[2,32,2,640]{3,2,1,0:T(2,128)} %param.8), channel_id=1, source_target_pairs={{8,0},{16,8},{24,16},{32,24},{40,32},{48,40},{56,48},{64,56},{72,6... | collective-permute-start | bytes 983048 | tf_op jit(solution)/shard_map/ppermute | solution.py:28
  15.5 31.1 %collective-permute-start.2 = (f32[6,32,2,640]{3,2,1,0:T(2,128)S(1)}, f32[6,32,2,640]{3,2,1,0:T(2,128)S(1)}, u32[]{:S(2)}, u32[]{:S(2)}) collective-permute-start(f32[6,32,2,640]{3,2,1,0:T(2,128)S(1)} %constant_dynamic-update-slice_fusion), channel_id=1, source_target_pairs={{0,1},{1,2},{2,3},{3,4},{4,5},{5,6},{6,7},{8,9},{9,10},{10,11},{11... | collective-permute-start | bytes 2949128 | tf_op jit(solution)/shard_map/ppermute | solution.py:26
  16.9 29.8 %collective-permute-start.3 = (f32[6,32,2,640]{3,2,1,0:T(2,128)S(1)}, f32[6,32,2,640]{3,2,1,0:T(2,128)}, u32[]{:S(2)}, u32[]{:S(2)}) collective-permute-start(f32[6,32,2,640]{3,2,1,0:T(2,128)S(1)} %constant_dynamic-update-slice_fusion), channel_id=1, source_target_pairs={{1,0},{2,1},{3,2},{4,3},{5,4},{6,5},{7,6},{9,8},{10,9},{11,10},{12... | collective-permute-start | bytes 2949128 | tf_op jit(solution)/shard_map/ppermute | solution.py:28
  19.2 0.7 copy-start.4
  20.1 3.8 %collective-permute-start.4 = (f32[2,256,32]{1,2,0:T(8,128)S(1)}, f32[2,256,32]{1,2,0:T(8,128)S(1)}, u32[]{:S(2)}, u32[]{:S(2)}) collective-permute-start(f32[2,256,32]{1,2,0:T(8,128)S(1)} %fusion.13), channel_id=1, source_target_pairs={{0,1},{1,0},{2,3},{3,2},{4,5},{5,4},{6,7},{7,6},{8,9},{9,8},{10,11... | collective-permute-start | bytes 196616 | tf_op jit(solution)/shard_map/ppermute | solution.py:196
  23.9 2.1 %copy-start.6 = (f32[2,32]{1,0:T(2,128)S(1)}, f32[2,32]{1,0:T(2,128)}, u32[]{:S(2)}) copy-start(f32[2,32]{1,0:T(2,128)} %param.13) | copy-start | bytes 772
  23.9 13.8 %collective-permute-start.5 = (f32[2,256,32]{1,2,0:T(8,128)S(1)}, f32[2,256,32]{1,2,0:T(8,128)S(1)}, u32[]{:S(2)}, u32[]{:S(2)}) collective-permute-start(f32[2,256,32]{1,2,0:T(8,128)S(1)} %add.74), channel_id=1, source_target_pairs={{0,2},{1,3},{2,0},{3,1},{4,6},{5,7},{6,4},{7,5},{8,10},{9,11},{10,... | collective-permute-start | bytes 196616 | tf_op jit(solution)/shard_map/ppermute | solution.py:196
  26.7 29.6 %all-to-all-start = ((f32[2,32,1]{0,2,1:T(1,128)}), f32[2,32,1]{0,2,1:T(1,128)S(1)}, u32[]{:S(2)}, u32[]{:S(2)}) async-start(f32[2,32,1]{0,2,1:T(1,128)} %copy.21), calls=%async_computation | async-start | bytes 32768 | tf_op jit(solution)/shard_map/all_to_all | solution.py:179
  37.7 2.9 %copy-start.7 = (f32[4]{0:T(128)S(1)}, f32[4]{0:T(128)}, u32[]{:S(2)}) copy-start(f32[4]{0:T(128)} %param.15) | copy-start | bytes 52
  37.7 2.9 %copy-start.8 = (f32[4]{0:T(128)S(1)}, f32[4]{0:T(128)}, u32[]{:S(2)}) copy-start(f32[4]{0:T(128)} %param.14) | copy-start | bytes 52
  37.8 5.9 %copy-start.5 = (f32[2,256]{1,0:T(2,128)S(1)}, f32[2,256]{1,0:T(2,128)}, u32[]{:S(2)}) copy-start(f32[2,256]{1,0:T(2,128)} %param.12) | copy-start | bytes 6148
  37.8 5.9 %collective-permute-start.6 = (f32[2,256,32]{1,2,0:T(8,128)S(1)}, f32[2,256,32]{1,2,0:T(8,128)S(1)}, u32[]{:S(2)}, u32[]{:S(2)}) collective-permute-start(f32[2,256,32]{1,2,0:T(8,128)S(1)} %add.75), channel_id=1, source_target_pairs={{0,4},{1,5},{2,6},{3,7},{4,0},{5,1},{6,2},{7,3},{8,12},{9,13},{10,... | collective-permute-start | bytes 196616 | tf_op jit(solution)/shard_map/ppermute | solution.py:196
  44.7 1.9 %copy-start.3 = (f32[2,2,640]{2,1,0:T(2,128)S(1)}, f32[2,2,640]{2,1,0:T(2,128)}, u32[]{:S(2)}) copy-start(f32[2,2,640]{2,1,0:T(2,128)} %param.9) | copy-start | bytes 30724
  53.3 1.0 copy-start.2
  56.3 28.6 %all-to-all-start.1 = ((f32[2,2,32,1280]{3,1,0,2:T(2,128)}), f32[2,2,32,1280]{3,1,0,2:T(2,128)S(1)}, u32[]{:S(2)}, u32[]{:S(2)}) async-start(f32[2,2,32,1280]{3,1,0,2:T(2,128)} %pad_maximum_fusion), calls=%async_computation.1 | async-start | bytes 1310720 | tf_op jit(solution)/shard_map/all_to_all | solution.py:178

commit v5 on v2

--- a/solution.py
+++ b/solution.py
@@ -149,27 +149,130 @@
         o_ref[:, index] = back[index] + upper[None] * from_above
 
 
+def exchange_kernel(count, ext_ref, out_ref, gathered, swept, send_sem, recv_sem, back_send, back_recv):
+    me = lax.axis_index("layer")
+    row = lax.axis_index("xs")
+    layers = ext_ref.shape[1]
+    tiles = out_ref.shape[3]
+    barrier = pltpu.get_barrier_semaphore()
+
+    def greet(step, carry):
+        pl.semaphore_signal(
+            barrier, inc=1, device_id=(lax.rem(me + step, count), row), device_id_type=MESH
+        )
+        return carry
+
+    lax.fori_loop(1, count, greet, 0)
+    pl.semaphore_wait(barrier, count - 1)
+
+    def outgoing(step, carry):
+        target = lax.rem(me + step, count)
+        pltpu.make_async_remote_copy(
+            src_ref=ext_ref.at[target],
+            dst_ref=gathered.at[me],
+            send_sem=send_sem.at[step],
+            recv_sem=recv_sem.at[step],
+            device_id=(target, row),
+            device_id_type=MESH,
+        ).start()
+        return carry
+
+    lax.fori_loop(1, count, outgoing, 0)
+    gathered[me] = ext_ref[me]
+
+    def arrived(step, carry):
+        copy = pltpu.make_async_remote_copy(
+            src_ref=ext_ref.at[me],
+            dst_ref=gathered.at[lax.rem(me + count - step, count)],
+            send_sem=send_sem.at[step],
+            recv_sem=recv_sem.at[step],
+            device_id=(lax.rem(me + step, count), row),
+            device_id_type=MESH,
+        )
+        copy.wait_send()
+        copy.wait_recv()
+        return carry
+
+    lax.fori_loop(1, count, arrived, 0)
+
+    zero = jnp.zeros(out_ref.shape[2:], jnp.float32)
+
+    def forward(source, state):
+        for layer in range(layers):
+            slab = gathered[source, layer]
+            rate = slab[0, tiles]
+            state = rate * state + (1.0 - rate) * slab[:, :tiles]
+            swept[source, layer] = state
+        return state
+
+    lax.fori_loop(0, count, forward, zero)
+
+    def backward(step, state):
+        source = count - 1 - step
+        for layer in reversed(range(layers)):
+            rate = gathered[source, layer, 0, tiles]
+            state = rate * state + (1.0 - rate) * swept[source, layer]
+            swept[source, layer] = state
+        return state
+
+    lax.fori_loop(0, count, backward, zero)
+
+    def returning(step, carry):
+        target = lax.rem(me + step, count)
+        pltpu.make_async_remote_copy(
+            src_ref=swept.at[target],
+            dst_ref=out_ref.at[me],
+            send_sem=back_send.at[step],
+            recv_sem=back_recv.at[step],
+            device_id=(target, row),
+            device_id_type=MESH,
+        ).start()
+        return carry
+
+    lax.fori_loop(1, count, returning, 0)
+    out_ref[me] = swept[me]
+
+    def returned(step, carry):
+        copy = pltpu.make_async_remote_copy(
+            src_ref=swept.at[me],
+            dst_ref=out_ref.at[lax.rem(me + count - step, count)],
+            send_sem=back_send.at[step],
+            recv_sem=back_recv.at[step],
+            device_id=(lax.rem(me + step, count), row),
+            device_id_type=MESH,
+        )
+        copy.wait_send()
+        copy.wait_recv()
+        return carry
+
+    lax.fori_loop(1, count, returned, 0)
+
+
 def sweeps(forcing, decay_rates):
-    moments, layers, columns, rows, depth = forcing.shape
-    width = rows * depth
+    layers, moments, columns, width = forcing.shape
     count = lax.axis_size("layer")
-    spans, _ = spans_of(count)
-    rounds = len(spans) + 2
-    flat = forcing.reshape(moments, layers, columns, width)
+    if columns != count:
+        raise ValueError("columns")
+    tiles = width // 128
+    lanes = jnp.broadcast_to(decay_rates[:, None, :, None], (layers, moments, columns, 128))
+    ext = jnp.concatenate([forcing, lanes], axis=3).reshape(layers, moments, columns, tiles + 1, 128)
+    ext = jnp.transpose(ext, (2, 0, 1, 3, 4))
     out = pl.pallas_call(
-        functools.partial(sweep_kernel, count),
-        out_shape=jax.ShapeDtypeStruct(flat.shape, jnp.float32),
-        in_specs=[pl.BlockSpec(memory_space=pltpu.VMEM)] * 2,
+        functools.partial(exchange_kernel, count),
+        out_shape=jax.ShapeDtypeStruct((columns, layers, moments, tiles, 128), jnp.float32),
+        in_specs=[pl.BlockSpec(memory_space=pltpu.VMEM)],
         out_specs=pl.BlockSpec(memory_space=pltpu.VMEM),
         scratch_shapes=[
-            pltpu.VMEM((2, rounds, moments, columns, width + 128), jnp.float32),
-            pltpu.VMEM((2, rounds, moments, columns, width + 128), jnp.float32),
-            pltpu.SemaphoreType.DMA((2, rounds)),
-            pltpu.SemaphoreType.DMA((2, rounds)),
+            pltpu.VMEM((count, layers, moments, tiles + 1, 128), jnp.float32),
+            pltpu.VMEM((count, layers, moments, tiles, 128), jnp.float32),
+            pltpu.SemaphoreType.DMA((count,)),
+            pltpu.SemaphoreType.DMA((count,)),
+            pltpu.SemaphoreType.DMA((count,)),
+            pltpu.SemaphoreType.DMA((count,)),
         ],
         compiler_params=pltpu.CompilerParams(collective_id=0, has_side_effects=True),
-    )(flat, decay_rates[:, :, None])
-    return out.reshape(forcing.shape)
+    )(ext)
+    return jnp.transpose(out, (1, 2, 0, 3, 4)).reshape(layers, moments, columns, width)
 
 
 def plane_sum(x, axis):
@@ -192,10 +295,11 @@
     node_weights,
 ):
     layers, columns, rows, depth = probes.shape
-    padded = with_halo(probes, (("layer", 0), ("xs", 2)), 2)
+    stacked = with_halo(probes, (("layer", 0),), 2)
+    beside = with_halo(probes, (("xs", 2),), 2)
     across = jnp.pad(probes, ((0, 0), (0, 0), (0, 0), (2, 2)))
-    laplace = second_along(padded[:, :, 2:-2, :], 0, layers)
-    laplace = laplace + second_along(padded[2:-2], 2, rows)
+    laplace = second_along(stacked, 0, layers)
+    laplace = laplace + second_along(beside, 2, rows)
     laplace = laplace + second_along(across, 3, depth)
     rounded = probes.astype(jnp.bfloat16).reshape(layers, columns, rows * depth)
     slot_coef = jnp.einsum("lsp,lcp->lsc", projector, rounded, preferred_element_type=jnp.float32)
@@ -215,8 +319,9 @@
     w0 = jnp.sum(node_weights)
     w1 = jnp.sum(node_weights * contour_nodes)
     w2 = jnp.sum(node_weights * contour_nodes * contour_nodes)
-    forcing = jnp.stack([w0 * hamil - w1 * probes, w1 * hamil - w2 * probes])
-    return sweeps(forcing, decay_rates)
+    forcing = jnp.stack([w0 * hamil - w1 * probes, w1 * hamil - w2 * probes], axis=1)
+    swept = sweeps(forcing.reshape(layers, 2, columns, rows * depth), decay_rates)
+    return jnp.swapaxes(swept, 0, 1).reshape(2, layers, columns, rows, depth)
 
 
 def solution(mesh):

time: 226 us -> 84.2 us (0.37)
  the two profiles are of different devices: /device:TPU:22 before, /device:TPU:32 now
where the time goes in v5:
time: 84.2 us; the launch traced here: 83.6 us
  Pallas kernels  50.6 us (60%)
  starting transfers between devices  15.9 us (19%)
  other arithmetic  6.7 us (8%)
  local copies, waits for them, and re-layouts  6.48 us (8%)
  waiting for transfers between devices  2.82 us (3%)
    pallas_call x1, Pallas kernels, sweeps(): pl.pallas_call(functools.partial(exchange_kernel, count), out_shape=jax.S...  50.6 us
    ppermute x3, starting transfers between devices, plane_sum(): x = x + lax.ppermute(x, axis, [(i, i ^ step) for i in range(count)])  6.96 us
    ppermute x2, starting transfers between devices, with_halo(): lax.ppermute(tail, axis, [(i, (i + 1) % count) for i in range(ends)])  5.06 us
    ppermute x2, starting transfers between devices, with_halo(): lax.ppermute(head, axis, [((i + 1) % count, i) for i in range(ends)])  3.87 us
    sub x1, other arithmetic, shards(): w0 * hamil - w1 * probes  3.46 us
    ppermute x3, waiting for transfers between devices, plane_sum(): x = x + lax.ppermute(x, axis, [(i, i ^ step) for i in range(count)])  2.81 us
    reshape x2, local copies, waits for them, and re-layouts, sweeps(): jnp.transpose(out, (1, 2, 0, 3, 4)).reshape(layers, moments, columns, width)  1.71 us
  transfers between devices with their start and end apart: 7, of which 2 were waited for; matrix products, arithmetic and copies ran while one was open for 1% of the time, Pallas kernels for 0%

profile of v5, /device:TPU:32, one launch (start us, length us, event | category | flops | bytes accessed | tf_op | source)
XLA Modules:
  0.0 83.6 jit_solution(16513910344600528364)
XLA Ops:
  0.0 0.0 copy-start
  0.0 1.1 %convert_element_type.19 = bf16[2,32,2,640]{3,2,1,0:T(2,128)(2,1)S(1)} convert(f32[2,32,2,640]{3,2,1,0:T(2,128)} %param.8) | non-fusion elementwise | flops 81920 | bytes 491520 | tf_op jit(solution)/shard_map/convert_element_type | solution.py:304
  1.1 0.1 reshape.24
  1.3 0.0 copy-done
  1.3 0.0 copy-start.3
  1.3 0.0 copy-start.1
  1.3 0.2 fusion.23
  1.5 0.5 copy-done.3
  1.9 0.2 fusion.16
  2.2 0.1 collective-permute-start.4
  2.3 1.2 %collective-permute-done.4 = f32[2,256,32]{1,2,0:T(8,128)S(1)} collective-permute-done((f32[2,256,32]{1,2,0:T(8,128)S(1)}, f32[2,256,32]{1,2,0:T(8,128)S(1)}, u32[]{:S(2)}, u32[]{:S(2)}) %collective-permute-start.4) | collective-permute-done | bytes 65568 | tf_op jit(solution)/shard_map/ppermute | solution.py:282
  3.5 0.0 copy-start.6
  3.6 0.0 copy-start.7
  3.6 1.6 %collective-permute-start.5 = (f32[2,256,32]{1,2,0:T(8,128)S(1)}, f32[2,256,32]{1,2,0:T(8,128)S(1)}, u32[]{:S(2)}, u32[]{:S(2)}) collective-permute-start(f32[2,256,32]{1,2,0:T(8,128)S(1)} %add.74), channel_id=1, source_target_pairs={{0,2},{1,3},{2,0},{3,1},{4,6},{5,7},{6,4},{7,5},{8,10},{9,11},{10,... | collective-permute-start | bytes 196616 | tf_op jit(solution)/shard_map/ppermute | solution.py:282
  5.1 0.0 copy-done.1
  5.2 1.8 %collective-permute-start.2 = (f32[2,32,2,640]{3,2,1,0:T(2,128)S(1)}, f32[2,32,2,640]{3,2,1,0:T(2,128)S(1)}, u32[]{:S(2)}, u32[]{:S(2)}) collective-permute-start(f32[2,32,2,640]{3,2,1,0:T(2,128)S(1)} %copy-done.1), channel_id=1, source_target_pairs={{0,1},{1,2},{2,3},{3,4},{4,5},{5,6},{6,7},{8,9},{9,10},{10,11},{11... | collective-permute-start | bytes 983048 | tf_op jit(solution)/shard_map/ppermute | solution.py:26
  6.9 1.3 %collective-permute-start.3 = (f32[2,32,2,640]{3,2,1,0:T(2,128)S(1)}, f32[2,32,2,640]{3,2,1,0:T(2,128)S(1)}, u32[]{:S(2)}, u32[]{:S(2)}) collective-permute-start(f32[2,32,2,640]{3,2,1,0:T(2,128)S(1)} %copy-done.1), channel_id=1, source_target_pairs={{1,0},{2,1},{3,2},{4,3},{5,4},{6,5},{7,6},{9,8},{10,9},{11,10},{12... | collective-permute-start | bytes 983048 | tf_op jit(solution)/shard_map/ppermute | solution.py:28
  8.2 2.6 %collective-permute-start.1 = (f32[2,32,2,640]{3,2,1,0:T(2,128)S(1)}, f32[2,32,2,640]{3,2,1,0:T(2,128)S(1)}, u32[]{:S(2)}, u32[]{:S(2)}) collective-permute-start(f32[2,32,2,640]{3,2,1,0:T(2,128)S(1)} %copy-done.1), channel_id=1, source_target_pairs={{8,0},{16,8},{24,16},{32,24},{40,32},{48,40},{56,48},{64,56},{72,6... | collective-permute-start | bytes 983048 | tf_op jit(solution)/shard_map/ppermute | solution.py:28
  10.8 3.3 %collective-permute-start = (f32[2,32,2,640]{3,2,1,0:T(2,128)S(1)}, f32[2,32,2,640]{3,2,1,0:T(2,128)S(1)}, u32[]{:S(2)}, u32[]{:S(2)}) collective-permute-start(f32[2,32,2,640]{3,2,1,0:T(2,128)S(1)} %copy-done.1), channel_id=1, source_target_pairs={{0,8},{8,16},{16,24},{24,32},{32,40},{40,48},{48,56},{56,64},{64,7... | collective-permute-start | bytes 983048 | tf_op jit(solution)/shard_map/ppermute | solution.py:26
  14.1 0.0 collective-permute-done.5
  14.1 0.0 copy-start.4
  14.1 5.3 %collective-permute-start.6 = (f32[2,256,32]{1,2,0:T(8,128)S(1)}, f32[2,256,32]{1,2,0:T(8,128)S(1)}, u32[]{:S(2)}, u32[]{:S(2)}) collective-permute-start(f32[2,256,32]{1,2,0:T(8,128)S(1)} %add.75), channel_id=1, source_target_pairs={{0,4},{1,5},{2,6},{3,7},{4,0},{5,1},{6,2},{7,3},{8,12},{9,13},{10,... | collective-permute-start | bytes 196616 | tf_op jit(solution)/shard_map/ppermute | solution.py:282
  19.4 0.0 copy-done.6
  19.4 0.0 copy-done.7
  19.4 0.7 multiply_reduce_fusion.1
  20.1 1.6 %collective-permute-done.6 = f32[2,256,32]{1,2,0:T(8,128)S(1)} collective-permute-done((f32[2,256,32]{1,2,0:T(8,128)S(1)}, f32[2,256,32]{1,2,0:T(8,128)S(1)}, u32[]{:S(2)}, u32[]{:S(2)}) %collective-permute-start.6) | collective-permute-done | bytes 65568 | tf_op jit(solution)/shard_map/ppermute | solution.py:282
  21.7 0.0 copy-done.4
  21.7 0.4 fusion
  22.1 0.0 copy-start.2
  22.1 0.2 reshape.25
  22.2 0.0 collective-permute-done.2
  22.3 0.0 collective-permute-done.3
  22.3 0.0 collective-permute-done.1
  22.3 0.0 collective-permute-done
  22.3 0.5 copy-done.2
  22.8 3.5 %multiply_subtract_fusion.1 = (f32[2,32,2,640]{3,2,1,0:T(2,128)S(1)}, f32[2,32,2,640]{3,2,1,0:T(2,128)S(1)}) fusion(f32[2,32,2,640]{3,2,1,0:T(2,128)S(1)} %copy-done.1, f32[]{:T(128)} %get-tuple-element.5, f32[]{:T(128)} %get-tuple-element.7, f32[2,32,2,640]{3,2,1,0:T(2,128)S(1)} %reshape.25, f32[2,2,640]{2,1,0:T(2,128)S(1)} %copy-done.2, ...), kind=kLoop, calls=%fused_computation.24 | loop fusion | flops 2621440 | bytes 2631688 | tf_op jit(solution)/shard_map/sub | solution.py:322
  26.2 0.3 stack.9
  26.5 1.4 %multiply_subtract_fusion = f32[2,8,8,640]{3,2,1,0:T(8,128)S(1)} fusion(f32[2,8,8,640]{3,2,1,0:T(8,128)S(1)} %bitcast.26, f32[2,8,8,640]{3,2,1,0:T(8,128)S(1)} %bitcast.31, f32[]{:T(128)} %get-tuple-element.6, f32[]{:T(128)} %get-tuple-element.5), kind=kLoop, calls=%fused_computation.23 | loop fusion | flops 245760 | bytes 983048 | tf_op jit(solution)/shard_map/sub | solution.py:322
  27.9 0.0 copy-start.5
  27.9 0.3 stack.10
  28.2 0.4 copy-done.5
  28.6 0.1 broadcast_in_dim.2
  28.6 0.1 pad_maximum_fusion
  28.7 0.1 reshape.26
  28.8 1.1 %copy.21 = f32[2,2,32,11,128]{4,3,1,0,2:T(8,128)} copy(f32[2,2,32,11,128]{4,3,2,1,0:T(8,128)S(1)} %reshape.26) | data formatting | bytes 1441792 | tf_op jit(solution)/shard_map/reshape | solution.py:258
  29.9 50.6 %shard_map.82 = f32[32,2,2,10,128]{4,3,2,1,0:T(8,128)} custom-call(f32[32,2,2,11,128]{4,3,2,1,0:T(8,128)} %bitcast.24), custom_call_target="tpu_custom_call" | custom-call | tf_op jit(solution)/shard_map/pallas_call | solution.py:260
  80.6 1.6 %reshape.29 = f32[2,2,32,1280]{3,1,0,2:T(2,128)S(1)} reshape(f32[2,2,32,10,128]{4,3,1,0,2:T(8,128)} %bitcast.25) | data formatting | bytes 1310720 | tf_op jit(solution)/shard_map/reshape | solution.py:275
  82.2 0.1 copy.22
  82.3 0.4 reshape.28
  82.6 0.9 %copy.17 = f32[2,2,32,2,640]{4,3,2,1,0:T(2,128)} copy(f32[2,2,32,2,640]{4,3,2,0,1:T(2,128)S(1)} %reshape.28) | data formatting | bytes 1310720 | tf_op jit(solution)/shard_map/reshape | solution.py:324
  (2 shorter events, 0.0 us)
Async XLA Ops:
  0.0 1.3 %copy-start = (bf16[2,64,1280]{2,1,0:T(8,128)(2,1)S(1)}, bf16[2,64,1280]{2,1,0:T(8,128)(2,1)}, u32[]{:S(2)}) copy-start(bf16[2,64,1280]{2,1,0:T(8,128)(2,1)} %param.10) | copy-start | bytes 983044
  1.3 0.7 copy-start.3
  1.3 3.9 %copy-start.1 = (f32[2,32,2,640]{3,2,1,0:T(2,128)S(1)}, f32[2,32,2,640]{3,2,1,0:T(2,128)}, u32[]{:S(2)}) copy-start(f32[2,32,2,640]{3,2,1,0:T(2,128)} %param.8) | copy-start | bytes 983044
  2.2 1.3 %collective-permute-start.4 = (f32[2,256,32]{1,2,0:T(8,128)S(1)}, f32[2,256,32]{1,2,0:T(8,128)S(1)}, u32[]{:S(2)}, u32[]{:S(2)}) collective-permute-start(f32[2,256,32]{1,2,0:T(8,128)S(1)} %fusion.16), channel_id=1, source_target_pairs={{0,1},{1,0},{2,3},{3,2},{4,5},{5,4},{6,7},{7,6},{8,9},{9,8},{10,11... | collective-permute-start | bytes 196616 | tf_op jit(solution)/shard_map/ppermute | solution.py:282
  3.5 15.9 %copy-start.6 = (f32[4]{0:T(128)S(1)}, f32[4]{0:T(128)}, u32[]{:S(2)}) copy-start(f32[4]{0:T(128)} %param.15) | copy-start | bytes 52
  3.6 15.9 %copy-start.7 = (f32[4]{0:T(128)S(1)}, f32[4]{0:T(128)}, u32[]{:S(2)}) copy-start(f32[4]{0:T(128)} %param.14) | copy-start | bytes 52
  3.6 10.5 %collective-permute-start.5 = (f32[2,256,32]{1,2,0:T(8,128)S(1)}, f32[2,256,32]{1,2,0:T(8,128)S(1)}, u32[]{:S(2)}, u32[]{:S(2)}) collective-permute-start(f32[2,256,32]{1,2,0:T(8,128)S(1)} %add.74), channel_id=1, source_target_pairs={{0,2},{1,3},{2,0},{3,1},{4,6},{5,7},{6,4},{7,5},{8,10},{9,11},{10,... | collective-permute-start | bytes 196616 | tf_op jit(solution)/shard_map/ppermute | solution.py:282
  5.2 17.1 %collective-permute-start.2 = (f32[2,32,2,640]{3,2,1,0:T(2,128)S(1)}, f32[2,32,2,640]{3,2,1,0:T(2,128)S(1)}, u32[]{:S(2)}, u32[]{:S(2)}) collective-permute-start(f32[2,32,2,640]{3,2,1,0:T(2,128)S(1)} %copy-done.1), channel_id=1, source_target_pairs={{0,1},{1,2},{2,3},{3,4},{4,5},{5,6},{6,7},{8,9},{9,10},{10,11},{11... | collective-permute-start | bytes 983048 | tf_op jit(solution)/shard_map/ppermute | solution.py:26
  6.9 15.3 %collective-permute-start.3 = (f32[2,32,2,640]{3,2,1,0:T(2,128)S(1)}, f32[2,32,2,640]{3,2,1,0:T(2,128)S(1)}, u32[]{:S(2)}, u32[]{:S(2)}) collective-permute-start(f32[2,32,2,640]{3,2,1,0:T(2,128)S(1)} %copy-done.1), channel_id=1, source_target_pairs={{1,0},{2,1},{3,2},{4,3},{5,4},{6,5},{7,6},{9,8},{10,9},{11,10},{12... | collective-permute-start | bytes 983048 | tf_op jit(solution)/shard_map/ppermute | solution.py:28
  8.2 14.0 %collective-permute-start.1 = (f32[2,32,2,640]{3,2,1,0:T(2,128)S(1)}, f32[2,32,2,640]{3,2,1,0:T(2,128)S(1)}, u32[]{:S(2)}, u32[]{:S(2)}) collective-permute-start(f32[2,32,2,640]{3,2,1,0:T(2,128)S(1)} %copy-done.1), channel_id=1, source_target_pairs={{8,0},{16,8},{24,16},{32,24},{40,32},{48,40},{56,48},{64,56},{72,6... | collective-permute-start | bytes 983048 | tf_op jit(solution)/shard_map/ppermute | solution.py:28
  10.8 11.4 %collective-permute-start = (f32[2,32,2,640]{3,2,1,0:T(2,128)S(1)}, f32[2,32,2,640]{3,2,1,0:T(2,128)S(1)}, u32[]{:S(2)}, u32[]{:S(2)}) collective-permute-start(f32[2,32,2,640]{3,2,1,0:T(2,128)S(1)} %copy-done.1), channel_id=1, source_target_pairs={{0,8},{8,16},{16,24},{24,32},{32,40},{40,48},{48,56},{56,64},{64,7... | collective-permute-start | bytes 983048 | tf_op jit(solution)/shard_map/ppermute | solution.py:26
  14.1 7.5 %copy-start.4 = (f32[2,256]{1,0:T(2,128)S(1)}, f32[2,256]{1,0:T(2,128)}, u32[]{:S(2)}) copy-start(f32[2,256]{1,0:T(2,128)} %param.12) | copy-start | bytes 6148
  14.1 7.5 %collective-permute-start.6 = (f32[2,256,32]{1,2,0:T(8,128)S(1)}, f32[2,256,32]{1,2,0:T(8,128)S(1)}, u32[]{:S(2)}, u32[]{:S(2)}) collective-permute-start(f32[2,256,32]{1,2,0:T(8,128)S(1)} %add.75), channel_id=1, source_target_pairs={{0,4},{1,5},{2,6},{3,7},{4,0},{5,1},{6,2},{7,3},{8,12},{9,13},{10,... | collective-permute-start | bytes 196616 | tf_op jit(solution)/shard_map/ppermute | solution.py:282
  22.1 0.7 copy-start.2
  27.9 0.7 copy-start.5

commit v6 on v5

--- a/solution.py
+++ b/solution.py
@@ -275,13 +275,73 @@
     return jnp.transpose(out, (1, 2, 0, 3, 4)).reshape(layers, moments, columns, width)
 
 
-def plane_sum(x, axis):
-    count = lax.axis_size(axis)
-    step = 1
-    while step < count:
-        x = x + lax.ppermute(x, axis, [(i, i ^ step) for i in range(count)])
-        step *= 2
-    return x
+def front_kernel(layer_count, row_count, block_ref, coef_ref, below, above, left, right, total,
+                 gathered, send_sem, recv_sem):
+    me = lax.axis_index("layer")
+    row = lax.axis_index("xs")
+    peers = row_count - 1
+    barrier = pltpu.get_barrier_semaphore()
+    for sign in (1, -1):
+        pl.semaphore_signal(
+            barrier, inc=1, device_id=(lax.rem(me + sign + layer_count, layer_count), row),
+            device_id_type=MESH,
+        )
+    for step in range(1, row_count):
+        pl.semaphore_signal(
+            barrier, inc=1, device_id=(me, lax.rem(row + step, row_count)), device_id_type=MESH
+        )
+    pl.semaphore_wait(barrier, 2 + peers)
+    copies = []
+    targets = [
+        (below, (lax.rem(me + 1, layer_count), row)),
+        (above, (lax.rem(me + layer_count - 1, layer_count), row)),
+        (left, (me, lax.rem(row + 1, row_count))),
+        (right, (me, lax.rem(row + row_count - 1, row_count))),
+    ]
+    for slot, (dst, device) in enumerate(targets):
+        copies.append(
+            pltpu.make_async_remote_copy(
+                src_ref=block_ref, dst_ref=dst, send_sem=send_sem.at[slot], recv_sem=recv_sem.at[slot],
+                device_id=device, device_id_type=MESH,
+            )
+        )
+    for step in range(1, row_count):
+        copies.append(
+            pltpu.make_async_remote_copy(
+                src_ref=coef_ref, dst_ref=gathered.at[step - 1], send_sem=send_sem.at[3 + step],
+                recv_sem=recv_sem.at[3 + step], device_id=(me, lax.rem(row + step, row_count)),
+                device_id_type=MESH,
+            )
+        )
+    for copy in copies:
+        copy.start()
+    for copy in copies[4:]:
+        copy.wait()
+    acc = coef_ref[...]
+    for step in range(peers):
+        acc = acc + gathered[step]
+    total[...] = acc
+    for copy in copies[:4]:
+        copy.wait()
+
+
+def front_exchange(block, coef):
+    layer_count = lax.axis_size("layer")
+    row_count = lax.axis_size("xs")
+    spec = pl.BlockSpec(memory_space=pltpu.VMEM)
+    return pl.pallas_call(
+        functools.partial(front_kernel, layer_count, row_count),
+        out_shape=[jax.ShapeDtypeStruct(block.shape, jnp.float32)] * 4
+        + [jax.ShapeDtypeStruct(coef.shape, jnp.float32)],
+        in_specs=[spec, spec],
+        out_specs=[spec] * 5,
+        scratch_shapes=[
+            pltpu.VMEM((row_count - 1,) + coef.shape, jnp.float32),
+            pltpu.SemaphoreType.DMA((3 + row_count,)),
+            pltpu.SemaphoreType.DMA((3 + row_count,)),
+        ],
+        compiler_params=pltpu.CompilerParams(collective_id=1, has_side_effects=True),
+    )(block, coef)
 
 
 def shards(
@@ -295,19 +355,28 @@
     node_weights,
 ):
     layers, columns, rows, depth = probes.shape
-    stacked = with_halo(probes, (("layer", 0),), 2)
-    beside = with_halo(probes, (("xs", 2),), 2)
-    across = jnp.pad(probes, ((0, 0), (0, 0), (0, 0), (2, 2)))
-    laplace = second_along(stacked, 0, layers)
-    laplace = laplace + second_along(beside, 2, rows)
-    laplace = laplace + second_along(across, 3, depth)
     rounded = probes.astype(jnp.bfloat16).reshape(layers, columns, rows * depth)
     slot_coef = jnp.einsum("lsp,lcp->lsc", projector, rounded, preferred_element_type=jnp.float32)
     onehot = (intersection_ids[:, :, None] == jnp.arange(NPROJ, dtype=jnp.int32)).astype(
         jnp.float32
     )
-    partial_coef = jnp.einsum("lsq,lsc->lqc", onehot, slot_coef, precision=lax.Precision.HIGHEST)
-    coef = plane_sum(partial_coef, "xs")
+    partial_coef = jnp.einsum("lsq,lsc->lcq", onehot, slot_coef, precision=lax.Precision.HIGHEST)
+    below, above, left, right, coef = front_exchange(
+        probes.reshape(layers, columns, rows * depth), partial_coef
+    )
+    me = lax.axis_index("layer")
+    row = lax.axis_index("xs")
+    below = jnp.where(me > 0, below, 0.0).reshape(probes.shape)
+    above = jnp.where(me < lax.axis_size("layer") - 1, above, 0.0).reshape(probes.shape)
+    left = jnp.where(row > 0, left, 0.0).reshape(probes.shape)
+    right = jnp.where(row < lax.axis_size("xs") - 1, right, 0.0).reshape(probes.shape)
+    stacked = jnp.concatenate([below, probes, above], axis=0)
+    beside = jnp.concatenate([left, probes, right], axis=2)
+    across = jnp.pad(probes, ((0, 0), (0, 0), (0, 0), (2, 2)))
+    laplace = second_along(stacked, 0, layers)
+    laplace = laplace + second_along(beside, 2, rows)
+    laplace = laplace + second_along(across, 3, depth)
+    coef = jnp.swapaxes(coef, 1, 2)
     scaled = (strength[:, :, None] * coef).astype(jnp.bfloat16)
     slot_back = jnp.einsum(
         "lsq,lqc->lsc", onehot.astype(jnp.bfloat16), scaled, preferred_element_type=jnp.float32

time: 84.2 us -> 84.8 us (level)
  starting transfers between devices: 15.9 us -> 0 us
  Pallas kernels: 50.6 us -> 64.2 us
  local copies, waits for them, and re-layouts: 6.48 us -> 9.93 us
  waiting for transfers between devices: 2.82 us -> 0 us
  other arithmetic: 6.7 us -> 7.81 us
    pallas_call x0 -> x1, Pallas kernels: none -> 18.1 us  [front_exchange(): pl.pallas_call(functools.partial(front_kernel, layer_count, row_count), o...]
    ppermute x7 -> x0, starting transfers between devices: 15.9 us -> none  [the longest x3 6.96 us: plane_sum(): x = x + lax.ppermute(x, axis, [(i, i ^ step) for i in range(count)])]
    pallas_call x1, Pallas kernels: 50.6 us -> 46.1 us  [sweeps(): pl.pallas_call(functools.partial(exchange_kernel, count), out_shape=jax.S...]
    ppermute x7 -> x0, waiting for transfers between devices: 2.82 us -> none  [the longest x3 2.81 us: plane_sum(): x = x + lax.ppermute(x, axis, [(i, i ^ step) for i in range(count)])]
    unnamed x16 -> x22, local copies, waits for them, and re-layouts: 1.37 us -> 3.14 us
    reshape x0 -> x5, local copies, waits for them, and re-layouts: none -> 1.68 us  [the longest x1 0.99 us: shards(): probes.reshape(layers, columns, rows * depth)]
    select_n x0 -> x2, other arithmetic: none -> 1.17 us  [the longest x1 1.13 us: shards(): jnp.where(me < lax.axis_size('layer') - 1, above, 0.0).reshape(probes.shape)]
  transfers between devices with their start and end apart: 7 -> 0, of which waited for: 2 -> 0; matrix products, arithmetic and copies ran while one was open for 1% -> 0% of each run, Pallas kernels for 0% -> 0%
where the time goes in v6:
time: 84.8 us; the launch traced here: 83.6 us
  Pallas kernels  64.2 us (76%)
  local copies, waits for them, and re-layouts  9.93 us (12%)
  other arithmetic  7.81 us (9%)
  matrix products  1.43 us (2%)
    pallas_call x1, Pallas kernels, sweeps(): pl.pallas_call(functools.partial(exchange_kernel, count), out_shape=jax.S...  46.1 us
    pallas_call x1, Pallas kernels, front_exchange(): pl.pallas_call(functools.partial(front_kernel, layer_count, row_count), o...  18.1 us
    sub x1, other arithmetic, shards(): w0 * hamil - w1 * probes  3.52 us
    unnamed x22, local copies, waits for them, and re-layouts  3.14 us
    reshape x2, local copies, waits for them, and re-layouts, sweeps(): jnp.transpose(out, (1, 2, 0, 3, 4)).reshape(layers, moments, columns, width)  1.71 us

profile of v6, /device:TPU:32, one launch (start us, length us, event | category | flops | bytes accessed | tf_op | source)
XLA Modules:
  0.0 83.6 jit_solution(15600919005218652741)
XLA Ops:
  0.0 0.0 copy-start
  0.0 1.1 %convert_element_type.18 = bf16[2,32,2,640]{3,2,1,0:T(2,128)(2,1)S(1)} convert(f32[2,32,2,640]{3,2,1,0:T(2,128)} %param.8) | non-fusion elementwise | flops 81920 | bytes 491520 | tf_op jit(solution)/shard_map/convert_element_type | solution.py:358
  1.1 0.1 reshape.40
  1.3 0.0 copy-done
  1.3 0.0 copy-start.6
  1.3 0.0 copy-start.1
  1.3 0.2 fusion.23
  1.5 0.5 copy-done.6
  1.9 0.9 %fusion.16.coef_ref = f32[2,32,256]{2,1,0:T(8,128)} fusion(f32[2,64,32]{1,2,0:T(8,128)S(1)} %fusion.23, s32[2,64]{1,0:T(2,128)S(1)} %copy-done.6), kind=kOutput, calls=%fused_computation.35 | convolution fusion | flops 12615680 | bytes 82432 | tf_op jit(solution)/shard_map/lsq,lsc->lcq/dot_general | solution.py:363
  2.8 0.0 copy-done.1
  2.8 1.0 %reshape.39.block_ref = f32[2,32,1280]{2,1,0:T(8,128)} reshape(f32[2,32,2,640]{3,2,1,0:T(2,128)S(1)} %copy-done.1) | data formatting | bytes 655360 | tf_op jit(solution)/shard_map/reshape | solution.py:365
  3.8 18.1 %shard_map.82 = (f32[2,32,1280]{2,1,0:T(8,128)}, f32[2,32,1280]{2,1,0:T(8,128)}, f32[2,32,1280]{2,1,0:T(8,128)}, f32[2,32,1280]{2,1,0:T(8,128)}, f32[2,32,256]{2,1,0:T(8,128)}) custom-call(f32[2,32,1280]{2,1,0:T(8,128)} %reshape.39.block_ref, f32[2,32,256]{2,1,0:T(8,128)} %fusion.16.coef_ref), custom_call_target="tpu_custom_call" | custom-call | tf_op jit(solution)/shard_map/pallas_call | solution.py:332
  21.9 1.1 %broadcast_select_fusion.2 = (f32[2,32,1280]{2,1,0:T(8,128)S(1)}, f32[2,32,1280]{2,1,0:T(8,128)S(1)}) fusion(f32[2,32,1280]{2,1,0:T(8,128)} %get-tuple-element.11, pred[]{:T(512)S(6)} %lt.6, f32[2,32,1280]{2,1,0:T(8,128)} %get-tuple-element.10, pred[]{:T(512)S(6)} %gt.6), kind=kLoop, calls=%fused_computation.31 | loop fusion | flops 163840 | bytes 1310722 | tf_op jit(solution)/shard_map/jit(_where)/select_n | solution.py:370
  23.0 0.2 reshape.41
  23.2 0.0 copy-start.2
  23.2 0.0 copy-start.3
  23.2 0.2 reshape.42
  23.4 0.8 copy-done.2
  24.2 0.1 copy-done.3
  24.3 0.2 reshape.43
  24.5 0.0 copy-start.4
  24.5 0.0 copy-start.7
  24.5 0.2 reshape.44
  24.7 0.6 copy-done.4
  25.4 0.0 copy-done.7
  25.4 0.4 fusion
  25.7 0.0 copy-start.9
  25.7 0.0 copy-start.10
  25.8 0.0 copy-start.5
  25.8 0.2 reshape.45
  26.0 0.4 copy-done.9
  26.4 0.0 copy-done.10
  26.4 0.7 multiply_reduce_fusion.1
  27.1 0.0 copy-done.5
  27.1 3.5 %multiply_subtract_fusion.1 = (f32[2,32,2,640]{3,2,1,0:T(2,128)S(1)}, f32[2,32,2,640]{3,2,1,0:T(2,128)S(1)}) fusion(f32[2,32,2,640]{3,2,1,0:T(2,128)S(1)} %copy-done.1, f32[]{:T(128)} %get-tuple-element.15, f32[]{:T(128)} %get-tuple-element.17, f32[2,32,2,640]{3,2,1,0:T(2,128)S(1)} %reshape.45, f32[2,2,640]{2,1,0:T(2,128)S(1)} %copy-done.5, ...), kind=kLoop, calls=%fused_computation.24 | loop fusion | flops 2621440 | bytes 2631688 | tf_op jit(solution)/shard_map/sub | solution.py:391
  30.6 1.3 %multiply_subtract_fusion = f32[2,8,8,640]{3,2,1,0:T(8,128)S(1)} fusion(f32[2,8,8,640]{3,2,1,0:T(8,128)S(1)} %bitcast.24, f32[2,8,8,640]{3,2,1,0:T(8,128)S(1)} %bitcast.31, f32[]{:T(128)} %get-tuple-element.16, f32[]{:T(128)} %get-tuple-element.15), kind=kLoop, calls=%fused_computation.23 | loop fusion | flops 245760 | bytes 983048 | tf_op jit(solution)/shard_map/sub | solution.py:391
  31.9 0.3 stack.10
  32.2 0.3 stack.9
  32.4 0.0 copy-start.8
  32.4 0.7 copy-done.8
  33.1 0.1 broadcast_in_dim.18
  33.2 0.1 pad_maximum_fusion
  33.2 0.1 reshape.46
  33.4 1.1 %copy.21 = f32[2,2,32,11,128]{4,3,1,0,2:T(8,128)} copy(f32[2,2,32,11,128]{4,3,2,1,0:T(8,128)S(1)} %reshape.46) | data formatting | bytes 1441792 | tf_op jit(solution)/shard_map/reshape | solution.py:258
  34.5 46.1 %shard_map.83 = f32[32,2,2,10,128]{4,3,2,1,0:T(8,128)} custom-call(f32[32,2,2,11,128]{4,3,2,1,0:T(8,128)} %bitcast.25), custom_call_target="tpu_custom_call" | custom-call | tf_op jit(solution)/shard_map/pallas_call | solution.py:260
  80.6 1.6 %reshape.49 = f32[2,2,32,1280]{3,1,0,2:T(2,128)S(1)} reshape(f32[2,2,32,10,128]{4,3,1,0,2:T(8,128)} %bitcast.26) | data formatting | bytes 1310720 | tf_op jit(solution)/shard_map/reshape | solution.py:275
  82.2 0.1 copy.22
  82.4 0.4 reshape.48
  82.7 0.9 %copy.17 = f32[2,2,32,2,640]{4,3,2,1,0:T(2,128)} copy(f32[2,2,32,2,640]{4,3,2,0,1:T(2,128)S(1)} %reshape.48) | data formatting | bytes 1310720 | tf_op jit(solution)/shard_map/reshape | solution.py:393
  (1 shorter events, 0.0 us)
Async XLA Ops:
  0.0 1.3 %copy-start = (bf16[2,64,1280]{2,1,0:T(8,128)(2,1)S(1)}, bf16[2,64,1280]{2,1,0:T(8,128)(2,1)}, u32[]{:S(2)}) copy-start(bf16[2,64,1280]{2,1,0:T(8,128)(2,1)} %param.10) | copy-start | bytes 983044
  1.3 0.7 copy-start.6
  1.3 1.5 %copy-start.1 = (f32[2,32,2,640]{3,2,1,0:T(2,128)S(1)}, f32[2,32,2,640]{3,2,1,0:T(2,128)}, u32[]{:S(2)}) copy-start(f32[2,32,2,640]{3,2,1,0:T(2,128)} %param.8) | copy-start | bytes 983044
  23.2 1.0 %copy-start.2 = (f32[2,32,1280]{2,1,0:T(8,128)S(1)}, f32[2,32,1280]{2,1,0:T(8,128)}, u32[]{:S(2)}) copy-start(f32[2,32,1280]{2,1,0:T(8,128)} %get-tuple-element.12) | copy-start | bytes 983044
  23.2 1.1 %copy-start.3 = (f32[2,32,1280]{2,1,0:T(8,128)S(1)}, f32[2,32,1280]{2,1,0:T(8,128)}, u32[]{:S(2)}) copy-start(f32[2,32,1280]{2,1,0:T(8,128)} %get-tuple-element.13) | copy-start | bytes 983044
  24.5 0.8 %copy-start.4 = (f32[2,32,256]{2,1,0:T(8,128)S(1)}, f32[2,32,256]{2,1,0:T(8,128)}, u32[]{:S(2)}) copy-start(f32[2,32,256]{2,1,0:T(8,128)} %get-tuple-element.14) | copy-start | bytes 196612
  24.5 0.8 copy-start.7
  25.7 0.7 copy-start.9
  25.7 0.7 copy-start.10
  25.8 1.3 %copy-start.5 = (f32[2,2,640]{2,1,0:T(2,128)S(1)}, f32[2,2,640]{2,1,0:T(2,128)}, u32[]{:S(2)}) copy-start(f32[2,2,640]{2,1,0:T(2,128)} %param.9) | copy-start | bytes 30724
  32.4 0.7 copy-start.8

commit v7 on v6

--- a/solution.py
+++ b/solution.py
@@ -149,11 +149,10 @@
         o_ref[:, index] = back[index] + upper[None] * from_above
 
 
-def exchange_kernel(count, ext_ref, out_ref, gathered, swept, send_sem, recv_sem, back_send, back_recv):
+def exchange_kernel(count, layer_count, ext_ref, out_ref, gathered, swept, send_sem, recv_sem, back_send, back_recv):
     me = lax.axis_index("layer")
     row = lax.axis_index("xs")
-    layers = ext_ref.shape[1]
-    tiles = out_ref.shape[3]
+    layers = layer_count
     barrier = pltpu.get_barrier_semaphore()
 
     def greet(step, carry):
@@ -195,14 +194,16 @@
 
     lax.fori_loop(1, count, arrived, 0)
 
-    zero = jnp.zeros(out_ref.shape[2:], jnp.float32)
+    rows_per_layer = out_ref.shape[1] // layers
+    zero = jnp.zeros((rows_per_layer, out_ref.shape[2]), jnp.float32)
+    data_rows = out_ref.shape[1]
 
     def forward(source, state):
         for layer in range(layers):
-            slab = gathered[source, layer]
-            rate = slab[0, tiles]
-            state = rate * state + (1.0 - rate) * slab[:, :tiles]
-            swept[source, layer] = state
+            rate = gathered[source, pl.ds(data_rows + layer, 1), :]
+            slab = gathered[source, pl.ds(layer * rows_per_layer, rows_per_layer), :]
+            state = rate * state + (1.0 - rate) * slab
+            swept[source, pl.ds(layer * rows_per_layer, rows_per_layer), :] = state
         return state
 
     lax.fori_loop(0, count, forward, zero)
@@ -210,9 +211,10 @@
     def backward(step, state):
         source = count - 1 - step
         for layer in reversed(range(layers)):
-            rate = gathered[source, layer, 0, tiles]
-            state = rate * state + (1.0 - rate) * swept[source, layer]
-            swept[source, layer] = state
+            rate = gathered[source, pl.ds(data_rows + layer, 1), :]
+            piece = pl.ds(layer * rows_per_layer, rows_per_layer)
+            state = rate * state + (1.0 - rate) * swept[source, piece, :]
+            swept[source, piece, :] = state
         return state
 
     lax.fori_loop(0, count, backward, zero)
@@ -254,17 +256,20 @@
     if columns != count:
         raise ValueError("columns")
     tiles = width // 128
-    lanes = jnp.broadcast_to(decay_rates[:, None, :, None], (layers, moments, columns, 128))
-    ext = jnp.concatenate([forcing, lanes], axis=3).reshape(layers, moments, columns, tiles + 1, 128)
-    ext = jnp.transpose(ext, (2, 0, 1, 3, 4))
+    data_rows = layers * moments * tiles
+    padded_rows = -(-(data_rows + layers) // 8) * 8
+    body = jnp.transpose(forcing, (2, 0, 1, 3)).reshape(columns, data_rows, 128)
+    lanes = jnp.broadcast_to(jnp.transpose(decay_rates)[:, :, None], (columns, layers, 128))
+    spare = jnp.zeros((columns, padded_rows - data_rows - layers, 128), jnp.float32)
+    ext = jnp.concatenate([body, lanes, spare], axis=1)
     out = pl.pallas_call(
-        functools.partial(exchange_kernel, count),
-        out_shape=jax.ShapeDtypeStruct((columns, layers, moments, tiles, 128), jnp.float32),
+        functools.partial(exchange_kernel, count, layers),
+        out_shape=jax.ShapeDtypeStruct((columns, data_rows, 128), jnp.float32),
         in_specs=[pl.BlockSpec(memory_space=pltpu.VMEM)],
         out_specs=pl.BlockSpec(memory_space=pltpu.VMEM),
         scratch_shapes=[
-            pltpu.VMEM((count, layers, moments, tiles + 1, 128), jnp.float32),
-            pltpu.VMEM((count, layers, moments, tiles, 128), jnp.float32),
+            pltpu.VMEM((count, padded_rows, 128), jnp.float32),
+            pltpu.VMEM((count, data_rows, 128), jnp.float32),
             pltpu.SemaphoreType.DMA((count,)),
             pltpu.SemaphoreType.DMA((count,)),
             pltpu.SemaphoreType.DMA((count,)),
@@ -272,7 +277,7 @@
         ],
         compiler_params=pltpu.CompilerParams(collective_id=0, has_side_effects=True),
     )(ext)
-    return jnp.transpose(out, (1, 2, 0, 3, 4)).reshape(layers, moments, columns, width)
+    return jnp.transpose(out.reshape(columns, layers, moments, width), (1, 2, 0, 3))
 
 
 def front_kernel(layer_count, row_count, block_ref, coef_ref, below, above, left, right, total,

time: 84.8 us -> 87.8 us (1.035)
  other arithmetic: 7.81 us -> 9.36 us
  Pallas kernels: 64.2 us -> 65.4 us
    pallas_call x1, Pallas kernels: 46.1 us -> 47.3 us  [sweeps(): pl.pallas_call(functools.partial(exchange_kernel, count, layers), out_sha...]
    reshape x4 -> x2, local copies, waits for them, and re-layouts: 2.96 us -> 1.95 us  [the longest x1 1.43 us: sweeps(): out.reshape(columns, layers, moments, width)]
    concatenate x1, other arithmetic: 0.05 us -> 1 us  [sweeps(): ext = jnp.concatenate([body, lanes, spare], axis=1)]
where the time goes in v7:
time: 87.8 us; the launch traced here: 86.6 us
  Pallas kernels  65.4 us (74%)
  local copies, waits for them, and re-layouts  10.2 us (12%)
  other arithmetic  9.36 us (11%)
  matrix products  1.43 us (2%)
    pallas_call x1, Pallas kernels, sweeps(): pl.pallas_call(functools.partial(exchange_kernel, count, layers), out_sha...  47.3 us
    pallas_call x1, Pallas kernels, front_exchange(): pl.pallas_call(functools.partial(front_kernel, layer_count, row_count), o...  18.1 us
    sub x1, other arithmetic, shards(): w0 * hamil - w1 * probes  3.52 us
    unnamed x22, local copies, waits for them, and re-layouts  3.14 us

profile of v7, /device:TPU:32, one launch (start us, length us, event | category | flops | bytes accessed | tf_op | source)
XLA Modules:
  0.0 86.6 jit_solution(12130710945872953061)
XLA Ops:
  0.0 0.0 copy-start
  0.0 1.1 %convert_element_type.18 = bf16[2,32,2,640]{3,2,1,0:T(2,128)(2,1)S(1)} convert(f32[2,32,2,640]{3,2,1,0:T(2,128)} %param.8) | non-fusion elementwise | flops 81920 | bytes 491520 | tf_op jit(solution)/shard_map/convert_element_type | solution.py:363
  1.1 0.1 reshape.40
  1.3 0.0 copy-done
  1.3 0.0 copy-start.6
  1.3 0.0 copy-start.1
  1.3 0.2 fusion.23
  1.5 0.5 copy-done.6
  1.9 0.9 fusion.16.coef_ref
  2.8 0.0 copy-done.1
  2.8 1.0 %reshape.39.block_ref = f32[2,32,1280]{2,1,0:T(8,128)} reshape(f32[2,32,2,640]{3,2,1,0:T(2,128)S(1)} %copy-done.1) | data formatting | bytes 655360 | tf_op jit(solution)/shard_map/reshape | solution.py:370
  3.8 18.1 %shard_map.82 = (f32[2,32,1280]{2,1,0:T(8,128)}, f32[2,32,1280]{2,1,0:T(8,128)}, f32[2,32,1280]{2,1,0:T(8,128)}, f32[2,32,1280]{2,1,0:T(8,128)}, f32[2,32,256]{2,1,0:T(8,128)}) custom-call(f32[2,32,1280]{2,1,0:T(8,128)} %reshape.39.block_ref, f32[2,32,256]{2,1,0:T(8,128)} %fusion.16.coef_ref), custom_call_target="tpu_custom_call" | custom-call | tf_op jit(solution)/shard_map/pallas_call | solution.py:337
  21.9 1.1 %broadcast_select_fusion.2 = (f32[2,32,1280]{2,1,0:T(8,128)S(1)}, f32[2,32,1280]{2,1,0:T(8,128)S(1)}) fusion(f32[2,32,1280]{2,1,0:T(8,128)} %get-tuple-element.11, pred[]{:T(512)S(6)} %lt.6, f32[2,32,1280]{2,1,0:T(8,128)} %get-tuple-element.10, pred[]{:T(512)S(6)} %gt.6), kind=kLoop, calls=%fused_computation.30 | loop fusion | flops 163840 | bytes 1310722 | tf_op jit(solution)/shard_map/jit(_where)/select_n | solution.py:375
  23.0 0.2 reshape.41
  23.2 0.0 copy-start.2
  23.2 0.0 copy-start.3
  23.2 0.2 reshape.42
  23.4 0.8 copy-done.2
  24.2 0.1 copy-done.3
  24.3 0.2 reshape.43
  24.5 0.0 copy-start.4
  24.5 0.0 copy-start.7
  24.5 0.2 reshape.44
  24.7 0.6 copy-done.4
  25.4 0.0 copy-done.7
  25.4 0.4 fusion
  25.7 0.0 copy-start.9
  25.7 0.0 copy-start.10
  25.8 0.0 copy-start.5
  25.8 0.2 reshape.45
  26.0 0.4 copy-done.9
  26.4 0.0 copy-done.10
  26.4 0.7 multiply_reduce_fusion.1
  27.1 0.0 copy-done.5
  27.1 3.5 %multiply_subtract_fusion.1 = (f32[2,32,2,640]{3,2,1,0:T(2,128)S(1)}, f32[2,32,2,640]{3,2,1,0:T(2,128)S(1)}) fusion(f32[2,32,2,640]{3,2,1,0:T(2,128)S(1)} %copy-done.1, f32[]{:T(128)} %get-tuple-element.15, f32[]{:T(128)} %get-tuple-element.17, f32[2,32,2,640]{3,2,1,0:T(2,128)S(1)} %reshape.45, f32[2,2,640]{2,1,0:T(2,128)S(1)} %copy-done.5, ...), kind=kLoop, calls=%fused_computation.23 | loop fusion | flops 2621440 | bytes 2631688 | tf_op jit(solution)/shard_map/sub | solution.py:396
  30.6 1.3 %multiply_subtract_fusion = f32[2,8,8,640]{3,2,1,0:T(8,128)S(1)} fusion(f32[2,8,8,640]{3,2,1,0:T(8,128)S(1)} %bitcast.13, f32[2,8,8,640]{3,2,1,0:T(8,128)S(1)} %bitcast.16, f32[]{:T(128)} %get-tuple-element.16, f32[]{:T(128)} %get-tuple-element.15), kind=kLoop, calls=%fused_computation.22 | loop fusion | flops 245760 | bytes 983048 | tf_op jit(solution)/shard_map/sub | solution.py:396
  31.9 0.3 stack.10
  32.2 0.3 copy.10
  32.5 0.3 stack.9
  32.8 0.3 copy.9
  33.1 0.6 maximum_bitcast_fusion
  33.7 0.5 reshape.46
  34.3 0.0 copy-start.8
  34.3 0.7 copy-done.8
  34.9 0.1 copy.11
  35.0 0.1 broadcast_in_dim.21
  35.1 0.1 pad.7.clone
  35.2 1.0 %maximum_maximum_fusion.ext_ref = f32[32,48,128]{2,1,0:T(8,128)} fusion(f32[32,2,128]{2,1,0:T(2,128)S(1)} %broadcast_in_dim.21, f32[32,40,128]{2,1,0:T(8,128)S(1)} %reshape.46, f32[48]{0:T(128)S(1)} %pad.7.clone), kind=kLoop, calls=%fused_computation.2 | loop fusion | flops 393216 | bytes 1474752 | tf_op jit(solution)/shard_map/concatenate | solution.py:264
  36.2 47.3 %shard_map.83 = f32[32,40,128]{2,1,0:T(8,128)} custom-call(f32[32,48,128]{2,1,0:T(8,128)} %maximum_maximum_fusion.ext_ref), custom_call_target="tpu_custom_call" | custom-call | tf_op jit(solution)/shard_map/pallas_call | solution.py:265
  83.5 1.4 %reshape.47 = f32[32,2,2,1280]{3,2,1,0:T(2,128)S(1)} reshape(f32[32,40,128]{2,1,0:T(8,128)} %shard_map.83) | data formatting | bytes 1310720 | tf_op jit(solution)/shard_map/reshape | solution.py:280
  84.9 0.8 reshape.49
  85.7 0.9 %copy.13 = f32[2,2,32,2,640]{4,3,2,1,0:T(2,128)} copy(f32[2,2,32,2,640]{4,3,0,1,2:T(2,128)S(1)} %reshape.49) | data formatting | bytes 1310720 | tf_op jit(solution)/shard_map/reshape | solution.py:398
  (2 shorter events, 0.0 us)
Async XLA Ops:
  0.0 1.3 %copy-start = (bf16[2,64,1280]{2,1,0:T(8,128)(2,1)S(1)}, bf16[2,64,1280]{2,1,0:T(8,128)(2,1)}, u32[]{:S(2)}) copy-start(bf16[2,64,1280]{2,1,0:T(8,128)(2,1)} %param.10) | copy-start | bytes 983044
  1.3 0.7 copy-start.6
  1.3 1.5 %copy-start.1 = (f32[2,32,2,640]{3,2,1,0:T(2,128)S(1)}, f32[2,32,2,640]{3,2,1,0:T(2,128)}, u32[]{:S(2)}) copy-start(f32[2,32,2,640]{3,2,1,0:T(2,128)} %param.8) | copy-start | bytes 983044
  23.2 1.0 %copy-start.2 = (f32[2,32,1280]{2,1,0:T(8,128)S(1)}, f32[2,32,1280]{2,1,0:T(8,128)}, u32[]{:S(2)}) copy-start(f32[2,32,1280]{2,1,0:T(8,128)} %get-tuple-element.12) | copy-start | bytes 983044
  23.2 1.1 %copy-start.3 = (f32[2,32,1280]{2,1,0:T(8,128)S(1)}, f32[2,32,1280]{2,1,0:T(8,128)}, u32[]{:S(2)}) copy-start(f32[2,32,1280]{2,1,0:T(8,128)} %get-tuple-element.13) | copy-start | bytes 983044
  24.5 0.8 copy-start.4
  24.5 0.8 copy-start.7
  25.7 0.7 copy-start.9
  25.7 0.7 copy-start.10
  25.8 1.3 %copy-start.5 = (f32[2,2,640]{2,1,0:T(2,128)S(1)}, f32[2,2,640]{2,1,0:T(2,128)}, u32[]{:S(2)}) copy-start(f32[2,2,640]{2,1,0:T(2,128)} %param.9) | copy-start | bytes 30724
  34.3 0.7 copy-start.8

commit v8 on v7

--- a/solution.py
+++ b/solution.py
@@ -149,7 +149,7 @@
         o_ref[:, index] = back[index] + upper[None] * from_above
 
 
-def exchange_kernel(count, layer_count, ext_ref, out_ref, gathered, swept, send_sem, recv_sem, back_send, back_recv):
+def exchange_kernel(count, layer_count, w_ref, ext_ref, out_ref, gathered, swept, send_sem, recv_sem, back_send, back_recv):
     me = lax.axis_index("layer")
     row = lax.axis_index("xs")
     layers = layer_count
@@ -195,13 +195,40 @@
     lax.fori_loop(1, count, arrived, 0)
 
     rows_per_layer = out_ref.shape[1] // layers
+    half = rows_per_layer // 2
     zero = jnp.zeros((rows_per_layer, out_ref.shape[2]), jnp.float32)
     data_rows = out_ref.shape[1]
+    total = count * layers
+    w0, w1, w2 = w_ref[0], w_ref[1], w_ref[2]
+
+    def probe_at(place):
+        inside = ((place >= 0) & (place < total)).astype(jnp.float32)
+        place = jnp.clip(place, 0, total - 1)
+        source = place // layers
+        layer = place - source * layers
+        return inside * gathered[source, pl.ds(layer * rows_per_layer + half, half), :]
+
+    def prepare(source, carry):
+        for layer in range(layers):
+            place = source * layers + layer
+            here = gathered[source, pl.ds(layer * rows_per_layer + half, half), :]
+            partial = gathered[source, pl.ds(layer * rows_per_layer, half), :]
+            second = (
+                FAR * (probe_at(place - 2) + probe_at(place + 2))
+                + NEAR * (probe_at(place - 1) + probe_at(place + 1))
+                + CENTER * here
+            )
+            hamil = partial - 0.5 * second
+            swept[source, pl.ds(layer * rows_per_layer, half), :] = w0 * hamil - w1 * here
+            swept[source, pl.ds(layer * rows_per_layer + half, half), :] = w1 * hamil - w2 * here
+        return carry
+
+    lax.fori_loop(0, count, prepare, 0)
 
     def forward(source, state):
         for layer in range(layers):
             rate = gathered[source, pl.ds(data_rows + layer, 1), :]
-            slab = gathered[source, pl.ds(layer * rows_per_layer, rows_per_layer), :]
+            slab = swept[source, pl.ds(layer * rows_per_layer, rows_per_layer), :]
             state = rate * state + (1.0 - rate) * slab
             swept[source, pl.ds(layer * rows_per_layer, rows_per_layer), :] = state
         return state
@@ -250,7 +277,7 @@
     lax.fori_loop(1, count, returned, 0)
 
 
-def sweeps(forcing, decay_rates):
+def sweeps(forcing, decay_rates, weights):
     layers, moments, columns, width = forcing.shape
     count = lax.axis_size("layer")
     if columns != count:
@@ -265,7 +292,7 @@
     out = pl.pallas_call(
         functools.partial(exchange_kernel, count, layers),
         out_shape=jax.ShapeDtypeStruct((columns, data_rows, 128), jnp.float32),
-        in_specs=[pl.BlockSpec(memory_space=pltpu.VMEM)],
+        in_specs=[pl.BlockSpec(memory_space=pltpu.SMEM), pl.BlockSpec(memory_space=pltpu.VMEM)],
         out_specs=pl.BlockSpec(memory_space=pltpu.VMEM),
         scratch_shapes=[
             pltpu.VMEM((count, padded_rows, 128), jnp.float32),
@@ -276,30 +303,22 @@
             pltpu.SemaphoreType.DMA((count,)),
         ],
         compiler_params=pltpu.CompilerParams(collective_id=0, has_side_effects=True),
-    )(ext)
+    )(weights, ext)
     return jnp.transpose(out.reshape(columns, layers, moments, width), (1, 2, 0, 3))
 
 
-def front_kernel(layer_count, row_count, block_ref, coef_ref, below, above, left, right, total,
-                 gathered, send_sem, recv_sem):
+def front_kernel(row_count, block_ref, coef_ref, left, right, total, gathered, send_sem, recv_sem):
     me = lax.axis_index("layer")
     row = lax.axis_index("xs")
     peers = row_count - 1
     barrier = pltpu.get_barrier_semaphore()
-    for sign in (1, -1):
-        pl.semaphore_signal(
-            barrier, inc=1, device_id=(lax.rem(me + sign + layer_count, layer_count), row),
-            device_id_type=MESH,
-        )
     for step in range(1, row_count):
         pl.semaphore_signal(
             barrier, inc=1, device_id=(me, lax.rem(row + step, row_count)), device_id_type=MESH
         )
-    pl.semaphore_wait(barrier, 2 + peers)
+    pl.semaphore_wait(barrier, peers)
     copies = []
     targets = [
-        (below, (lax.rem(me + 1, layer_count), row)),
-        (above, (lax.rem(me + layer_count - 1, layer_count), row)),
         (left, (me, lax.rem(row + 1, row_count))),
         (right, (me, lax.rem(row + row_count - 1, row_count))),
     ]
@@ -313,37 +332,36 @@
     for step in range(1, row_count):
         copies.append(
             pltpu.make_async_remote_copy(
-                src_ref=coef_ref, dst_ref=gathered.at[step - 1], send_sem=send_sem.at[3 + step],
-                recv_sem=recv_sem.at[3 + step], device_id=(me, lax.rem(row + step, row_count)),
+                src_ref=coef_ref, dst_ref=gathered.at[step - 1], send_sem=send_sem.at[1 + step],
+                recv_sem=recv_sem.at[1 + step], device_id=(me, lax.rem(row + step, row_count)),
                 device_id_type=MESH,
             )
         )
     for copy in copies:
         copy.start()
-    for copy in copies[4:]:
+    for copy in copies[2:]:
         copy.wait()
     acc = coef_ref[...]
     for step in range(peers):
         acc = acc + gathered[step]
     total[...] = acc
-    for copy in copies[:4]:
+    for copy in copies[:2]:
         copy.wait()
 
 
 def front_exchange(block, coef):
-    layer_count = lax.axis_size("layer")
     row_count = lax.axis_size("xs")
     spec = pl.BlockSpec(memory_space=pltpu.VMEM)
     return pl.pallas_call(
-        functools.partial(front_kernel, layer_count, row_count),
-        out_shape=[jax.ShapeDtypeStruct(block.shape, jnp.float32)] * 4
+        functools.partial(front_kernel, row_count),
+        out_shape=[jax.ShapeDtypeStruct(block.shape, jnp.float32)] * 2
         + [jax.ShapeDtypeStruct(coef.shape, jnp.float32)],
         in_specs=[spec, spec],
-        out_specs=[spec] * 5,
+        out_specs=[spec] * 3,
         scratch_shapes=[
             pltpu.VMEM((row_count - 1,) + coef.shape, jnp.float32),
-            pltpu.SemaphoreType.DMA((3 + row_count,)),
-            pltpu.SemaphoreType.DMA((3 + row_count,)),
+            pltpu.SemaphoreType.DMA((1 + row_count,)),
+            pltpu.SemaphoreType.DMA((1 + row_count,)),
         ],
         compiler_params=pltpu.CompilerParams(collective_id=1, has_side_effects=True),
     )(block, coef)
@@ -366,20 +384,13 @@
         jnp.float32
     )
     partial_coef = jnp.einsum("lsq,lsc->lcq", onehot, slot_coef, precision=lax.Precision.HIGHEST)
-    below, above, left, right, coef = front_exchange(
-        probes.reshape(layers, columns, rows * depth), partial_coef
-    )
-    me = lax.axis_index("layer")
+    left, right, coef = front_exchange(probes.reshape(layers, columns, rows * depth), partial_coef)
     row = lax.axis_index("xs")
-    below = jnp.where(me > 0, below, 0.0).reshape(probes.shape)
-    above = jnp.where(me < lax.axis_size("layer") - 1, above, 0.0).reshape(probes.shape)
     left = jnp.where(row > 0, left, 0.0).reshape(probes.shape)
     right = jnp.where(row < lax.axis_size("xs") - 1, right, 0.0).reshape(probes.shape)
-    stacked = jnp.concatenate([below, probes, above], axis=0)
     beside = jnp.concatenate([left, probes, right], axis=2)
     across = jnp.pad(probes, ((0, 0), (0, 0), (0, 0), (2, 2)))
-    laplace = second_along(stacked, 0, layers)
-    laplace = laplace + second_along(beside, 2, rows)
+    laplace = second_along(beside, 2, rows)
     laplace = laplace + second_along(across, 3, depth)
     coef = jnp.swapaxes(coef, 1, 2)
     scaled = (strength[:, :, None] * coef).astype(jnp.bfloat16)
@@ -389,12 +400,16 @@
     projected = jnp.einsum(
         "lsp,lsc->lcp", projector, slot_back, preferred_element_type=jnp.float32
     ).reshape(layers, columns, rows, depth)
-    hamil = -0.5 * laplace + potential[:, None] * probes + projected
-    w0 = jnp.sum(node_weights)
-    w1 = jnp.sum(node_weights * contour_nodes)
-    w2 = jnp.sum(node_weights * contour_nodes * contour_nodes)
-    forcing = jnp.stack([w0 * hamil - w1 * probes, w1 * hamil - w2 * probes], axis=1)
-    swept = sweeps(forcing.reshape(layers, 2, columns, rows * depth), decay_rates)
+    partial = -0.5 * laplace + potential[:, None] * probes + projected
+    weights = jnp.stack(
+        [
+            jnp.sum(node_weights),
+            jnp.sum(node_weights * contour_nodes),
+            jnp.sum(node_weights * contour_nodes * contour_nodes),
+        ]
+    )
+    fields = jnp.stack([partial, probes], axis=1)
+    swept = sweeps(fields.reshape(layers, 2, columns, rows * depth), decay_rates, weights)
     return jnp.swapaxes(swept, 0, 1).reshape(2, layers, columns, rows, depth)
 
 

time: 87.8 us -> 88.1 us (level)
  the two profiles are of different devices: /device:TPU:32 before, /device:TPU:1 now
where the time goes in v8:
time: 88.1 us; the launch traced here: 87.7 us
  Pallas kernels  68.4 us (78%)
  local copies, waits for them, and re-layouts  9.01 us (10%)
  other arithmetic  8.65 us (10%)
  matrix products  1.42 us (2%)
    pallas_call x1, Pallas kernels, sweeps(): pl.pallas_call(functools.partial(exchange_kernel, count, layers), out_sha...  50.2 us
    pallas_call x1, Pallas kernels, front_exchange(): pl.pallas_call(functools.partial(front_kernel, row_count), out_shape=[jax...  18.3 us
    another operation x1, other arithmetic, shards(): jnp.stack([jnp.sum(node_weights), jnp.sum(node_weights * contour_nodes),...  2.55 us
    unnamed x18, local copies, waits for them, and re-layouts  2.32 us

profile of v8, /device:TPU:1, one launch (start us, length us, event | category | flops | bytes accessed | tf_op | source)
XLA Modules:
  0.0 87.7 jit_solution(17247240368724006525)
XLA Ops:
  0.0 0.0 copy-start
  0.0 1.1 %convert_element_type.18 = bf16[2,32,2,640]{3,2,1,0:T(2,128)(2,1)S(1)} convert(f32[2,32,2,640]{3,2,1,0:T(2,128)} %param.8) | non-fusion elementwise | flops 81920 | bytes 491520 | tf_op jit(solution)/shard_map/convert_element_type | solution.py:381
  1.1 0.1 reshape.34
  1.3 0.0 copy-done
  1.3 0.0 copy-start.4
  1.3 0.0 copy-start.1
  1.3 0.2 fusion.14
  1.5 0.5 copy-done.4
  1.9 0.9 fusion.8.coef_ref
  2.8 0.0 copy-done.1
  2.8 1.0 %reshape.33.block_ref = f32[2,32,1280]{2,1,0:T(8,128)} reshape(f32[2,32,2,640]{3,2,1,0:T(2,128)S(1)} %copy-done.1) | data formatting | bytes 655360 | tf_op jit(solution)/shard_map/reshape | solution.py:387
  3.8 18.3 %shard_map.82 = (f32[2,32,1280]{2,1,0:T(8,128)}, f32[2,32,1280]{2,1,0:T(8,128)}, f32[2,32,256]{2,1,0:T(8,128)}) custom-call(f32[2,32,1280]{2,1,0:T(8,128)} %reshape.33.block_ref, f32[2,32,256]{2,1,0:T(8,128)} %fusion.8.coef_ref), custom_call_target="tpu_custom_call" | custom-call | tf_op jit(solution)/shard_map/pallas_call | solution.py:355
  22.1 1.1 %broadcast_select_fusion = (f32[2,32,1280]{2,1,0:T(8,128)S(1)}, f32[2,32,1280]{2,1,0:T(8,128)S(1)}) fusion(f32[2,32,1280]{2,1,0:T(8,128)} %get-tuple-element.9, pred[]{:T(512)S(6)} %lt.3, f32[2,32,1280]{2,1,0:T(8,128)} %get-tuple-element.8, pred[]{:T(512)S(6)} %gt.3), kind=kLoop, calls=%fused_computation.16 | loop fusion | flops 163840 | bytes 1310722 | tf_op jit(solution)/shard_map/jit(_where)/select_n | solution.py:390
  23.2 0.2 reshape.35
  23.4 0.0 copy-start.2
  23.4 0.0 copy-start.5
  23.4 0.2 reshape.36
  23.6 0.6 copy-done.2
  24.2 0.0 copy-done.5
  24.2 0.4 fusion
  24.6 0.0 copy-start.3
  24.6 0.2 reshape.37
  24.8 0.5 copy-done.3
  25.3 1.6 %add_add_fusion = f32[2,32,2,640]{3,2,1,0:T(2,128)S(1)} fusion(f32[2,32,2,640]{3,2,1,0:T(2,128)S(1)} %reshape.37, f32[2,32,2,640]{3,2,1,0:T(2,128)S(1)} %copy-done.1, f32[2,32,2,640]{3,2,1,0:T(2,128)S(1)} %reshape.36, f32[2,32,2,640]{3,2,1,0:T(2,128)S(1)} %reshape.35, f32[2,2,640]{2,1,0:T(2,128)S(1)} %copy-done.3), kind=kLoop, calls=%fused_computation.11 | loop fusion | flops 1638400 | bytes 1648640 | tf_op jit(solution)/shard_map/add | solution.py:403
  26.9 0.3 stack.25
  27.2 0.3 copy.9
  27.5 0.3 stack.26
  27.8 0.3 copy.10
  28.1 0.6 maximum_bitcast_fusion
  28.7 0.5 reshape.38
  29.3 0.0 copy-start.6
  29.3 0.7 copy-done.6
  29.9 0.1 copy.11
  30.0 0.1 broadcast_in_dim.10
  30.1 0.1 pad.7.clone
  30.2 0.0 copy-start.7
  30.2 0.0 copy-start.8
  30.2 1.0 %maximum_maximum_fusion.ext_ref = f32[32,48,128]{2,1,0:T(8,128)} fusion(f32[32,2,128]{2,1,0:T(2,128)S(1)} %broadcast_in_dim.10, f32[32,40,128]{2,1,0:T(8,128)S(1)} %reshape.38, f32[48]{0:T(128)S(1)} %pad.7.clone), kind=kLoop, calls=%fused_computation.2 | loop fusion | flops 393216 | bytes 1474752 | tf_op jit(solution)/shard_map/concatenate | solution.py:291
  31.2 0.0 copy-done.7
  31.2 0.0 copy-done.8
  31.2 0.7 multiply_reduce_fusion.1
  31.9 2.5 %pad_maximum_fusion.2.w_ref = f32[3]{0:T(128)} fusion(f32[1]{0:T(128)} %bitcast.2, f32[1]{0:T(128)} %bitcast.1, f32[1]{0:T(128)} %bitcast), kind=kLoop, calls=%fused_computation.25 | loop fusion | flops 6 | bytes 24 | tf_op jit(solution)/shard_map/stack | solution.py:404
  34.4 50.2 %shard_map.83 = f32[32,40,128]{2,1,0:T(8,128)} custom-call(f32[3]{0:T(128)} %pad_maximum_fusion.2.w_ref, f32[32,48,128]{2,1,0:T(8,128)} %maximum_maximum_fusion.ext_ref), custom_call_target="tpu_custom_call" | custom-call | tf_op jit(solution)/shard_map/pallas_call | solution.py:292
  84.6 1.4 %reshape.39 = f32[32,2,2,1280]{3,2,1,0:T(2,128)S(1)} reshape(f32[32,40,128]{2,1,0:T(8,128)} %shard_map.83) | data formatting | bytes 1310720 | tf_op jit(solution)/shard_map/reshape | solution.py:307
  86.1 0.8 reshape.41
  86.8 0.9 %copy.13 = f32[2,2,32,2,640]{4,3,2,1,0:T(2,128)} copy(f32[2,2,32,2,640]{4,3,0,1,2:T(2,128)S(1)} %reshape.41) | data formatting | bytes 1310720 | tf_op jit(solution)/shard_map/reshape | solution.py:413
  (1 shorter events, 0.0 us)
Async XLA Ops:
  0.0 1.3 %copy-start = (bf16[2,64,1280]{2,1,0:T(8,128)(2,1)S(1)}, bf16[2,64,1280]{2,1,0:T(8,128)(2,1)}, u32[]{:S(2)}) copy-start(bf16[2,64,1280]{2,1,0:T(8,128)(2,1)} %param.10) | copy-start | bytes 983044
  1.3 0.7 copy-start.4
  1.3 1.5 %copy-start.1 = (f32[2,32,2,640]{3,2,1,0:T(2,128)S(1)}, f32[2,32,2,640]{3,2,1,0:T(2,128)}, u32[]{:S(2)}) copy-start(f32[2,32,2,640]{3,2,1,0:T(2,128)} %param.8) | copy-start | bytes 983044
  23.4 0.8 copy-start.2
  23.4 0.8 copy-start.5
  24.6 0.7 copy-start.3
  29.3 0.7 copy-start.6
  30.2 1.0 %copy-start.7 = (f32[4]{0:T(128)S(1)}, f32[4]{0:T(128)}, u32[]{:S(2)}) copy-start(f32[4]{0:T(128)} %param.15) | copy-start | bytes 52
  30.2 1.0 %copy-start.8 = (f32[4]{0:T(128)S(1)}, f32[4]{0:T(128)}, u32[]{:S(2)}) copy-start(f32[4]{0:T(128)} %param.14) | copy-start | bytes 52

commit v9 on v8

--- a/solution.py
+++ b/solution.py
@@ -149,7 +149,7 @@
         o_ref[:, index] = back[index] + upper[None] * from_above
 
 
-def exchange_kernel(count, layer_count, w_ref, ext_ref, out_ref, gathered, swept, send_sem, recv_sem, back_send, back_recv):
+def exchange_kernel(count, layer_count, w_ref, ext_ref, probe_ref, out_ref, gathered, swept, send_sem, recv_sem, back_send, back_recv):
     me = lax.axis_index("layer")
     row = lax.axis_index("xs")
     layers = layer_count
@@ -197,7 +197,7 @@
     rows_per_layer = out_ref.shape[1] // layers
     half = rows_per_layer // 2
     zero = jnp.zeros((rows_per_layer, out_ref.shape[2]), jnp.float32)
-    data_rows = out_ref.shape[1]
+    data_rows = layers * half
     total = count * layers
     w0, w1, w2 = w_ref[0], w_ref[1], w_ref[2]
 
@@ -206,13 +206,13 @@
         place = jnp.clip(place, 0, total - 1)
         source = place // layers
         layer = place - source * layers
-        return inside * gathered[source, pl.ds(layer * rows_per_layer + half, half), :]
+        return inside * probe_ref[source, pl.ds(layer * half, half), :]
 
     def prepare(source, carry):
         for layer in range(layers):
             place = source * layers + layer
-            here = gathered[source, pl.ds(layer * rows_per_layer + half, half), :]
-            partial = gathered[source, pl.ds(layer * rows_per_layer, half), :]
+            here = probe_ref[source, pl.ds(layer * half, half), :]
+            partial = gathered[source, pl.ds(layer * half, half), :]
             second = (
                 FAR * (probe_at(place - 2) + probe_at(place + 2))
                 + NEAR * (probe_at(place - 1) + probe_at(place + 1))
@@ -277,37 +277,40 @@
     lax.fori_loop(1, count, returned, 0)
 
 
-def sweeps(forcing, decay_rates, weights):
-    layers, moments, columns, width = forcing.shape
+def sweeps(partial, gathered_probes, decay_rates, weights):
+    layers, columns, width = partial.shape
+    moments = 2
     count = lax.axis_size("layer")
     if columns != count:
         raise ValueError("columns")
     tiles = width // 128
-    data_rows = layers * moments * tiles
+    data_rows = layers * tiles
     padded_rows = -(-(data_rows + layers) // 8) * 8
-    body = jnp.transpose(forcing, (2, 0, 1, 3)).reshape(columns, data_rows, 128)
+    body = jnp.transpose(partial, (1, 0, 2)).reshape(columns, data_rows, 128)
     lanes = jnp.broadcast_to(jnp.transpose(decay_rates)[:, :, None], (columns, layers, 128))
     spare = jnp.zeros((columns, padded_rows - data_rows - layers, 128), jnp.float32)
     ext = jnp.concatenate([body, lanes, spare], axis=1)
+    vmem = pl.BlockSpec(memory_space=pltpu.VMEM)
     out = pl.pallas_call(
         functools.partial(exchange_kernel, count, layers),
-        out_shape=jax.ShapeDtypeStruct((columns, data_rows, 128), jnp.float32),
-        in_specs=[pl.BlockSpec(memory_space=pltpu.SMEM), pl.BlockSpec(memory_space=pltpu.VMEM)],
-        out_specs=pl.BlockSpec(memory_space=pltpu.VMEM),
+        out_shape=jax.ShapeDtypeStruct((columns, moments * data_rows, 128), jnp.float32),
+        in_specs=[pl.BlockSpec(memory_space=pltpu.SMEM), vmem, vmem],
+        out_specs=vmem,
         scratch_shapes=[
             pltpu.VMEM((count, padded_rows, 128), jnp.float32),
-            pltpu.VMEM((count, data_rows, 128), jnp.float32),
+            pltpu.VMEM((count, moments * data_rows, 128), jnp.float32),
             pltpu.SemaphoreType.DMA((count,)),
             pltpu.SemaphoreType.DMA((count,)),
             pltpu.SemaphoreType.DMA((count,)),
             pltpu.SemaphoreType.DMA((count,)),
         ],
         compiler_params=pltpu.CompilerParams(collective_id=0, has_side_effects=True),
-    )(weights, ext)
+    )(weights, ext, gathered_probes)
     return jnp.transpose(out.reshape(columns, layers, moments, width), (1, 2, 0, 3))
 
 
-def front_kernel(row_count, block_ref, coef_ref, left, right, total, gathered, send_sem, recv_sem):
+def front_kernel(row_count, layer_count, block_ref, coef_ref, pieces_ref, left, right, total, regrouped,
+                 gathered, send_sem, recv_sem, piece_send, piece_recv):
     me = lax.axis_index("layer")
     row = lax.axis_index("xs")
     peers = row_count - 1
@@ -316,7 +319,28 @@
         pl.semaphore_signal(
             barrier, inc=1, device_id=(me, lax.rem(row + step, row_count)), device_id_type=MESH
         )
-    pl.semaphore_wait(barrier, peers)
+
+    def greet(step, carry):
+        pl.semaphore_signal(
+            barrier, inc=1, device_id=(lax.rem(me + step, layer_count), row), device_id_type=MESH
+        )
+        return carry
+
+    lax.fori_loop(1, layer_count, greet, 0)
+    pl.semaphore_wait(barrier, peers + layer_count - 1)
+
+    def outgoing(step, carry):
+        target = lax.rem(me + step, layer_count)
+        pltpu.make_async_remote_copy(
+            src_ref=pieces_ref.at[target],
+            dst_ref=regrouped.at[me],
+            send_sem=piece_send.at[step],
+            recv_sem=piece_recv.at[step],
+            device_id=(target, row),
+            device_id_type=MESH,
+        ).start()
+        return carry
+
     copies = []
     targets = [
         (left, (me, lax.rem(row + 1, row_count))),
@@ -339,6 +363,8 @@
         )
     for copy in copies:
         copy.start()
+    lax.fori_loop(1, layer_count, outgoing, 0)
+    regrouped[me] = pieces_ref[me]
     for copy in copies[2:]:
         copy.wait()
     acc = coef_ref[...]
@@ -348,23 +374,44 @@
     for copy in copies[:2]:
         copy.wait()
 
+    def arrived(step, carry):
+        copy = pltpu.make_async_remote_copy(
+            src_ref=pieces_ref.at[me],
+            dst_ref=regrouped.at[lax.rem(me + layer_count - step, layer_count)],
+            send_sem=piece_send.at[step],
+            recv_sem=piece_recv.at[step],
+            device_id=(lax.rem(me + step, layer_count), row),
+            device_id_type=MESH,
+        )
+        copy.wait_send()
+        copy.wait_recv()
+        return carry
+
+    lax.fori_loop(1, layer_count, arrived, 0)
+
 
 def front_exchange(block, coef):
     row_count = lax.axis_size("xs")
+    layer_count = lax.axis_size("layer")
+    layers, columns, width = block.shape
+    pieces = jnp.transpose(block, (1, 0, 2)).reshape(columns, layers * width // 128, 128)
     spec = pl.BlockSpec(memory_space=pltpu.VMEM)
     return pl.pallas_call(
-        functools.partial(front_kernel, row_count),
+        functools.partial(front_kernel, row_count, layer_count),
         out_shape=[jax.ShapeDtypeStruct(block.shape, jnp.float32)] * 2
-        + [jax.ShapeDtypeStruct(coef.shape, jnp.float32)],
-        in_specs=[spec, spec],
-        out_specs=[spec] * 3,
+        + [jax.ShapeDtypeStruct(coef.shape, jnp.float32),
+           jax.ShapeDtypeStruct((layer_count,) + pieces.shape[1:], jnp.float32)],
+        in_specs=[spec, spec, spec],
+        out_specs=[spec] * 4,
         scratch_shapes=[
             pltpu.VMEM((row_count - 1,) + coef.shape, jnp.float32),
             pltpu.SemaphoreType.DMA((1 + row_count,)),
             pltpu.SemaphoreType.DMA((1 + row_count,)),
+            pltpu.SemaphoreType.DMA((layer_count,)),
+            pltpu.SemaphoreType.DMA((layer_count,)),
         ],
         compiler_params=pltpu.CompilerParams(collective_id=1, has_side_effects=True),
-    )(block, coef)
+    )(block, coef, pieces)
 
 
 def shards(
@@ -384,7 +431,9 @@
         jnp.float32
     )
     partial_coef = jnp.einsum("lsq,lsc->lcq", onehot, slot_coef, precision=lax.Precision.HIGHEST)
-    left, right, coef = front_exchange(probes.reshape(layers, columns, rows * depth), partial_coef)
+    left, right, coef, regrouped = front_exchange(
+        probes.reshape(layers, columns, rows * depth), partial_coef
+    )
     row = lax.axis_index("xs")
     left = jnp.where(row > 0, left, 0.0).reshape(probes.shape)
     right = jnp.where(row < lax.axis_size("xs") - 1, right, 0.0).reshape(probes.shape)
@@ -408,8 +457,7 @@
             jnp.sum(node_weights * contour_nodes * contour_nodes),
         ]
     )
-    fields = jnp.stack([partial, probes], axis=1)
-    swept = sweeps(fields.reshape(layers, 2, columns, rows * depth), decay_rates, weights)
+    swept = sweeps(partial.reshape(layers, columns, rows * depth), regrouped, decay_rates, weights)
     return jnp.swapaxes(swept, 0, 1).reshape(2, layers, columns, rows, depth)
 
 

time: 88.1 us -> 80.3 us (0.911)
  the two profiles are of different devices: /device:TPU:1 before, /device:TPU:32 now
where the time goes in v9:
time: 80.3 us; the launch traced here: 79.8 us
  Pallas kernels  61.4 us (76%)
  local copies, waits for them, and re-layouts  10.1 us (13%)
  other arithmetic  6.77 us (8%)
  matrix products  1.43 us (2%)
    pallas_call x1, Pallas kernels, sweeps(): pl.pallas_call(functools.partial(exchange_kernel, count, layers), out_sha...  37.4 us
    pallas_call x1, Pallas kernels, front_exchange(): pl.pallas_call(functools.partial(front_kernel, row_count, layer_count), o...  23.9 us
    unnamed x20, local copies, waits for them, and re-layouts  2.77 us
    another operation x1, other arithmetic, shards(): jnp.stack([jnp.sum(node_weights), jnp.sum(node_weights * contour_nodes),...  2.52 us
    reshape x2, local copies, waits for them, and re-layouts, shards(): return jnp.swapaxes(swept, 0, 1).reshape(2, layers, columns, rows, depth)  1.67 us

profile of v9, /device:TPU:32, one launch (start us, length us, event | category | flops | bytes accessed | tf_op | source)
XLA Modules:
  0.0 79.8 jit_solution(4583201821252615692)
XLA Ops:
  0.0 0.0 copy-start
  0.0 1.3 %reshape.34.block_ref = f32[2,32,1280]{2,1,0:T(8,128)S(1)} reshape(f32[2,32,2,640]{3,2,1,0:T(2,128)} %param.8) | data formatting | bytes 655360 | tf_op jit(solution)/shard_map/reshape | solution.py:435
  1.3 0.0 copy-start.1
  1.3 0.3 copy.13
  1.6 0.4 copy-done.1
  2.0 0.0 copy-start.2
  2.0 1.0 %reshape.36.pieces_ref = f32[32,20,128]{2,1,0:T(8,128)} reshape(f32[32,2,1280]{2,1,0:T(2,128)S(1)} %copy.13) | data formatting | bytes 655360 | tf_op jit(solution)/shard_map/reshape | solution.py:397
  3.0 0.0 copy-done.2
  3.0 0.1 convert_element_type.18
  3.1 0.1 reshape.35
  3.2 0.0 copy-done
  3.3 0.0 copy-start.5
  3.3 0.2 fusion.14
  3.5 0.5 copy-done.5
  3.9 0.9 %fusion.8.coef_ref = f32[2,32,256]{2,1,0:T(8,128)} fusion(f32[2,64,32]{1,2,0:T(8,128)S(1)} %fusion.14, s32[2,64]{1,0:T(2,128)S(1)} %copy-done.5), kind=kOutput, calls=%fused_computation.20 | convolution fusion | flops 12615680 | bytes 82432 | tf_op jit(solution)/shard_map/lsq,lsc->lcq/dot_general | solution.py:433
  4.8 23.9 %shard_map.82 = (f32[2,32,1280]{2,1,0:T(8,128)}, f32[2,32,1280]{2,1,0:T(8,128)}, f32[2,32,256]{2,1,0:T(8,128)}, f32[32,20,128]{2,1,0:T(8,128)}) custom-call(f32[2,32,1280]{2,1,0:T(8,128)} %copy-done.1, f32[2,32,256]{2,1,0:T(8,128)} %fusion.8.coef_ref, f32[32,20,128]{2,1,0:T(8,128)} %reshape.36.pieces_ref), custom_call_target="tpu_custom_call" | custom-call | tf_op jit(solution)/shard_map/pallas_call | solution.py:399
  28.8 1.0 %broadcast_select_fusion = (f32[2,32,1280]{2,1,0:T(8,128)S(1)}, f32[2,32,1280]{2,1,0:T(8,128)S(1)}) fusion(f32[2,32,1280]{2,1,0:T(8,128)} %get-tuple-element.10, pred[]{:T(512)S(6)} %lt.3, f32[2,32,1280]{2,1,0:T(8,128)} %get-tuple-element.9, pred[]{:T(512)S(6)} %gt.3), kind=kLoop, calls=%fused_computation.16 | loop fusion | flops 163840 | bytes 1310722 | tf_op jit(solution)/shard_map/jit(_where)/select_n | solution.py:439
  29.8 0.2 reshape.37
  30.0 0.0 copy-start.3
  30.0 0.0 copy-start.6
  30.0 0.2 reshape.38
  30.2 0.6 copy-done.3
  30.8 0.0 copy-done.6
  30.8 0.4 fusion
  31.2 0.0 copy-start.4
  31.2 0.2 reshape.39
  31.4 0.5 copy-done.4
  31.9 1.6 %add_add_fusion = f32[2,32,2,640]{3,2,1,0:T(2,128)S(1)} fusion(f32[2,32,2,640]{3,2,1,0:T(2,128)S(1)} %reshape.39, f32[2,32,2,640]{3,2,1,0:T(2,128)S(1)} %copy-done.2, f32[2,32,2,640]{3,2,1,0:T(2,128)S(1)} %reshape.38, f32[2,32,2,640]{3,2,1,0:T(2,128)S(1)} %reshape.37, f32[2,2,640]{2,1,0:T(2,128)S(1)} %copy-done.4), kind=kLoop, calls=%fused_computation.11 | loop fusion | flops 1638400 | bytes 1648640 | tf_op jit(solution)/shard_map/add | solution.py:452
  33.5 0.3 reshape.40
  33.8 0.3 copy.19
  34.0 0.3 reshape.41
  34.3 0.0 copy-start.7
  34.3 0.7 copy-done.7
  35.0 0.1 copy.15
  35.1 0.1 broadcast_in_dim.10
  35.2 0.1 pad.7.clone
  35.2 0.0 copy-start.8
  35.2 0.0 copy-start.9
  35.2 0.8 %maximum_maximum_fusion.ext_ref = f32[32,24,128]{2,1,0:T(8,128)} fusion(f32[32,2,128]{2,1,0:T(2,128)S(1)} %broadcast_in_dim.10, f32[32,20,128]{2,1,0:T(8,128)S(1)} %reshape.41, f32[24]{0:T(128)S(1)} %pad.7.clone), kind=kLoop, calls=%fused_computation.2 | loop fusion | flops 196608 | bytes 753760 | tf_op jit(solution)/shard_map/concatenate | solution.py:292
  36.1 0.0 copy-done.8
  36.1 0.0 copy-done.9
  36.1 0.7 multiply_reduce_fusion.1
  36.8 2.5 %pad_maximum_fusion.2.w_ref = f32[3]{0:T(128)} fusion(f32[1]{0:T(128)} %bitcast.2, f32[1]{0:T(128)} %bitcast.1, f32[1]{0:T(128)} %bitcast), kind=kLoop, calls=%fused_computation.25 | loop fusion | flops 6 | bytes 24 | tf_op jit(solution)/shard_map/stack | solution.py:453
  39.3 37.4 %shard_map.83 = f32[32,40,128]{2,1,0:T(8,128)} custom-call(f32[3]{0:T(128)} %pad_maximum_fusion.2.w_ref, f32[32,24,128]{2,1,0:T(8,128)} %maximum_maximum_fusion.ext_ref, f32[32,20,128]{2,1,0:T(8,128)} %get-tuple-element.12.probe_ref), custom_call_target="tpu_custom_call" | custom-call | tf_op jit(solution)/shard_map/pallas_call | solution.py:294
  76.7 1.4 %reshape.42 = f32[32,2,2,1280]{3,2,1,0:T(2,128)S(1)} reshape(f32[32,40,128]{2,1,0:T(8,128)} %shard_map.83) | data formatting | bytes 1310720 | tf_op jit(solution)/shard_map/reshape | solution.py:309
  78.2 0.8 reshape.44
  78.9 0.9 %copy.17 = f32[2,2,32,2,640]{4,3,2,1,0:T(2,128)} copy(f32[2,2,32,2,640]{4,3,0,1,2:T(2,128)S(1)} %reshape.44) | data formatting | bytes 1310720 | tf_op jit(solution)/shard_map/reshape | solution.py:461
  (1 shorter events, 0.0 us)
Async XLA Ops:
  0.0 3.2 %copy-start = (bf16[2,64,1280]{2,1,0:T(8,128)(2,1)S(1)}, bf16[2,64,1280]{2,1,0:T(8,128)(2,1)}, u32[]{:S(2)}) copy-start(bf16[2,64,1280]{2,1,0:T(8,128)(2,1)} %param.10) | copy-start | bytes 983044
  1.3 0.7 copy-start.1
  2.0 1.0 %copy-start.2 = (f32[2,32,2,640]{3,2,1,0:T(2,128)S(1)}, f32[2,32,2,640]{3,2,1,0:T(2,128)}, u32[]{:S(2)}) copy-start(f32[2,32,2,640]{3,2,1,0:T(2,128)} %param.8) | copy-start | bytes 983044
  3.3 0.7 copy-start.5
  30.0 0.8 %copy-start.3 = (f32[2,32,256]{2,1,0:T(8,128)S(1)}, f32[2,32,256]{2,1,0:T(8,128)}, u32[]{:S(2)}) copy-start(f32[2,32,256]{2,1,0:T(8,128)} %get-tuple-element.11) | copy-start | bytes 196612
  30.0 0.8 %copy-start.6 = (f32[2,256]{1,0:T(2,128)S(1)}, f32[2,256]{1,0:T(2,128)}, u32[]{:S(2)}) copy-start(f32[2,256]{1,0:T(2,128)} %param.12) | copy-start | bytes 6148
  31.2 0.7 copy-start.4
  34.3 0.7 copy-start.7
  35.2 0.8 %copy-start.8 = (f32[4]{0:T(128)S(1)}, f32[4]{0:T(128)}, u32[]{:S(2)}) copy-start(f32[4]{0:T(128)} %param.15) | copy-start | bytes 52
  35.2 0.8 %copy-start.9 = (f32[4]{0:T(128)S(1)}, f32[4]{0:T(128)}, u32[]{:S(2)}) copy-start(f32[4]{0:T(128)} %param.14) | copy-start | bytes 52

commit v10 on v9

--- a/solution.py
+++ b/solution.py
@@ -194,9 +194,9 @@
 
     lax.fori_loop(1, count, arrived, 0)
 
-    rows_per_layer = out_ref.shape[1] // layers
-    half = rows_per_layer // 2
-    zero = jnp.zeros((rows_per_layer, out_ref.shape[2]), jnp.float32)
+    half = out_ref.shape[3]
+    rows_per_layer = 2 * half
+    zero = jnp.zeros((half, out_ref.shape[4]), jnp.float32)
     data_rows = layers * half
     total = count * layers
     w0, w1, w2 = w_ref[0], w_ref[1], w_ref[2]
@@ -219,8 +219,8 @@
                 + CENTER * here
             )
             hamil = partial - 0.5 * second
-            swept[source, pl.ds(layer * rows_per_layer, half), :] = w0 * hamil - w1 * here
-            swept[source, pl.ds(layer * rows_per_layer + half, half), :] = w1 * hamil - w2 * here
+            swept[source, 0, layer] = w0 * hamil - w1 * here
+            swept[source, 1, layer] = w1 * hamil - w2 * here
         return carry
 
     lax.fori_loop(0, count, prepare, 0)
@@ -228,29 +228,33 @@
     def forward(source, state):
         for layer in range(layers):
             rate = gathered[source, pl.ds(data_rows + layer, 1), :]
-            slab = swept[source, pl.ds(layer * rows_per_layer, rows_per_layer), :]
-            state = rate * state + (1.0 - rate) * slab
-            swept[source, pl.ds(layer * rows_per_layer, rows_per_layer), :] = state
+            state = tuple(
+                rate * state[m] + (1.0 - rate) * swept[source, m, layer] for m in range(2)
+            )
+            for m in range(2):
+                swept[source, m, layer] = state[m]
         return state
 
-    lax.fori_loop(0, count, forward, zero)
+    lax.fori_loop(0, count, forward, (zero, zero))
 
     def backward(step, state):
         source = count - 1 - step
         for layer in reversed(range(layers)):
             rate = gathered[source, pl.ds(data_rows + layer, 1), :]
-            piece = pl.ds(layer * rows_per_layer, rows_per_layer)
-            state = rate * state + (1.0 - rate) * swept[source, piece, :]
-            swept[source, piece, :] = state
+            state = tuple(
+                rate * state[m] + (1.0 - rate) * swept[source, m, layer] for m in range(2)
+            )
+            for m in range(2):
+                swept[source, m, layer] = state[m]
         return state
 
-    lax.fori_loop(0, count, backward, zero)
+    lax.fori_loop(0, count, backward, (zero, zero))
 
     def returning(step, carry):
         target = lax.rem(me + step, count)
         pltpu.make_async_remote_copy(
             src_ref=swept.at[target],
-            dst_ref=out_ref.at[me],
+            dst_ref=out_ref.at[:, :, me],
             send_sem=back_send.at[step],
             recv_sem=back_recv.at[step],
             device_id=(target, row),
@@ -259,12 +263,12 @@
         return carry
 
     lax.fori_loop(1, count, returning, 0)
-    out_ref[me] = swept[me]
+    out_ref[:, :, me] = swept[me]
 
     def returned(step, carry):
         copy = pltpu.make_async_remote_copy(
             src_ref=swept.at[me],
-            dst_ref=out_ref.at[lax.rem(me + count - step, count)],
+            dst_ref=out_ref.at[:, :, lax.rem(me + count - step, count)],
             send_sem=back_send.at[step],
             recv_sem=back_recv.at[step],
             device_id=(lax.rem(me + step, count), row),
@@ -293,12 +297,12 @@
     vmem = pl.BlockSpec(memory_space=pltpu.VMEM)
     out = pl.pallas_call(
         functools.partial(exchange_kernel, count, layers),
-        out_shape=jax.ShapeDtypeStruct((columns, moments * data_rows, 128), jnp.float32),
+        out_shape=jax.ShapeDtypeStruct((moments, layers, columns, tiles, 128), jnp.float32),
         in_specs=[pl.BlockSpec(memory_space=pltpu.SMEM), vmem, vmem],
         out_specs=vmem,
         scratch_shapes=[
             pltpu.VMEM((count, padded_rows, 128), jnp.float32),
-            pltpu.VMEM((count, moments * data_rows, 128), jnp.float32),
+            pltpu.VMEM((count, moments, layers, tiles, 128), jnp.float32),
             pltpu.SemaphoreType.DMA((count,)),
             pltpu.SemaphoreType.DMA((count,)),
             pltpu.SemaphoreType.DMA((count,)),
@@ -306,7 +310,7 @@
         ],
         compiler_params=pltpu.CompilerParams(collective_id=0, has_side_effects=True),
     )(weights, ext, gathered_probes)
-    return jnp.transpose(out.reshape(columns, layers, moments, width), (1, 2, 0, 3))
+    return out.reshape(moments, layers, columns, width)
 
 
 def front_kernel(row_count, layer_count, block_ref, coef_ref, pieces_ref, left, right, total, regrouped,
@@ -458,7 +462,7 @@
         ]
     )
     swept = sweeps(partial.reshape(layers, columns, rows * depth), regrouped, decay_rates, weights)
-    return jnp.swapaxes(swept, 0, 1).reshape(2, layers, columns, rows, depth)
+    return swept.reshape(2, layers, columns, rows, depth)
 
 
 def solution(mesh):

time: 80.3 us -> 79.8 us (level)
    reshape x3 -> x0, local copies, waits for them, and re-layouts: 3.1 us -> none  [the longest x2 1.67 us: shards(): return jnp.swapaxes(swept, 0, 1).reshape(2, layers, columns, rows, depth)]
    another operation x0 -> x1, local copies, waits for them, and re-layouts: none -> 2.46 us  [shards(): return swept.reshape(2, layers, columns, rows, depth)]
where the time goes in v10:
time: 79.8 us; the launch traced here: 79.3 us
  Pallas kernels  61.5 us (77%)
  local copies, waits for them, and re-layouts  9.44 us (12%)
  other arithmetic  6.73 us (8%)
  matrix products  1.44 us (2%)
    pallas_call x1, Pallas kernels, sweeps(): pl.pallas_call(functools.partial(exchange_kernel, count, layers), out_sha...  37.6 us
    pallas_call x1, Pallas kernels, front_exchange(): pl.pallas_call(functools.partial(front_kernel, row_count, layer_count), o...  24 us
    unnamed x20, local copies, waits for them, and re-layouts  2.77 us
    another operation x1, other arithmetic, shards(): jnp.stack([jnp.sum(node_weights), jnp.sum(node_weights * contour_nodes),...  2.48 us
    another operation x1, local copies, waits for them, and re-layouts, shards(): return swept.reshape(2, layers, columns, rows, depth)  2.46 us

profile of v10, /device:TPU:32, one launch (start us, length us, event | category | flops | bytes accessed | tf_op | source)
XLA Modules:
  0.0 79.3 jit_solution(5509119992167044378)
XLA Ops:
  0.0 0.0 copy-start
  0.0 1.3 %reshape.28.block_ref = f32[2,32,1280]{2,1,0:T(8,128)S(1)} reshape(f32[2,32,2,640]{3,2,1,0:T(2,128)} %param.8) | data formatting | bytes 655360 | tf_op jit(solution)/shard_map/reshape | solution.py:439
  1.3 0.0 copy-start.1
  1.3 0.3 copy.12
  1.6 0.4 copy-done.1
  2.0 0.0 copy-start.2
  2.0 1.0 %reshape.30.pieces_ref = f32[32,20,128]{2,1,0:T(8,128)} reshape(f32[32,2,1280]{2,1,0:T(2,128)S(1)} %copy.12) | data formatting | bytes 655360 | tf_op jit(solution)/shard_map/reshape | solution.py:401
  3.0 0.0 copy-done.2
  3.0 0.1 convert_element_type.18
  3.1 0.1 reshape.29
  3.2 0.0 copy-done
  3.3 0.0 copy-start.5
  3.3 0.2 fusion.14
  3.5 0.5 copy-done.5
  3.9 0.9 %fusion.8.coef_ref = f32[2,32,256]{2,1,0:T(8,128)} fusion(f32[2,64,32]{1,2,0:T(8,128)S(1)} %fusion.14, s32[2,64]{1,0:T(2,128)S(1)} %copy-done.5), kind=kOutput, calls=%fused_computation.20 | convolution fusion | flops 12615680 | bytes 82432 | tf_op jit(solution)/shard_map/lsq,lsc->lcq/dot_general | solution.py:437
  4.8 24.0 %shard_map.82 = (f32[2,32,1280]{2,1,0:T(8,128)}, f32[2,32,1280]{2,1,0:T(8,128)}, f32[2,32,256]{2,1,0:T(8,128)}, f32[32,20,128]{2,1,0:T(8,128)}) custom-call(f32[2,32,1280]{2,1,0:T(8,128)} %copy-done.1, f32[2,32,256]{2,1,0:T(8,128)} %fusion.8.coef_ref, f32[32,20,128]{2,1,0:T(8,128)} %reshape.30.pieces_ref), custom_call_target="tpu_custom_call" | custom-call | tf_op jit(solution)/shard_map/pallas_call | solution.py:403
  28.8 1.0 %broadcast_select_fusion = (f32[2,32,1280]{2,1,0:T(8,128)S(1)}, f32[2,32,1280]{2,1,0:T(8,128)S(1)}) fusion(f32[2,32,1280]{2,1,0:T(8,128)} %get-tuple-element.10, pred[]{:T(512)S(6)} %lt.3, f32[2,32,1280]{2,1,0:T(8,128)} %get-tuple-element.9, pred[]{:T(512)S(6)} %gt.3), kind=kLoop, calls=%fused_computation.16 | loop fusion | flops 163840 | bytes 1310722 | tf_op jit(solution)/shard_map/jit(_where)/select_n | solution.py:443
  29.8 0.2 reshape.31
  30.0 0.0 copy-start.3
  30.0 0.0 copy-start.6
  30.0 0.2 reshape.32
  30.2 0.6 copy-done.3
  30.9 0.0 copy-done.6
  30.9 0.4 fusion
  31.2 0.0 copy-start.4
  31.2 0.2 reshape.33
  31.4 0.5 copy-done.4
  31.9 1.6 %add_add_fusion = f32[2,32,2,640]{3,2,1,0:T(2,128)S(1)} fusion(f32[2,32,2,640]{3,2,1,0:T(2,128)S(1)} %reshape.33, f32[2,32,2,640]{3,2,1,0:T(2,128)S(1)} %copy-done.2, f32[2,32,2,640]{3,2,1,0:T(2,128)S(1)} %reshape.32, f32[2,32,2,640]{3,2,1,0:T(2,128)S(1)} %reshape.31, f32[2,2,640]{2,1,0:T(2,128)S(1)} %copy-done.4), kind=kLoop, calls=%fused_computation.11 | loop fusion | flops 1638400 | bytes 1648640 | tf_op jit(solution)/shard_map/add | solution.py:456
  33.5 0.3 reshape.34
  33.8 0.3 copy.16
  34.1 0.3 reshape.35
  34.3 0.0 copy-start.7
  34.3 0.7 copy-done.7
  35.0 0.1 copy.14
  35.1 0.1 broadcast_in_dim.10
  35.2 0.1 pad.7.clone
  35.3 0.0 copy-start.8
  35.3 0.0 copy-start.9
  35.3 0.8 %maximum_maximum_fusion.ext_ref = f32[32,24,128]{2,1,0:T(8,128)} fusion(f32[32,2,128]{2,1,0:T(2,128)S(1)} %broadcast_in_dim.10, f32[32,20,128]{2,1,0:T(8,128)S(1)} %reshape.35, f32[24]{0:T(128)S(1)} %pad.7.clone), kind=kLoop, calls=%fused_computation.2 | loop fusion | flops 196608 | bytes 753760 | tf_op jit(solution)/shard_map/concatenate | solution.py:296
  36.1 0.0 copy-done.8
  36.1 0.0 copy-done.9
  36.1 0.7 multiply_reduce_fusion.1
  36.8 2.5 %pad_maximum_fusion.2.w_ref = f32[3]{0:T(128)} fusion(f32[1]{0:T(128)} %bitcast.2, f32[1]{0:T(128)} %bitcast.1, f32[1]{0:T(128)} %bitcast), kind=kLoop, calls=%fused_computation.25 | loop fusion | flops 6 | bytes 24 | tf_op jit(solution)/shard_map/stack | solution.py:457
  39.3 37.6 %shard_map.83 = f32[2,2,32,10,128]{4,3,2,1,0:T(8,128)} custom-call(f32[3]{0:T(128)} %pad_maximum_fusion.2.w_ref, f32[32,24,128]{2,1,0:T(8,128)} %maximum_maximum_fusion.ext_ref, f32[32,20,128]{2,1,0:T(8,128)} %get-tuple-element.12.probe_ref), custom_call_target="tpu_custom_call" | custom-call | tf_op jit(solution)/shard_map/pallas_call | solution.py:298
  76.9 2.5 %reshape_reshape.3 = f32[2,2,32,2,640]{4,3,2,1,0:T(2,128)} reshape(f32[2,2,32,10,128]{4,3,2,1,0:T(8,128)} %shard_map.83) | data formatting | bytes 1310720 | tf_op jit(solution)/shard_map/reshape;reshape | solution.py:465
  (1 shorter events, 0.0 us)
Async XLA Ops:
  0.0 3.2 %copy-start = (bf16[2,64,1280]{2,1,0:T(8,128)(2,1)S(1)}, bf16[2,64,1280]{2,1,0:T(8,128)(2,1)}, u32[]{:S(2)}) copy-start(bf16[2,64,1280]{2,1,0:T(8,128)(2,1)} %param.10) | copy-start | bytes 983044
  1.3 0.7 copy-start.1
  2.0 1.0 %copy-start.2 = (f32[2,32,2,640]{3,2,1,0:T(2,128)S(1)}, f32[2,32,2,640]{3,2,1,0:T(2,128)}, u32[]{:S(2)}) copy-start(f32[2,32,2,640]{3,2,1,0:T(2,128)} %param.8) | copy-start | bytes 983044
  3.3 0.7 copy-start.5
  30.0 0.8 %copy-start.3 = (f32[2,32,256]{2,1,0:T(8,128)S(1)}, f32[2,32,256]{2,1,0:T(8,128)}, u32[]{:S(2)}) copy-start(f32[2,32,256]{2,1,0:T(8,128)} %get-tuple-element.11) | copy-start | bytes 196612
  30.0 0.8 %copy-start.6 = (f32[2,256]{1,0:T(2,128)S(1)}, f32[2,256]{1,0:T(2,128)}, u32[]{:S(2)}) copy-start(f32[2,256]{1,0:T(2,128)} %param.12) | copy-start | bytes 6148
  31.2 0.7 copy-start.4
  34.3 0.7 copy-start.7
  35.3 0.8 %copy-start.8 = (f32[4]{0:T(128)S(1)}, f32[4]{0:T(128)}, u32[]{:S(2)}) copy-start(f32[4]{0:T(128)} %param.15) | copy-start | bytes 52
  35.3 0.8 %copy-start.9 = (f32[4]{0:T(128)S(1)}, f32[4]{0:T(128)}, u32[]{:S(2)}) copy-start(f32[4]{0:T(128)} %param.14) | copy-start | bytes 52

commit v11 on v10

--- a/solution.py
+++ b/solution.py
@@ -149,7 +149,7 @@
         o_ref[:, index] = back[index] + upper[None] * from_above
 
 
-def exchange_kernel(count, layer_count, w_ref, ext_ref, probe_ref, out_ref, gathered, swept, send_sem, recv_sem, back_send, back_recv):
+def exchange_kernel(count, layer_count, nodes_ref, weights_ref, ext_ref, probe_ref, out_ref, gathered, swept, send_sem, recv_sem, back_send, back_recv):
     me = lax.axis_index("layer")
     row = lax.axis_index("xs")
     layers = layer_count
@@ -199,7 +199,14 @@
     zero = jnp.zeros((half, out_ref.shape[4]), jnp.float32)
     data_rows = layers * half
     total = count * layers
-    w0, w1, w2 = w_ref[0], w_ref[1], w_ref[2]
+    w0 = w1 = w2 = None
+    for node in range(nodes_ref.shape[0]):
+        weight = weights_ref[node]
+        scaled = weight * nodes_ref[node]
+        if w0 is None:
+            w0, w1, w2 = weight, scaled, scaled * nodes_ref[node]
+        else:
+            w0, w1, w2 = w0 + weight, w1 + scaled, w2 + scaled * nodes_ref[node]
 
     def probe_at(place):
         inside = ((place >= 0) & (place < total)).astype(jnp.float32)
@@ -281,7 +288,7 @@
     lax.fori_loop(1, count, returned, 0)
 
 
-def sweeps(partial, gathered_probes, decay_rates, weights):
+def sweeps(partial, gathered_probes, decay_rates, nodes, weights):
     layers, columns, width = partial.shape
     moments = 2
     count = lax.axis_size("layer")
@@ -298,7 +305,7 @@
     out = pl.pallas_call(
         functools.partial(exchange_kernel, count, layers),
         out_shape=jax.ShapeDtypeStruct((moments, layers, columns, tiles, 128), jnp.float32),
-        in_specs=[pl.BlockSpec(memory_space=pltpu.SMEM), vmem, vmem],
+        in_specs=[pl.BlockSpec(memory_space=pltpu.SMEM)] * 2 + [vmem, vmem],
         out_specs=vmem,
         scratch_shapes=[
             pltpu.VMEM((count, padded_rows, 128), jnp.float32),
@@ -309,7 +316,7 @@
             pltpu.SemaphoreType.DMA((count,)),
         ],
         compiler_params=pltpu.CompilerParams(collective_id=0, has_side_effects=True),
-    )(weights, ext, gathered_probes)
+    )(nodes, weights, ext, gathered_probes)
     return out.reshape(moments, layers, columns, width)
 
 
@@ -377,6 +384,8 @@
     total[...] = acc
     for copy in copies[:2]:
         copy.wait()
+    left[...] = left[...] * (row > 0).astype(jnp.float32)
+    right[...] = right[...] * (row < row_count - 1).astype(jnp.float32)
 
     def arrived(step, carry):
         copy = pltpu.make_async_remote_copy(
@@ -438,9 +447,8 @@
     left, right, coef, regrouped = front_exchange(
         probes.reshape(layers, columns, rows * depth), partial_coef
     )
-    row = lax.axis_index("xs")
-    left = jnp.where(row > 0, left, 0.0).reshape(probes.shape)
-    right = jnp.where(row < lax.axis_size("xs") - 1, right, 0.0).reshape(probes.shape)
+    left = left.reshape(probes.shape)
+    right = right.reshape(probes.shape)
     beside = jnp.concatenate([left, probes, right], axis=2)
     across = jnp.pad(probes, ((0, 0), (0, 0), (0, 0), (2, 2)))
     laplace = second_along(beside, 2, rows)
@@ -454,14 +462,10 @@
         "lsp,lsc->lcp", projector, slot_back, preferred_element_type=jnp.float32
     ).reshape(layers, columns, rows, depth)
     partial = -0.5 * laplace + potential[:, None] * probes + projected
-    weights = jnp.stack(
-        [
-            jnp.sum(node_weights),
-            jnp.sum(node_weights * contour_nodes),
-            jnp.sum(node_weights * contour_nodes * contour_nodes),
-        ]
+    swept = sweeps(
+        partial.reshape(layers, columns, rows * depth), regrouped, decay_rates, contour_nodes,
+        node_weights,
     )
-    swept = sweeps(partial.reshape(layers, columns, rows * depth), regrouped, decay_rates, weights)
     return swept.reshape(2, layers, columns, rows, depth)
 
 

time: 79.8 us -> 77.3 us (0.969)
  other arithmetic: 6.73 us -> 2.54 us
  local copies, waits for them, and re-layouts: 9.44 us -> 10.4 us
  matrix products: 1.44 us -> 2.27 us
    another operation x1 -> x0, other arithmetic: 2.48 us -> none  [shards(): jnp.stack([jnp.sum(node_weights), jnp.sum(node_weights * contour_nodes),...]
    select_n x1 -> x0, other arithmetic: 1.03 us -> none  [shards(): jnp.where(row < lax.axis_size('xs') - 1, right, 0.0).reshape(probes.shape)]
    unnamed x20 -> x18, local copies, waits for them, and re-layouts: 2.77 us -> 3.71 us
    dot_general x1, matrix products: 0.37 us -> 1.21 us  [shards(): jnp.einsum('lsp,lsc->lcp', projector, slot_back, preferred_element_type=j...]
where the time goes in v11:
time: 77.3 us; the launch traced here: 76.8 us
  Pallas kernels  61.5 us (80%)
  local copies, waits for them, and re-layouts  10.4 us (13%)
  other arithmetic  2.54 us (3%)
  matrix products  2.27 us (3%)
    pallas_call x1, Pallas kernels, sweeps(): pl.pallas_call(functools.partial(exchange_kernel, count, layers), out_sha...  37.4 us
    pallas_call x1, Pallas kernels, front_exchange(): pl.pallas_call(functools.partial(front_kernel, row_count, layer_count), o...  24 us
    unnamed x18, local copies, waits for them, and re-layouts  3.71 us
    another operation x1, local copies, waits for them, and re-layouts, shards(): return swept.reshape(2, layers, columns, rows, depth)  2.46 us
    add x1, other arithmetic, shards(): partial = -0.5 * laplace + potential[:, None] * probes + projected  1.58 us

profile of v11, /device:TPU:32, one launch (start us, length us, event | category | flops | bytes accessed | tf_op | source)
XLA Modules:
  0.0 76.8 jit_solution(15636903215430947178)
XLA Ops:
  0.0 0.0 copy-start
  0.0 1.3 %reshape.28.block_ref = f32[2,32,1280]{2,1,0:T(8,128)S(1)} reshape(f32[2,32,2,640]{3,2,1,0:T(2,128)} %param.8) | data formatting | bytes 655360 | tf_op jit(solution)/shard_map/reshape | solution.py:448
  1.3 0.0 copy-start.1
  1.3 0.3 copy.12
  1.6 0.4 copy-done.1
  2.0 0.0 copy-start.2
  2.0 1.0 %reshape.30.pieces_ref = f32[32,20,128]{2,1,0:T(8,128)} reshape(f32[32,2,1280]{2,1,0:T(2,128)S(1)} %copy.12) | data formatting | bytes 655360 | tf_op jit(solution)/shard_map/reshape | solution.py:410
  3.0 0.0 copy-done.2
  3.0 0.1 convert_element_type.18
  3.1 0.1 reshape.29
  3.3 0.0 copy-done
  3.3 0.0 copy-start.6
  3.3 0.2 fusion.14
  3.5 0.5 copy-done.6
  3.9 0.9 %fusion.8.coef_ref = f32[2,32,256]{2,1,0:T(8,128)} fusion(f32[2,64,32]{1,2,0:T(8,128)S(1)} %fusion.14, s32[2,64]{1,0:T(2,128)S(1)} %copy-done.6), kind=kOutput, calls=%fused_computation.18 | convolution fusion | flops 12615680 | bytes 82432 | tf_op jit(solution)/shard_map/lsq,lsc->lcq/dot_general | solution.py:446
  4.8 0.0 copy-start.7
  4.8 24.0 %shard_map.82 = (f32[2,32,1280]{2,1,0:T(8,128)}, f32[2,32,1280]{2,1,0:T(8,128)}, f32[2,32,256]{2,1,0:T(8,128)}, f32[32,20,128]{2,1,0:T(8,128)}) custom-call(f32[2,32,1280]{2,1,0:T(8,128)} %copy-done.1, f32[2,32,256]{2,1,0:T(8,128)} %fusion.8.coef_ref, f32[32,20,128]{2,1,0:T(8,128)} %reshape.30.pieces_ref), custom_call_target="tpu_custom_call" | custom-call | tf_op jit(solution)/shard_map/pallas_call | solution.py:412
  28.8 0.0 copy-done.7
  28.8 1.2 %fusion = f32[2,32,1280]{2,1,0:T(8,128)S(1)} fusion(bf16[2,64,1280]{2,1,0:T(8,128)(2,1)S(1)} %copy-done, s32[2,64]{1,0:T(2,128)S(1)} %copy-done.6, f32[2,32,256]{2,1,0:T(8,128)} %get-tuple-element.11, f32[2,256]{1,0:T(2,128)S(1)} %copy-done.7), kind=kOutput, calls=%fused_computation.1 | convolution fusion | flops 12718080 | bytes 723456 | tf_op jit(solution)/shard_map/lsp,lsc->lcp/dot_general | solution.py:461
  30.0 0.0 copy-start.4
  30.1 0.2 reshape.33
  30.2 0.8 %copy-done.4 = f32[2,32,1280]{2,1,0:T(8,128)S(1)} copy-done((f32[2,32,1280]{2,1,0:T(8,128)S(1)}, f32[2,32,1280]{2,1,0:T(8,128)}, u32[]{:S(2)}) %copy-start.4) | copy-done | bytes 327704
  31.0 0.0 copy-start.3
  31.0 0.2 reshape.31
  31.2 0.8 %copy-done.3 = f32[2,32,1280]{2,1,0:T(8,128)S(1)} copy-done((f32[2,32,1280]{2,1,0:T(8,128)S(1)}, f32[2,32,1280]{2,1,0:T(8,128)}, u32[]{:S(2)}) %copy-start.3) | copy-done | bytes 327704
  32.0 0.0 copy-start.5
  32.0 0.2 reshape.32
  32.2 0.5 copy-done.5
  32.7 1.6 %add_add_fusion = f32[2,32,2,640]{3,2,1,0:T(2,128)S(1)} fusion(f32[2,32,2,640]{3,2,1,0:T(2,128)S(1)} %reshape.33, f32[2,32,2,640]{3,2,1,0:T(2,128)S(1)} %copy-done.2, f32[2,32,2,640]{3,2,1,0:T(2,128)S(1)} %reshape.32, f32[2,32,2,640]{3,2,1,0:T(2,128)S(1)} %reshape.31, f32[2,2,640]{2,1,0:T(2,128)S(1)} %copy-done.5), kind=kLoop, calls=%fused_computation.11 | loop fusion | flops 1638400 | bytes 1648640 | tf_op jit(solution)/shard_map/add | solution.py:464
  34.3 0.3 reshape.34
  34.6 0.3 copy.16
  34.8 0.3 reshape.35
  35.1 0.0 copy-start.8
  35.1 0.7 copy-done.8
  35.8 0.1 copy.14
  35.9 0.1 broadcast_in_dim.4
  36.0 0.1 pad.7.clone
  36.0 0.8 %maximum_maximum_fusion.ext_ref = f32[32,24,128]{2,1,0:T(8,128)} fusion(f32[32,2,128]{2,1,0:T(2,128)S(1)} %broadcast_in_dim.4, f32[32,20,128]{2,1,0:T(8,128)S(1)} %reshape.35, f32[24]{0:T(128)S(1)} %pad.7.clone), kind=kLoop, calls=%fused_computation.2 | loop fusion | flops 196608 | bytes 753760 | tf_op jit(solution)/shard_map/concatenate | solution.py:303
  36.9 37.4 %shard_map.83 = f32[2,2,32,10,128]{4,3,2,1,0:T(8,128)} custom-call(f32[4]{0:T(128)} %nodes_ref.1, f32[4]{0:T(128)} %weights_ref.1, f32[32,24,128]{2,1,0:T(8,128)} %maximum_maximum_fusion.ext_ref, f32[32,20,128]{2,1,0:T(8,128)} %get-tuple-element.12.probe_ref), custom_call_target="tpu_custom_call" | custom-call | tf_op jit(solution)/shard_map/pallas_call | solution.py:305
  74.3 2.5 %reshape_reshape.3 = f32[2,2,32,2,640]{4,3,2,1,0:T(2,128)} reshape(f32[2,2,32,10,128]{4,3,2,1,0:T(8,128)} %shard_map.83) | data formatting | bytes 1310720 | tf_op jit(solution)/shard_map/reshape;reshape | solution.py:469
  (1 shorter events, 0.0 us)
Async XLA Ops:
  0.0 3.3 %copy-start = (bf16[2,64,1280]{2,1,0:T(8,128)(2,1)S(1)}, bf16[2,64,1280]{2,1,0:T(8,128)(2,1)}, u32[]{:S(2)}) copy-start(bf16[2,64,1280]{2,1,0:T(8,128)(2,1)} %param.10) | copy-start | bytes 983044
  1.3 0.7 copy-start.1
  2.0 1.0 %copy-start.2 = (f32[2,32,2,640]{3,2,1,0:T(2,128)S(1)}, f32[2,32,2,640]{3,2,1,0:T(2,128)}, u32[]{:S(2)}) copy-start(f32[2,32,2,640]{3,2,1,0:T(2,128)} %param.8) | copy-start | bytes 983044
  3.3 0.7 copy-start.6
  4.8 24.0 %copy-start.7 = (f32[2,256]{1,0:T(2,128)S(1)}, f32[2,256]{1,0:T(2,128)}, u32[]{:S(2)}) copy-start(f32[2,256]{1,0:T(2,128)} %param.12) | copy-start | bytes 6148
  30.0 1.0 %copy-start.4 = (f32[2,32,1280]{2,1,0:T(8,128)S(1)}, f32[2,32,1280]{2,1,0:T(8,128)}, u32[]{:S(2)}) copy-start(f32[2,32,1280]{2,1,0:T(8,128)} %get-tuple-element.9) | copy-start | bytes 983044
  31.0 1.0 %copy-start.3 = (f32[2,32,1280]{2,1,0:T(8,128)S(1)}, f32[2,32,1280]{2,1,0:T(8,128)}, u32[]{:S(2)}) copy-start(f32[2,32,1280]{2,1,0:T(8,128)} %get-tuple-element.10) | copy-start | bytes 983044
  32.0 0.7 copy-start.5
  35.1 0.7 copy-start.8

commit v12 on v11

--- a/solution.py
+++ b/solution.py
@@ -320,8 +320,8 @@
     return out.reshape(moments, layers, columns, width)
 
 
-def front_kernel(row_count, layer_count, block_ref, coef_ref, pieces_ref, left, right, total, regrouped,
-                 gathered, send_sem, recv_sem, piece_send, piece_recv):
+def front_kernel(row_count, layer_count, depth, block_ref, coef_ref, pieces_ref, across, total, regrouped,
+                 left, right, gathered, send_sem, recv_sem, piece_send, piece_recv):
     me = lax.axis_index("layer")
     row = lax.axis_index("xs")
     peers = row_count - 1
@@ -384,8 +384,20 @@
     total[...] = acc
     for copy in copies[:2]:
         copy.wait()
-    left[...] = left[...] * (row > 0).astype(jnp.float32)
-    right[...] = right[...] * (row < row_count - 1).astype(jnp.float32)
+    before = left[...] * (row > 0).astype(jnp.float32)
+    after = right[...] * (row < row_count - 1).astype(jnp.float32)
+    mine = block_ref[...]
+    first, second = slice(0, depth), slice(depth, 2 * depth)
+    across[:, :, first] = (
+        FAR * (before[:, :, first] + after[:, :, first])
+        + NEAR * (before[:, :, second] + mine[:, :, second])
+        + CENTER * mine[:, :, first]
+    )
+    across[:, :, second] = (
+        FAR * (before[:, :, second] + after[:, :, second])
+        + NEAR * (mine[:, :, first] + after[:, :, first])
+        + CENTER * mine[:, :, second]
+    )
 
     def arrived(step, carry):
         copy = pltpu.make_async_remote_copy(
@@ -403,20 +415,22 @@
     lax.fori_loop(1, layer_count, arrived, 0)
 
 
-def front_exchange(block, coef):
+def front_exchange(block, coef, depth):
     row_count = lax.axis_size("xs")
     layer_count = lax.axis_size("layer")
     layers, columns, width = block.shape
     pieces = jnp.transpose(block, (1, 0, 2)).reshape(columns, layers * width // 128, 128)
     spec = pl.BlockSpec(memory_space=pltpu.VMEM)
     return pl.pallas_call(
-        functools.partial(front_kernel, row_count, layer_count),
-        out_shape=[jax.ShapeDtypeStruct(block.shape, jnp.float32)] * 2
+        functools.partial(front_kernel, row_count, layer_count, depth),
+        out_shape=[jax.ShapeDtypeStruct(block.shape, jnp.float32)]
         + [jax.ShapeDtypeStruct(coef.shape, jnp.float32),
            jax.ShapeDtypeStruct((layer_count,) + pieces.shape[1:], jnp.float32)],
         in_specs=[spec, spec, spec],
-        out_specs=[spec] * 4,
+        out_specs=[spec] * 3,
         scratch_shapes=[
+            pltpu.VMEM(block.shape, jnp.float32),
+            pltpu.VMEM(block.shape, jnp.float32),
             pltpu.VMEM((row_count - 1,) + coef.shape, jnp.float32),
             pltpu.SemaphoreType.DMA((1 + row_count,)),
             pltpu.SemaphoreType.DMA((1 + row_count,)),
@@ -444,15 +458,13 @@
         jnp.float32
     )
     partial_coef = jnp.einsum("lsq,lsc->lcq", onehot, slot_coef, precision=lax.Precision.HIGHEST)
-    left, right, coef, regrouped = front_exchange(
-        probes.reshape(layers, columns, rows * depth), partial_coef
-    )
-    left = left.reshape(probes.shape)
-    right = right.reshape(probes.shape)
-    beside = jnp.concatenate([left, probes, right], axis=2)
+    if rows != 2:
+        raise ValueError("rows")
+    along_rows, coef, regrouped = front_exchange(
+        probes.reshape(layers, columns, rows * depth), partial_coef, depth
+    )
     across = jnp.pad(probes, ((0, 0), (0, 0), (0, 0), (2, 2)))
-    laplace = second_along(beside, 2, rows)
-    laplace = laplace + second_along(across, 3, depth)
+    laplace = along_rows.reshape(probes.shape) + second_along(across, 3, depth)
     coef = jnp.swapaxes(coef, 1, 2)
     scaled = (strength[:, :, None] * coef).astype(jnp.bfloat16)
     slot_back = jnp.einsum(

time: 77.3 us -> 75.3 us (0.974)
  local copies, waits for them, and re-layouts: 10.4 us -> 8.57 us
  matrix products: 2.27 us -> 1.44 us
  other arithmetic: 2.54 us -> 3.35 us
    unnamed x18 -> x16, local copies, waits for them, and re-layouts: 3.71 us -> 2.1 us
    reshape x1, local copies, waits for them, and re-layouts: 1.28 us -> 0.26 us  [shards(): probes.reshape(layers, columns, rows * depth)]
    convert_element_type x1, other arithmetic: 0.11 us -> 1.09 us  [shards(): rounded = probes.astype(jnp.bfloat16).reshape(layers, columns, rows * depth)]
    dot_general x1, matrix products: 1.21 us -> 0.37 us  [shards(): jnp.einsum('lsp,lsc->lcp', projector, slot_back, preferred_element_type=j...]
    reshape x2 -> x1, local copies, waits for them, and re-layouts: 0.35 us -> 1.18 us  [shards(): laplace = along_rows.reshape(probes.shape) + second_along(across, 3, depth)]
where the time goes in v12:
time: 75.3 us; the launch traced here: 74.9 us
  Pallas kernels  61.4 us (82%)
  local copies, waits for them, and re-layouts  8.57 us (11%)
  other arithmetic  3.35 us (4%)
  matrix products  1.44 us (2%)
    pallas_call x1, Pallas kernels, sweeps(): pl.pallas_call(functools.partial(exchange_kernel, count, layers), out_sha...  37.5 us
    pallas_call x1, Pallas kernels, front_exchange(): pl.pallas_call(functools.partial(front_kernel, row_count, layer_count, de...  23.9 us
    another operation x1, local copies, waits for them, and re-layouts, shards(): return swept.reshape(2, layers, columns, rows, depth)  2.46 us
    unnamed x16, local copies, waits for them, and re-layouts  2.1 us

profile of v12, /device:TPU:32, one launch (start us, length us, event | category | flops | bytes accessed | tf_op | source)
XLA Modules:
  0.0 74.9 jit_solution(9504762257447207038)
XLA Ops:
  0.0 0.0 copy-start
  0.0 0.0 copy-start.7
  0.0 0.1 pad.7.clone
  0.1 0.6 copy-done.7
  0.7 0.1 copy.14
  0.8 0.1 broadcast_in_dim.4
  0.9 1.1 %convert_element_type.18 = bf16[2,32,2,640]{3,2,1,0:T(2,128)(2,1)S(1)} convert(f32[2,32,2,640]{3,2,1,0:T(2,128)} %param.8) | non-fusion elementwise | flops 81920 | bytes 491520 | tf_op jit(solution)/shard_map/convert_element_type | solution.py:455
  2.0 0.1 reshape.26
  2.1 0.0 copy-done
  2.1 0.0 copy-start.5
  2.1 0.0 copy-start.1
  2.2 0.2 fusion.9
  2.4 0.5 copy-done.5
  2.8 0.9 %fusion.3.coef_ref = f32[2,32,256]{2,1,0:T(8,128)} fusion(f32[2,64,32]{1,2,0:T(8,128)S(1)} %fusion.9, s32[2,64]{1,0:T(2,128)S(1)} %copy-done.5), kind=kOutput, calls=%fused_computation.11 | convolution fusion | flops 12615680 | bytes 82432 | tf_op jit(solution)/shard_map/lsq,lsc->lcq/dot_general | solution.py:460
  3.7 0.0 copy-done.1
  3.7 0.3 reshape.25.block_ref
  4.0 0.0 copy-start.2
  4.0 0.3 copy.12
  4.2 0.4 copy-done.2
  4.7 1.0 %reshape.27.pieces_ref = f32[32,20,128]{2,1,0:T(8,128)} reshape(f32[32,2,1280]{2,1,0:T(2,128)S(1)} %copy.12) | data formatting | bytes 655360 | tf_op jit(solution)/shard_map/reshape | solution.py:422
  5.7 23.9 %shard_map.82 = (f32[2,32,1280]{2,1,0:T(8,128)}, f32[2,32,256]{2,1,0:T(8,128)}, f32[32,20,128]{2,1,0:T(8,128)}) custom-call(f32[2,32,1280]{2,1,0:T(8,128)} %copy-done.2, f32[2,32,256]{2,1,0:T(8,128)} %fusion.3.coef_ref, f32[32,20,128]{2,1,0:T(8,128)} %reshape.27.pieces_ref), custom_call_target="tpu_custom_call" | custom-call | tf_op jit(solution)/shard_map/pallas_call | solution.py:424
  29.6 0.0 copy-start.3
  29.6 0.0 copy-start.6
  29.7 1.2 %reshape.28 = f32[2,32,2,640]{3,2,1,0:T(2,128)S(1)} reshape(f32[2,32,1280]{2,1,0:T(8,128)} %get-tuple-element.8) | data formatting | bytes 655360 | tf_op jit(solution)/shard_map/reshape | solution.py:467
  30.8 0.0 copy-done.3
  30.9 0.0 copy-done.6
  30.9 0.4 fusion
  31.2 0.0 copy-start.4
  31.2 0.2 reshape.29
  31.4 0.5 copy-done.4
  31.9 1.4 %add_add_fusion = f32[2,32,2,640]{3,2,1,0:T(2,128)S(1)} fusion(f32[2,32,2,640]{3,2,1,0:T(2,128)S(1)} %reshape.29, f32[2,32,2,640]{3,2,1,0:T(2,128)S(1)} %copy-done.1, f32[2,32,2,640]{3,2,1,0:T(2,128)S(1)} %reshape.28, f32[2,2,640]{2,1,0:T(2,128)S(1)} %copy-done.4), kind=kLoop, calls=%fused_computation.4 | loop fusion | flops 983040 | bytes 1320960 | tf_op jit(solution)/shard_map/add | solution.py:476
  33.4 0.3 reshape.30
  33.6 0.3 copy.16
  33.9 0.3 reshape.31
  34.2 0.8 %maximum_maximum_fusion.ext_ref = f32[32,24,128]{2,1,0:T(8,128)} fusion(f32[32,2,128]{2,1,0:T(2,128)S(1)} %broadcast_in_dim.4, f32[32,20,128]{2,1,0:T(8,128)S(1)} %reshape.31, f32[24]{0:T(128)S(1)} %pad.7.clone), kind=kLoop, calls=%fused_computation.2 | loop fusion | flops 196608 | bytes 753760 | tf_op jit(solution)/shard_map/concatenate | solution.py:303
  35.0 37.5 %shard_map.83 = f32[2,2,32,10,128]{4,3,2,1,0:T(8,128)} custom-call(f32[4]{0:T(128)} %nodes_ref.1, f32[4]{0:T(128)} %weights_ref.1, f32[32,24,128]{2,1,0:T(8,128)} %maximum_maximum_fusion.ext_ref, f32[32,20,128]{2,1,0:T(8,128)} %get-tuple-element.10.probe_ref), custom_call_target="tpu_custom_call" | custom-call | tf_op jit(solution)/shard_map/pallas_call | solution.py:305
  72.5 2.5 %reshape_reshape.3 = f32[2,2,32,2,640]{4,3,2,1,0:T(2,128)} reshape(f32[2,2,32,10,128]{4,3,2,1,0:T(8,128)} %shard_map.83) | data formatting | bytes 1310720 | tf_op jit(solution)/shard_map/reshape;reshape | solution.py:481
  (1 shorter events, 0.0 us)
Async XLA Ops:
  0.0 2.1 %copy-start = (bf16[2,64,1280]{2,1,0:T(8,128)(2,1)S(1)}, bf16[2,64,1280]{2,1,0:T(8,128)(2,1)}, u32[]{:S(2)}) copy-start(bf16[2,64,1280]{2,1,0:T(8,128)(2,1)} %param.10) | copy-start | bytes 983044
  0.0 0.7 copy-start.7
  2.1 0.7 copy-start.5
  2.1 1.5 %copy-start.1 = (f32[2,32,2,640]{3,2,1,0:T(2,128)S(1)}, f32[2,32,2,640]{3,2,1,0:T(2,128)}, u32[]{:S(2)}) copy-start(f32[2,32,2,640]{3,2,1,0:T(2,128)} %param.8) | copy-start | bytes 983044
  4.0 0.7 copy-start.2
  29.6 1.2 %copy-start.3 = (f32[2,32,256]{2,1,0:T(8,128)S(1)}, f32[2,32,256]{2,1,0:T(8,128)}, u32[]{:S(2)}) copy-start(f32[2,32,256]{2,1,0:T(8,128)} %get-tuple-element.9) | copy-start | bytes 196612
  29.6 1.2 %copy-start.6 = (f32[2,256]{1,0:T(2,128)S(1)}, f32[2,256]{1,0:T(2,128)}, u32[]{:S(2)}) copy-start(f32[2,256]{1,0:T(2,128)} %param.12) | copy-start | bytes 6148
  31.2 0.7 copy-start.4

commit v13 on v12

--- a/solution.py
+++ b/solution.py
@@ -30,6 +30,21 @@
             axis=dim,
         )
     return cells
+
+
+def second_along_flat(flat, depth):
+    width = flat.shape[-1]
+    padded = jnp.pad(flat, [(0, 0)] * (flat.ndim - 1) + [(2, 2)])
+    spot = lax.broadcasted_iota(jnp.int32, (width,), 0) % depth
+
+    def piece(offset):
+        shifted = lax.slice_in_dim(padded, 2 + offset, 2 + offset + width, axis=flat.ndim - 1)
+        if offset == 0:
+            return shifted
+        inside = (spot + offset >= 0) & (spot + offset < depth)
+        return jnp.where(inside, shifted, 0.0)
+
+    return FAR * (piece(-2) + piece(2)) + NEAR * (piece(-1) + piece(1)) + CENTER * piece(0)
 
 
 def second_along(padded, axis, count):
@@ -460,11 +475,9 @@
     partial_coef = jnp.einsum("lsq,lsc->lcq", onehot, slot_coef, precision=lax.Precision.HIGHEST)
     if rows != 2:
         raise ValueError("rows")
-    along_rows, coef, regrouped = front_exchange(
-        probes.reshape(layers, columns, rows * depth), partial_coef, depth
-    )
-    across = jnp.pad(probes, ((0, 0), (0, 0), (0, 0), (2, 2)))
-    laplace = along_rows.reshape(probes.shape) + second_along(across, 3, depth)
+    flat = probes.reshape(layers, columns, rows * depth)
+    along_rows, coef, regrouped = front_exchange(flat, partial_coef, depth)
+    laplace = along_rows + second_along_flat(flat, depth)
     coef = jnp.swapaxes(coef, 1, 2)
     scaled = (strength[:, :, None] * coef).astype(jnp.bfloat16)
     slot_back = jnp.einsum(
@@ -472,10 +485,10 @@
     ).astype(jnp.bfloat16)
     projected = jnp.einsum(
         "lsp,lsc->lcp", projector, slot_back, preferred_element_type=jnp.float32
-    ).reshape(layers, columns, rows, depth)
-    partial = -0.5 * laplace + potential[:, None] * probes + projected
+    )
+    partial = -0.5 * laplace + potential.reshape(layers, 1, rows * depth) * flat + projected
     swept = sweeps(
-        partial.reshape(layers, columns, rows * depth), regrouped, decay_rates, contour_nodes,
+        partial, regrouped, decay_rates, contour_nodes,
         node_weights,
     )
     return swept.reshape(2, layers, columns, rows, depth)

time: 75.3 us -> 74.2 us (0.985)
  other arithmetic: 3.35 us -> 1.96 us
  matrix products: 1.44 us -> 2.58 us
  local copies, waits for them, and re-layouts: 8.57 us -> 7.77 us
    reshape x5 -> x1, local copies, waits for them, and re-layouts: 2.13 us -> 0.26 us  [shards(): flat = probes.reshape(layers, columns, rows * depth)]
    add x1 -> x0, other arithmetic: 1.42 us -> none  [shards(): partial = -0.5 * laplace + potential[:, None] * probes + projected]
    dot_general x1, matrix products: 0.37 us -> 1.5 us  [shards(): jnp.einsum('lsp,lsc->lcp', projector, slot_back, preferred_element_type=j...]
    unnamed x16 -> x17, local copies, waits for them, and re-layouts: 2.1 us -> 2.91 us
where the time goes in v13:
time: 74.2 us; the launch traced here: 73.9 us
  Pallas kernels  61.4 us (83%)
  local copies, waits for them, and re-layouts  7.77 us (10%)
  matrix products  2.58 us (3%)
  other arithmetic  1.96 us (3%)
    pallas_call x1, Pallas kernels, sweeps(): pl.pallas_call(functools.partial(exchange_kernel, count, layers), out_sha...  37.5 us
    pallas_call x1, Pallas kernels, front_exchange(): pl.pallas_call(functools.partial(front_kernel, row_count, layer_count, de...  24 us
    unnamed x17, local copies, waits for them, and re-layouts  2.91 us
    another operation x1, local copies, waits for them, and re-layouts, shards(): return swept.reshape(2, layers, columns, rows, depth)  2.46 us
    dot_general x1, matrix products, shards(): jnp.einsum('lsp,lsc->lcp', projector, slot_back, preferred_element_type=j...  1.5 us

profile of v13, /device:TPU:32, one launch (start us, length us, event | category | flops | bytes accessed | tf_op | source)
XLA Modules:
  0.0 73.9 jit_solution(530464644556585106)
XLA Ops:
  0.0 0.0 copy-start
  0.0 0.0 copy-start.4
  0.0 0.1 pad.7.clone
  0.1 0.6 copy-done.4
  0.8 0.0 copy-start.6
  0.8 0.7 copy-done.6
  1.4 0.1 copy.14
  1.5 0.1 broadcast_in_dim.37
  1.6 1.1 %convert_element_type.18 = bf16[2,32,2,640]{3,2,1,0:T(2,128)(2,1)S(1)} convert(f32[2,32,2,640]{3,2,1,0:T(2,128)} %param.8) | non-fusion elementwise | flops 81920 | bytes 491520 | tf_op jit(solution)/shard_map/convert_element_type | solution.py:470
  2.7 0.1 reshape.18
  2.8 0.0 copy-done
  2.8 0.0 copy-start.5
  2.9 0.0 copy-start.3
  2.9 0.2 fusion.39
  3.1 0.5 copy-done.5
  3.5 0.9 %fusion.14.coef_ref = f32[2,32,256]{2,1,0:T(8,128)} fusion(f32[2,64,32]{1,2,0:T(8,128)S(1)} %fusion.39, s32[2,64]{1,0:T(2,128)S(1)} %copy-done.5), kind=kOutput, calls=%fused_computation.23 | convolution fusion | flops 12615680 | bytes 82432 | tf_op jit(solution)/shard_map/lsq,lsc->lcq/dot_general | solution.py:475
  4.4 0.0 copy-done.3
  4.4 0.3 reshape.17.block_ref
  4.7 0.0 copy-start.1
  4.7 0.3 copy.12
  4.9 0.5 copy-done.1
  5.4 1.0 %reshape.19.pieces_ref = f32[32,20,128]{2,1,0:T(8,128)} reshape(f32[32,2,1280]{2,1,0:T(2,128)S(1)} %copy.12) | data formatting | bytes 655360 | tf_op jit(solution)/shard_map/reshape | solution.py:437
  6.4 0.0 copy-start.2
  6.4 24.0 %shard_map.82 = (f32[2,32,1280]{2,1,0:T(8,128)}, f32[2,32,256]{2,1,0:T(8,128)}, f32[32,20,128]{2,1,0:T(8,128)}) custom-call(f32[2,32,1280]{2,1,0:T(8,128)} %copy-done.1, f32[2,32,256]{2,1,0:T(8,128)} %fusion.14.coef_ref, f32[32,20,128]{2,1,0:T(8,128)} %reshape.19.pieces_ref), custom_call_target="tpu_custom_call" | custom-call | tf_op jit(solution)/shard_map/pallas_call | solution.py:439
  30.4 0.0 copy-start.7
  30.4 0.0 copy-done.2
  30.4 0.7 copy-done.7
  31.1 1.5 %fusion = f32[32,2,1280]{2,0,1:T(8,128)S(1)} fusion(bf16[2,64,1280]{2,1,0:T(8,128)(2,1)S(1)} %copy-done, f32[2,32,1280]{2,1,0:T(8,128)} %get-tuple-element.8, f32[2,32,1280]{2,1,0:T(8,128)S(1)} %copy-done.2, f32[2,1280]{1,0:T(2,128)S(1)} %bitcast.12, pred[1280]{0:T(1024)(128)(4,1)S(1)} %get-tuple-element.11, pred[1280]{0:T(1024)(128)(4,1)S(1)} %get-tuple-element.12, ...), kind=kOutput, calls=%fused_computation.1 | convolution fusion | flops 14028800 | bytes 1394176 | tf_op jit(solution)/shard_map/lsp,lsc->lcp/dot_general | solution.py:486
  32.6 0.3 copy.13
  32.8 0.3 reshape.20
  33.1 0.8 %maximum_maximum_fusion.ext_ref = f32[32,24,128]{2,1,0:T(8,128)} fusion(f32[32,2,128]{2,1,0:T(2,128)S(1)} %broadcast_in_dim.37, f32[32,20,128]{2,1,0:T(8,128)S(1)} %reshape.20, f32[24]{0:T(128)S(1)} %pad.7.clone), kind=kLoop, calls=%fused_computation.3 | loop fusion | flops 196608 | bytes 753760 | tf_op jit(solution)/shard_map/concatenate | solution.py:318
  34.0 37.5 %shard_map.83 = f32[2,2,32,10,128]{4,3,2,1,0:T(8,128)} custom-call(f32[4]{0:T(128)} %nodes_ref.1, f32[4]{0:T(128)} %weights_ref.1, f32[32,24,128]{2,1,0:T(8,128)} %maximum_maximum_fusion.ext_ref, f32[32,20,128]{2,1,0:T(8,128)} %get-tuple-element.10.probe_ref), custom_call_target="tpu_custom_call" | custom-call | tf_op jit(solution)/shard_map/pallas_call | solution.py:320
  71.4 2.5 %reshape_reshape.3 = f32[2,2,32,2,640]{4,3,2,1,0:T(2,128)} reshape(f32[2,2,32,10,128]{4,3,2,1,0:T(8,128)} %shard_map.83) | data formatting | bytes 1310720 | tf_op jit(solution)/shard_map/reshape;reshape | solution.py:494
  (4 shorter events, 0.0 us)
Async XLA Ops:
  0.0 2.8 %copy-start = (bf16[2,64,1280]{2,1,0:T(8,128)(2,1)S(1)}, bf16[2,64,1280]{2,1,0:T(8,128)(2,1)}, u32[]{:S(2)}) copy-start(bf16[2,64,1280]{2,1,0:T(8,128)(2,1)} %param.10) | copy-start | bytes 983044
  0.0 0.7 %copy-start.4 = (f32[2,2,640]{2,1,0:T(2,128)S(1)}, f32[2,2,640]{2,1,0:T(2,128)}, u32[]{:S(2)}) copy-start(f32[2,2,640]{2,1,0:T(2,128)} %param.9) | copy-start | bytes 30724
  0.8 0.7 copy-start.6
  2.8 0.7 copy-start.5
  2.9 1.5 %copy-start.3 = (f32[2,32,2,640]{3,2,1,0:T(2,128)S(1)}, f32[2,32,2,640]{3,2,1,0:T(2,128)}, u32[]{:S(2)}) copy-start(f32[2,32,2,640]{3,2,1,0:T(2,128)} %param.8) | copy-start | bytes 983044
  4.7 0.7 copy-start.1
  6.4 24.0 %copy-start.2 = (f32[2,32,1280]{2,1,0:T(8,128)S(1)}, f32[2,32,1280]{2,1,0:T(8,128)}, u32[]{:S(2)}) copy-start(f32[2,32,1280]{2,1,0:T(8,128)} %copy-done.1) | copy-start | bytes 983044
  30.4 0.7 copy-start.7

commit v14 on v13

--- a/solution.py
+++ b/solution.py
@@ -249,7 +249,7 @@
 
     def forward(source, state):
         for layer in range(layers):
-            rate = gathered[source, pl.ds(data_rows + layer, 1), :]
+            rate = probe_ref[source, pl.ds(data_rows + layer, 1), :]
             state = tuple(
                 rate * state[m] + (1.0 - rate) * swept[source, m, layer] for m in range(2)
             )
@@ -262,7 +262,7 @@
     def backward(step, state):
         source = count - 1 - step
         for layer in reversed(range(layers)):
-            rate = gathered[source, pl.ds(data_rows + layer, 1), :]
+            rate = probe_ref[source, pl.ds(data_rows + layer, 1), :]
             state = tuple(
                 rate * state[m] + (1.0 - rate) * swept[source, m, layer] for m in range(2)
             )
@@ -311,11 +311,7 @@
         raise ValueError("columns")
     tiles = width // 128
     data_rows = layers * tiles
-    padded_rows = -(-(data_rows + layers) // 8) * 8
-    body = jnp.transpose(partial, (1, 0, 2)).reshape(columns, data_rows, 128)
-    lanes = jnp.broadcast_to(jnp.transpose(decay_rates)[:, :, None], (columns, layers, 128))
-    spare = jnp.zeros((columns, padded_rows - data_rows - layers, 128), jnp.float32)
-    ext = jnp.concatenate([body, lanes, spare], axis=1)
+    ext = jnp.transpose(partial, (1, 0, 2)).reshape(columns, data_rows, 128)
     vmem = pl.BlockSpec(memory_space=pltpu.VMEM)
     out = pl.pallas_call(
         functools.partial(exchange_kernel, count, layers),
@@ -323,7 +319,7 @@
         in_specs=[pl.BlockSpec(memory_space=pltpu.SMEM)] * 2 + [vmem, vmem],
         out_specs=vmem,
         scratch_shapes=[
-            pltpu.VMEM((count, padded_rows, 128), jnp.float32),
+            pltpu.VMEM((count, data_rows, 128), jnp.float32),
             pltpu.VMEM((count, moments, layers, tiles, 128), jnp.float32),
             pltpu.SemaphoreType.DMA((count,)),
             pltpu.SemaphoreType.DMA((count,)),
@@ -430,11 +426,16 @@
     lax.fori_loop(1, layer_count, arrived, 0)
 
 
-def front_exchange(block, coef, depth):
+def front_exchange(block, coef, depth, decay_rates):
     row_count = lax.axis_size("xs")
     layer_count = lax.axis_size("layer")
     layers, columns, width = block.shape
-    pieces = jnp.transpose(block, (1, 0, 2)).reshape(columns, layers * width // 128, 128)
+    data_rows = layers * width // 128
+    padded_rows = -(-(data_rows + layers) // 8) * 8
+    body = jnp.transpose(block, (1, 0, 2)).reshape(columns, data_rows, 128)
+    lanes = jnp.broadcast_to(jnp.transpose(decay_rates)[:, :, None], (columns, layers, 128))
+    spare = jnp.zeros((columns, padded_rows - data_rows - layers, 128), jnp.float32)
+    pieces = jnp.concatenate([body, lanes, spare], axis=1)
     spec = pl.BlockSpec(memory_space=pltpu.VMEM)
     return pl.pallas_call(
         functools.partial(front_kernel, row_count, layer_count, depth),
@@ -467,7 +468,8 @@
     node_weights,
 ):
     layers, columns, rows, depth = probes.shape
-    rounded = probes.astype(jnp.bfloat16).reshape(layers, columns, rows * depth)
+    flat = probes.reshape(layers, columns, rows * depth)
+    rounded = flat.astype(jnp.bfloat16)
     slot_coef = jnp.einsum("lsp,lcp->lsc", projector, rounded, preferred_element_type=jnp.float32)
     onehot = (intersection_ids[:, :, None] == jnp.arange(NPROJ, dtype=jnp.int32)).astype(
         jnp.float32
@@ -475,8 +477,7 @@
     partial_coef = jnp.einsum("lsq,lsc->lcq", onehot, slot_coef, precision=lax.Precision.HIGHEST)
     if rows != 2:
         raise ValueError("rows")
-    flat = probes.reshape(layers, columns, rows * depth)
-    along_rows, coef, regrouped = front_exchange(flat, partial_coef, depth)
+    along_rows, coef, regrouped = front_exchange(flat, partial_coef, depth, decay_rates)
     laplace = along_rows + second_along_flat(flat, depth)
     coef = jnp.swapaxes(coef, 1, 2)
     scaled = (strength[:, :, None] * coef).astype(jnp.bfloat16)

time: 74.2 us -> 71.8 us (0.968)
  Pallas kernels: 61.4 us -> 59.6 us
  other arithmetic: 1.96 us -> 0.87 us
    pallas_call x1, Pallas kernels: 37.5 us -> 35.6 us  [sweeps(): pl.pallas_call(functools.partial(exchange_kernel, count, layers), out_sha...]
    convert_element_type x1 -> x0, other arithmetic: 1.09 us -> none  [shards(): rounded = probes.astype(jnp.bfloat16).reshape(layers, columns, rows * depth)]
    reshape x1, local copies, waits for them, and re-layouts: 0.26 us -> 1.24 us  [shards(): flat = probes.reshape(layers, columns, rows * depth)]
    unnamed x17 -> x15, local copies, waits for them, and re-layouts: 2.91 us -> 2.51 us
where the time goes in v14:
time: 71.8 us; the launch traced here: 71.3 us
  Pallas kernels  59.6 us (83%)
  local copies, waits for them, and re-layouts  8.24 us (11%)
  matrix products  2.57 us (4%)
  other arithmetic  0.87 us (1%)
    pallas_call x1, Pallas kernels, sweeps(): pl.pallas_call(functools.partial(exchange_kernel, count, layers), out_sha...  35.6 us
    pallas_call x1, Pallas kernels, front_exchange(): pl.pallas_call(functools.partial(front_kernel, row_count, layer_count, de...  24 us
    unnamed x15, local copies, waits for them, and re-layouts  2.51 us
    another operation x1, local copies, waits for them, and re-layouts, shards(): return swept.reshape(2, layers, columns, rows, depth)  2.46 us
    dot_general x1, matrix products, shards(): jnp.einsum('lsp,lsc->lcp', projector, slot_back, preferred_element_type=j...  1.5 us

profile of v14, /device:TPU:32, one launch (start us, length us, event | category | flops | bytes accessed | tf_op | source)
XLA Modules:
  0.0 71.3 jit_solution(18323894048092061496)
XLA Ops:
  0.0 0.0 copy-start
  0.0 0.0 copy-start.3
  0.0 0.1 pad.7.clone
  0.1 0.6 copy-done.3
  0.8 0.0 copy-start.5
  0.8 0.7 copy-done.5
  1.4 0.1 copy.13
  1.5 0.1 broadcast_in_dim.32
  1.6 1.2 %reshape.14.block_ref = f32[2,32,1280]{2,1,0:T(8,128)S(1)} reshape(f32[2,32,2,640]{3,2,1,0:T(2,128)} %param.8) | data formatting | bytes 655360 | tf_op jit(solution)/shard_map/reshape | solution.py:471
  2.9 0.0 copy-start.1
  2.9 0.0 copy-done
  2.9 0.0 copy-start.4
  2.9 0.2 fusion.14
  3.1 0.5 copy-done.4
  3.6 0.9 %fusion.16.coef_ref = f32[2,32,256]{2,1,0:T(8,128)} fusion(f32[2,64,32]{1,2,0:T(8,128)S(1)} %fusion.14, s32[2,64]{1,0:T(2,128)S(1)} %copy-done.4), kind=kOutput, calls=%fused_computation.25 | convolution fusion | flops 12615680 | bytes 82432 | tf_op jit(solution)/shard_map/lsq,lsc->lcq/dot_general | solution.py:477
  4.5 0.0 copy-done.1
  4.5 0.3 copy.12
  4.7 0.3 reshape.15
  5.0 0.8 %maximum_maximum_fusion.pieces_ref = f32[32,24,128]{2,1,0:T(8,128)} fusion(f32[32,2,128]{2,1,0:T(2,128)S(1)} %broadcast_in_dim.32, f32[32,20,128]{2,1,0:T(8,128)S(1)} %reshape.15, f32[24]{0:T(128)S(1)} %pad.7.clone), kind=kLoop, calls=%fused_computation.3 | loop fusion | flops 196608 | bytes 753760 | tf_op jit(solution)/shard_map/concatenate | solution.py:438
  5.8 0.0 copy-start.2
  5.9 24.0 %shard_map.82 = (f32[2,32,1280]{2,1,0:T(8,128)}, f32[2,32,256]{2,1,0:T(8,128)}, f32[32,24,128]{2,1,0:T(8,128)}) custom-call(f32[2,32,1280]{2,1,0:T(8,128)} %copy-done.1, f32[2,32,256]{2,1,0:T(8,128)} %fusion.16.coef_ref, f32[32,24,128]{2,1,0:T(8,128)} %maximum_maximum_fusion.pieces_ref), custom_call_target="tpu_custom_call" | custom-call | tf_op jit(solution)/shard_map/pallas_call | solution.py:440
  29.9 0.0 copy-start.6
  29.9 0.0 copy-done.2
  29.9 0.7 copy-done.6
  30.5 1.5 %fusion = f32[32,2,1280]{2,0,1:T(8,128)S(1)} fusion(bf16[2,64,1280]{2,1,0:T(8,128)(2,1)S(1)} %copy-done, f32[2,32,1280]{2,1,0:T(8,128)} %get-tuple-element.8, f32[2,32,1280]{2,1,0:T(8,128)S(1)} %copy-done.2, f32[2,1280]{1,0:T(2,128)S(1)} %bitcast.11, pred[1280]{0:T(1024)(128)(4,1)S(1)} %get-tuple-element.11, pred[1280]{0:T(1024)(128)(4,1)S(1)} %get-tuple-element.12, ...), kind=kOutput, calls=%fused_computation.1 | convolution fusion | flops 14028800 | bytes 1394176 | tf_op jit(solution)/shard_map/lsp,lsc->lcp/dot_general | solution.py:487
  32.0 0.3 copy.14
  32.3 1.0 %reshape.16.ext_ref = f32[32,20,128]{2,1,0:T(8,128)} reshape(f32[32,2,1280]{2,1,0:T(2,128)S(1)} %copy.14) | data formatting | bytes 655360 | tf_op jit(solution)/shard_map/reshape | solution.py:314
  33.3 35.6 %shard_map.83 = f32[2,2,32,10,128]{4,3,2,1,0:T(8,128)} custom-call(f32[4]{0:T(128)} %nodes_ref.1, f32[4]{0:T(128)} %weights_ref.1, f32[32,20,128]{2,1,0:T(8,128)} %reshape.16.ext_ref, f32[32,24,128]{2,1,0:T(8,128)} %get-tuple-element.10.probe_ref), custom_call_target="tpu_custom_call" | custom-call | tf_op jit(solution)/shard_map/pallas_call | solution.py:316
  68.9 2.5 %reshape_reshape.3 = f32[2,2,32,2,640]{4,3,2,1,0:T(2,128)} reshape(f32[2,2,32,10,128]{4,3,2,1,0:T(8,128)} %shard_map.83) | data formatting | bytes 1310720 | tf_op jit(solution)/shard_map/reshape;reshape | solution.py:495
  (4 shorter events, 0.0 us)
Async XLA Ops:
  0.0 2.9 %copy-start = (bf16[2,64,1280]{2,1,0:T(8,128)(2,1)S(1)}, bf16[2,64,1280]{2,1,0:T(8,128)(2,1)}, u32[]{:S(2)}) copy-start(bf16[2,64,1280]{2,1,0:T(8,128)(2,1)} %param.10) | copy-start | bytes 983044
  0.0 0.7 %copy-start.3 = (f32[2,2,640]{2,1,0:T(2,128)S(1)}, f32[2,2,640]{2,1,0:T(2,128)}, u32[]{:S(2)}) copy-start(f32[2,2,640]{2,1,0:T(2,128)} %param.9) | copy-start | bytes 30724
  0.8 0.7 copy-start.5
  2.9 1.6 %copy-start.1 = (f32[2,32,1280]{2,1,0:T(8,128)}, f32[2,32,1280]{2,1,0:T(8,128)S(1)}, u32[]{:S(2)}) copy-start(f32[2,32,1280]{2,1,0:T(8,128)S(1)} %reshape.14.block_ref) | copy-start | bytes 983044
  2.9 0.7 %copy-start.4 = (s32[2,64]{1,0:T(2,128)S(1)}, s32[2,64]{1,0:T(2,128)}, u32[]{:S(2)}) copy-start(s32[2,64]{1,0:T(2,128)} %param.11) | copy-start | bytes 1540
  5.8 24.0 %copy-start.2 = (f32[2,32,1280]{2,1,0:T(8,128)S(1)}, f32[2,32,1280]{2,1,0:T(8,128)}, u32[]{:S(2)}) copy-start(f32[2,32,1280]{2,1,0:T(8,128)} %copy-done.1) | copy-start | bytes 983044
  29.9 0.7 copy-start.6

commit v15 on v14

--- a/solution.py
+++ b/solution.py
@@ -303,15 +303,14 @@
     lax.fori_loop(1, count, returned, 0)
 
 
-def sweeps(partial, gathered_probes, decay_rates, nodes, weights):
-    layers, columns, width = partial.shape
+def sweeps(ext, gathered_probes, nodes, weights, width):
+    columns, data_rows, _ = ext.shape
+    tiles = width // 128
+    layers = data_rows // tiles
     moments = 2
     count = lax.axis_size("layer")
     if columns != count:
         raise ValueError("columns")
-    tiles = width // 128
-    data_rows = layers * tiles
-    ext = jnp.transpose(partial, (1, 0, 2)).reshape(columns, data_rows, 128)
     vmem = pl.BlockSpec(memory_space=pltpu.VMEM)
     out = pl.pallas_call(
         functools.partial(exchange_kernel, count, layers),
@@ -398,17 +397,20 @@
     before = left[...] * (row > 0).astype(jnp.float32)
     after = right[...] * (row < row_count - 1).astype(jnp.float32)
     mine = block_ref[...]
-    first, second = slice(0, depth), slice(depth, 2 * depth)
-    across[:, :, first] = (
-        FAR * (before[:, :, first] + after[:, :, first])
-        + NEAR * (before[:, :, second] + mine[:, :, second])
-        + CENTER * mine[:, :, first]
-    )
-    across[:, :, second] = (
-        FAR * (before[:, :, second] + after[:, :, second])
-        + NEAR * (mine[:, :, first] + after[:, :, first])
-        + CENTER * mine[:, :, second]
-    )
+    segment = depth // 128
+    for layer in range(block_ref.shape[1] // (2 * segment)):
+        first = slice(2 * layer * segment, (2 * layer + 1) * segment)
+        second = slice((2 * layer + 1) * segment, (2 * layer + 2) * segment)
+        across[:, first] = (
+            FAR * (before[:, first] + after[:, first])
+            + NEAR * (before[:, second] + mine[:, second])
+            + CENTER * mine[:, first]
+        )
+        across[:, second] = (
+            FAR * (before[:, second] + after[:, second])
+            + NEAR * (mine[:, first] + after[:, first])
+            + CENTER * mine[:, second]
+        )
 
     def arrived(step, carry):
         copy = pltpu.make_async_remote_copy(
@@ -426,16 +428,16 @@
     lax.fori_loop(1, layer_count, arrived, 0)
 
 
-def front_exchange(block, coef, depth, decay_rates):
+def front_exchange(body, coef, depth, decay_rates):
     row_count = lax.axis_size("xs")
     layer_count = lax.axis_size("layer")
-    layers, columns, width = block.shape
-    data_rows = layers * width // 128
+    columns, data_rows, _ = body.shape
+    layers = decay_rates.shape[0]
     padded_rows = -(-(data_rows + layers) // 8) * 8
-    body = jnp.transpose(block, (1, 0, 2)).reshape(columns, data_rows, 128)
     lanes = jnp.broadcast_to(jnp.transpose(decay_rates)[:, :, None], (columns, layers, 128))
     spare = jnp.zeros((columns, padded_rows - data_rows - layers, 128), jnp.float32)
     pieces = jnp.concatenate([body, lanes, spare], axis=1)
+    block = body
     spec = pl.BlockSpec(memory_space=pltpu.VMEM)
     return pl.pallas_call(
         functools.partial(front_kernel, row_count, layer_count, depth),
@@ -468,29 +470,32 @@
     node_weights,
 ):
     layers, columns, rows, depth = probes.shape
-    flat = probes.reshape(layers, columns, rows * depth)
+    width = rows * depth
+    flat = jnp.transpose(probes, (1, 0, 2, 3)).reshape(columns, layers, width)
     rounded = flat.astype(jnp.bfloat16)
-    slot_coef = jnp.einsum("lsp,lcp->lsc", projector, rounded, preferred_element_type=jnp.float32)
+    slot_coef = jnp.einsum("lsp,clp->lsc", projector, rounded, preferred_element_type=jnp.float32)
     onehot = (intersection_ids[:, :, None] == jnp.arange(NPROJ, dtype=jnp.int32)).astype(
         jnp.float32
     )
     partial_coef = jnp.einsum("lsq,lsc->lcq", onehot, slot_coef, precision=lax.Precision.HIGHEST)
     if rows != 2:
         raise ValueError("rows")
-    along_rows, coef, regrouped = front_exchange(flat, partial_coef, depth, decay_rates)
-    laplace = along_rows + second_along_flat(flat, depth)
+    along_rows, coef, regrouped = front_exchange(
+        flat.reshape(columns, layers * width // 128, 128), partial_coef, depth, decay_rates
+    )
+    laplace = along_rows.reshape(columns, layers, width) + second_along_flat(flat, depth)
     coef = jnp.swapaxes(coef, 1, 2)
     scaled = (strength[:, :, None] * coef).astype(jnp.bfloat16)
     slot_back = jnp.einsum(
         "lsq,lqc->lsc", onehot.astype(jnp.bfloat16), scaled, preferred_element_type=jnp.float32
     ).astype(jnp.bfloat16)
     projected = jnp.einsum(
-        "lsp,lsc->lcp", projector, slot_back, preferred_element_type=jnp.float32
+        "lsp,lsc->clp", projector, slot_back, preferred_element_type=jnp.float32
     )
-    partial = -0.5 * laplace + potential.reshape(layers, 1, rows * depth) * flat + projected
+    partial = -0.5 * laplace + potential.reshape(1, layers, width) * flat + projected
     swept = sweeps(
-        partial, regrouped, decay_rates, contour_nodes,
-        node_weights,
+        partial.reshape(columns, layers * width // 128, 128), regrouped, contour_nodes, node_weights,
+        width,
     )
     return swept.reshape(2, layers, columns, rows, depth)
 

time: 71.8 us -> 72.3 us (level)
  local copies, waits for them, and re-layouts: 8.24 us -> 9.4 us
  matrix products: 2.57 us -> 1.57 us
    dot_general x2, matrix products: 1.71 us -> 0.7 us  [the longest x1 0.5 us: shards(): jnp.einsum('lsp,lsc->clp', projector, slot_back, preferred_element_type=j...]
    unnamed x15 -> x17, local copies, waits for them, and re-layouts: 2.51 us -> 2.64 us
where the time goes in v15:
time: 72.3 us; the launch traced here: 71.7 us
  Pallas kernels  59.7 us (83%)
  local copies, waits for them, and re-layouts  9.4 us (13%)
  matrix products  1.57 us (2%)
  other arithmetic  0.87 us (1%)
    pallas_call x1, Pallas kernels, sweeps(): pl.pallas_call(functools.partial(exchange_kernel, count, layers), out_sha...  35.6 us
    pallas_call x1, Pallas kernels, front_exchange(): pl.pallas_call(functools.partial(front_kernel, row_count, layer_count, de...  24.1 us
    unnamed x17, local copies, waits for them, and re-layouts  2.64 us
    another operation x1, local copies, waits for them, and re-layouts, shards(): return swept.reshape(2, layers, columns, rows, depth)  2.46 us

profile of v15, /device:TPU:32, one launch (start us, length us, event | category | flops | bytes accessed | tf_op | source)
XLA Modules:
  0.0 71.7 jit_solution(1271517454816312928)
XLA Ops:
  0.0 0.0 copy-start
  0.0 1.1 %copy.13 = f32[32,2,2,640]{3,2,1,0:T(2,128)S(1)} copy(f32[32,2,2,640]{3,2,0,1:T(2,128)} %bitcast.13) | data formatting | bytes 655360 | tf_op jit(solution)/shard_map/transpose | solution.py:474
  1.1 0.3 reshape_reshape.6.block_ref
  1.3 0.0 copy-start.1
  1.4 0.0 copy-start.5
  1.4 0.7 copy-done.5
  2.1 0.1 copy.14
  2.1 0.1 broadcast_in_dim.32
  2.2 0.1 pad.7.clone
  2.3 0.0 copy-start.2
  2.3 0.8 %maximum_maximum_fusion.pieces_ref = f32[32,24,128]{2,1,0:T(8,128)} fusion(f32[32,2,128]{2,1,0:T(2,128)S(1)} %broadcast_in_dim.32, f32[32,20,128]{2,1,0:T(8,128)S(1)} %reshape_reshape.6.block_ref, f32[24]{0:T(128)S(1)} %pad.7.clone), kind=kLoop, calls=%fused_computation.3 | loop fusion | flops 196608 | bytes 753760 | tf_op jit(solution)/shard_map/concatenate | solution.py:439
  3.2 0.0 copy-done.1
  3.2 0.1 copy-done.2
  3.3 0.3 reshape.14
  3.6 0.0 copy-done
  3.6 0.0 copy-start.4
  3.6 0.2 fusion.14
  3.8 0.5 copy-done.4
  4.3 0.9 %fusion.16.coef_ref = f32[2,32,256]{2,1,0:T(8,128)} fusion(f32[2,64,32]{1,2,0:T(8,128)S(1)} %fusion.14, s32[2,64]{1,0:T(2,128)S(1)} %copy-done.4), kind=kOutput, calls=%fused_computation.25 | convolution fusion | flops 12615680 | bytes 82432 | tf_op jit(solution)/shard_map/lsq,lsc->lcq/dot_general | solution.py:480
  5.1 24.1 %shard_map.82 = (f32[32,20,128]{2,1,0:T(8,128)}, f32[2,32,256]{2,1,0:T(8,128)}, f32[32,24,128]{2,1,0:T(8,128)}) custom-call(f32[32,20,128]{2,1,0:T(8,128)} %copy-done.1, f32[2,32,256]{2,1,0:T(8,128)} %fusion.16.coef_ref, f32[32,24,128]{2,1,0:T(8,128)} %maximum_maximum_fusion.pieces_ref), custom_call_target="tpu_custom_call" | custom-call | tf_op jit(solution)/shard_map/pallas_call | solution.py:442
  29.3 0.0 copy-start.6
  29.3 1.2 %reshape.15 = f32[32,2,1280]{2,1,0:T(2,128)S(1)} reshape(f32[32,20,128]{2,1,0:T(8,128)} %get-tuple-element.8) | data formatting | bytes 655360 | tf_op jit(solution)/shard_map/reshape | solution.py:486
  30.5 0.0 copy-start.3
  30.5 0.7 copy-done.3
  31.2 0.0 copy-start.7
  31.2 0.0 copy-done.6
  31.2 0.7 copy-done.7
  31.9 0.5 fusion
  32.4 0.3 copy.16
  32.6 1.0 %reshape.16.ext_ref = f32[32,20,128]{2,1,0:T(8,128)} reshape(f32[32,2,1280]{2,1,0:T(2,128)S(1)} %copy.16) | data formatting | bytes 655360 | tf_op jit(solution)/shard_map/reshape | solution.py:497
  33.6 35.6 %shard_map.83 = f32[2,2,32,10,128]{4,3,2,1,0:T(8,128)} custom-call(f32[4]{0:T(128)} %nodes_ref.1, f32[4]{0:T(128)} %weights_ref.1, f32[32,20,128]{2,1,0:T(8,128)} %reshape.16.ext_ref, f32[32,24,128]{2,1,0:T(8,128)} %get-tuple-element.10.probe_ref), custom_call_target="tpu_custom_call" | custom-call | tf_op jit(solution)/shard_map/pallas_call | solution.py:315
  69.2 2.5 %reshape_reshape.7 = f32[2,2,32,2,640]{4,3,2,1,0:T(2,128)} reshape(f32[2,2,32,10,128]{4,3,2,1,0:T(8,128)} %shard_map.83) | data formatting | bytes 1310720 | tf_op jit(solution)/shard_map/reshape;reshape | solution.py:500
  (4 shorter events, 0.0 us)
Async XLA Ops:
  0.0 3.6 %copy-start = (bf16[2,64,1280]{2,1,0:T(8,128)(2,1)S(1)}, bf16[2,64,1280]{2,1,0:T(8,128)(2,1)}, u32[]{:S(2)}) copy-start(bf16[2,64,1280]{2,1,0:T(8,128)(2,1)} %param.10) | copy-start | bytes 983044
  1.3 1.8 %copy-start.1 = (f32[32,20,128]{2,1,0:T(8,128)}, f32[32,20,128]{2,1,0:T(8,128)S(1)}, u32[]{:S(2)}) copy-start(f32[32,20,128]{2,1,0:T(8,128)S(1)} %reshape_reshape.6.block_ref) | copy-start | bytes 983044
  1.4 0.7 copy-start.5
  2.3 1.0 %copy-start.2 = (f32[2,32,2,640]{3,2,1,0:T(2,128)S(1)}, f32[2,32,2,640]{3,2,1,0:T(2,128)}, u32[]{:S(2)}) copy-start(f32[2,32,2,640]{3,2,1,0:T(2,128)} %param.8) | copy-start | bytes 983044
  3.6 0.7 copy-start.4
  29.3 1.9 %copy-start.6 = (f32[2,32,256]{2,1,0:T(8,128)S(1)}, f32[2,32,256]{2,1,0:T(8,128)}, u32[]{:S(2)}) copy-start(f32[2,32,256]{2,1,0:T(8,128)} %get-tuple-element.9) | copy-start | bytes 196612
  30.5 0.7 copy-start.3
  31.2 0.7 copy-start.7

commit v16 on v14

--- a/solution.py
+++ b/solution.py
@@ -230,7 +230,7 @@
         layer = place - source * layers
         return inside * probe_ref[source, pl.ds(layer * half, half), :]
 
-    def prepare(source, carry):
+    def forward(source, state):
         for layer in range(layers):
             place = source * layers + layer
             here = probe_ref[source, pl.ds(layer * half, half), :]
@@ -241,18 +241,9 @@
                 + CENTER * here
             )
             hamil = partial - 0.5 * second
-            swept[source, 0, layer] = w0 * hamil - w1 * here
-            swept[source, 1, layer] = w1 * hamil - w2 * here
-        return carry
-
-    lax.fori_loop(0, count, prepare, 0)
-
-    def forward(source, state):
-        for layer in range(layers):
+            forcing = (w0 * hamil - w1 * here, w1 * hamil - w2 * here)
             rate = probe_ref[source, pl.ds(data_rows + layer, 1), :]
-            state = tuple(
-                rate * state[m] + (1.0 - rate) * swept[source, m, layer] for m in range(2)
-            )
+            state = tuple(rate * state[m] + (1.0 - rate) * forcing[m] for m in range(2))
             for m in range(2):
                 swept[source, m, layer] = state[m]
         return state

time: 71.8 us -> 71.5 us (level)
  no operation moved by 1% of the time
where the time goes in v16:
time: 71.5 us; the launch traced here: 71.1 us
  Pallas kernels  59.3 us (83%)
  local copies, waits for them, and re-layouts  8.24 us (12%)
  matrix products  2.57 us (4%)
  other arithmetic  0.87 us (1%)
    pallas_call x1, Pallas kernels, sweeps(): pl.pallas_call(functools.partial(exchange_kernel, count, layers), out_sha...  35.3 us
    pallas_call x1, Pallas kernels, front_exchange(): pl.pallas_call(functools.partial(front_kernel, row_count, layer_count, de...  24 us
    unnamed x15, local copies, waits for them, and re-layouts  2.51 us
    another operation x1, local copies, waits for them, and re-layouts, shards(): return swept.reshape(2, layers, columns, rows, depth)  2.46 us
    dot_general x1, matrix products, shards(): jnp.einsum('lsp,lsc->lcp', projector, slot_back, preferred_element_type=j...  1.5 us

profile of v16, /device:TPU:32, one launch (start us, length us, event | category | flops | bytes accessed | tf_op | source)
XLA Modules:
  0.0 71.1 jit_solution(13434106175804317244)
XLA Ops:
  0.0 0.0 copy-start
  0.0 0.0 copy-start.3
  0.0 0.1 pad.7.clone
  0.1 0.6 copy-done.3
  0.8 0.0 copy-start.5
  0.8 0.7 copy-done.5
  1.4 0.1 copy.13
  1.5 0.1 broadcast_in_dim.32
  1.6 1.2 %reshape.14.block_ref = f32[2,32,1280]{2,1,0:T(8,128)S(1)} reshape(f32[2,32,2,640]{3,2,1,0:T(2,128)} %param.8) | data formatting | bytes 655360 | tf_op jit(solution)/shard_map/reshape | solution.py:462
  2.9 0.0 copy-start.1
  2.9 0.0 copy-done
  2.9 0.0 copy-start.4
  2.9 0.2 fusion.14
  3.1 0.5 copy-done.4
  3.6 0.9 %fusion.16.coef_ref = f32[2,32,256]{2,1,0:T(8,128)} fusion(f32[2,64,32]{1,2,0:T(8,128)S(1)} %fusion.14, s32[2,64]{1,0:T(2,128)S(1)} %copy-done.4), kind=kOutput, calls=%fused_computation.25 | convolution fusion | flops 12615680 | bytes 82432 | tf_op jit(solution)/shard_map/lsq,lsc->lcq/dot_general | solution.py:468
  4.5 0.0 copy-done.1
  4.5 0.3 copy.12
  4.7 0.3 reshape.15
  5.0 0.8 %maximum_maximum_fusion.pieces_ref = f32[32,24,128]{2,1,0:T(8,128)} fusion(f32[32,2,128]{2,1,0:T(2,128)S(1)} %broadcast_in_dim.32, f32[32,20,128]{2,1,0:T(8,128)S(1)} %reshape.15, f32[24]{0:T(128)S(1)} %pad.7.clone), kind=kLoop, calls=%fused_computation.3 | loop fusion | flops 196608 | bytes 753760 | tf_op jit(solution)/shard_map/concatenate | solution.py:429
  5.8 0.0 copy-start.2
  5.9 24.0 %shard_map.82 = (f32[2,32,1280]{2,1,0:T(8,128)}, f32[2,32,256]{2,1,0:T(8,128)}, f32[32,24,128]{2,1,0:T(8,128)}) custom-call(f32[2,32,1280]{2,1,0:T(8,128)} %copy-done.1, f32[2,32,256]{2,1,0:T(8,128)} %fusion.16.coef_ref, f32[32,24,128]{2,1,0:T(8,128)} %maximum_maximum_fusion.pieces_ref), custom_call_target="tpu_custom_call" | custom-call | tf_op jit(solution)/shard_map/pallas_call | solution.py:431
  29.9 0.0 copy-start.6
  29.9 0.0 copy-done.2
  29.9 0.7 copy-done.6
  30.5 1.5 %fusion = f32[32,2,1280]{2,0,1:T(8,128)S(1)} fusion(bf16[2,64,1280]{2,1,0:T(8,128)(2,1)S(1)} %copy-done, f32[2,32,1280]{2,1,0:T(8,128)} %get-tuple-element.8, f32[2,32,1280]{2,1,0:T(8,128)S(1)} %copy-done.2, f32[2,1280]{1,0:T(2,128)S(1)} %bitcast.11, pred[1280]{0:T(1024)(128)(4,1)S(1)} %get-tuple-element.11, pred[1280]{0:T(1024)(128)(4,1)S(1)} %get-tuple-element.12, ...), kind=kOutput, calls=%fused_computation.1 | convolution fusion | flops 14028800 | bytes 1394176 | tf_op jit(solution)/shard_map/lsp,lsc->lcp/dot_general | solution.py:478
  32.0 0.3 copy.14
  32.3 1.0 %reshape.16.ext_ref = f32[32,20,128]{2,1,0:T(8,128)} reshape(f32[32,2,1280]{2,1,0:T(2,128)S(1)} %copy.14) | data formatting | bytes 655360 | tf_op jit(solution)/shard_map/reshape | solution.py:305
  33.3 35.3 %shard_map.83 = f32[2,2,32,10,128]{4,3,2,1,0:T(8,128)} custom-call(f32[4]{0:T(128)} %nodes_ref.1, f32[4]{0:T(128)} %weights_ref.1, f32[32,20,128]{2,1,0:T(8,128)} %reshape.16.ext_ref, f32[32,24,128]{2,1,0:T(8,128)} %get-tuple-element.10.probe_ref), custom_call_target="tpu_custom_call" | custom-call | tf_op jit(solution)/shard_map/pallas_call | solution.py:307
  68.6 2.5 %reshape_reshape.3 = f32[2,2,32,2,640]{4,3,2,1,0:T(2,128)} reshape(f32[2,2,32,10,128]{4,3,2,1,0:T(8,128)} %shard_map.83) | data formatting | bytes 1310720 | tf_op jit(solution)/shard_map/reshape;reshape | solution.py:486
  (4 shorter events, 0.0 us)
Async XLA Ops:
  0.0 2.9 %copy-start = (bf16[2,64,1280]{2,1,0:T(8,128)(2,1)S(1)}, bf16[2,64,1280]{2,1,0:T(8,128)(2,1)}, u32[]{:S(2)}) copy-start(bf16[2,64,1280]{2,1,0:T(8,128)(2,1)} %param.10) | copy-start | bytes 983044
  0.0 0.7 %copy-start.3 = (f32[2,2,640]{2,1,0:T(2,128)S(1)}, f32[2,2,640]{2,1,0:T(2,128)}, u32[]{:S(2)}) copy-start(f32[2,2,640]{2,1,0:T(2,128)} %param.9) | copy-start | bytes 30724
  0.8 0.7 copy-start.5
  2.9 1.6 %copy-start.1 = (f32[2,32,1280]{2,1,0:T(8,128)}, f32[2,32,1280]{2,1,0:T(8,128)S(1)}, u32[]{:S(2)}) copy-start(f32[2,32,1280]{2,1,0:T(8,128)S(1)} %reshape.14.block_ref) | copy-start | bytes 983044
  2.9 0.7 %copy-start.4 = (s32[2,64]{1,0:T(2,128)S(1)}, s32[2,64]{1,0:T(2,128)}, u32[]{:S(2)}) copy-start(s32[2,64]{1,0:T(2,128)} %param.11) | copy-start | bytes 1540
  5.8 24.0 %copy-start.2 = (f32[2,32,1280]{2,1,0:T(8,128)S(1)}, f32[2,32,1280]{2,1,0:T(8,128)}, u32[]{:S(2)}) copy-start(f32[2,32,1280]{2,1,0:T(8,128)} %copy-done.1) | copy-start | bytes 983044
  29.9 0.7 copy-start.6

commit v17 on v16

--- a/solution.py
+++ b/solution.py
@@ -235,9 +235,14 @@
             place = source * layers + layer
             here = probe_ref[source, pl.ds(layer * half, half), :]
             partial = gathered[source, pl.ds(layer * half, half), :]
+            def near(offset):
+                if 0 <= layer + offset < layers:
+                    return probe_ref[source, pl.ds((layer + offset) * half, half), :]
+                return probe_at(place + offset)
+
             second = (
-                FAR * (probe_at(place - 2) + probe_at(place + 2))
-                + NEAR * (probe_at(place - 1) + probe_at(place + 1))
+                FAR * (near(-2) + near(2))
+                + NEAR * (near(-1) + near(1))
                 + CENTER * here
             )
             hamil = partial - 0.5 * second

time: 71.5 us -> 71 us (level)
  no operation moved by 1% of the time
where the time goes in v17:
time: 71 us; the launch traced here: 70.6 us
  Pallas kernels  58.8 us (83%)
  local copies, waits for them, and re-layouts  8.24 us (12%)
  matrix products  2.57 us (4%)
  other arithmetic  0.87 us (1%)
    pallas_call x1, Pallas kernels, sweeps(): pl.pallas_call(functools.partial(exchange_kernel, count, layers), out_sha...  34.8 us
    pallas_call x1, Pallas kernels, front_exchange(): pl.pallas_call(functools.partial(front_kernel, row_count, layer_count, de...  24 us
    unnamed x15, local copies, waits for them, and re-layouts  2.51 us
    another operation x1, local copies, waits for them, and re-layouts, shards(): return swept.reshape(2, layers, columns, rows, depth)  2.46 us
    dot_general x1, matrix products, shards(): jnp.einsum('lsp,lsc->lcp', projector, slot_back, preferred_element_type=j...  1.5 us

profile of v17, /device:TPU:32, one launch (start us, length us, event | category | flops | bytes accessed | tf_op | source)
XLA Modules:
  0.0 70.6 jit_solution(4501193184312581119)
XLA Ops:
  0.0 0.0 copy-start
  0.0 0.0 copy-start.3
  0.0 0.1 pad.7.clone
  0.1 0.6 copy-done.3
  0.8 0.0 copy-start.5
  0.8 0.7 copy-done.5
  1.4 0.1 copy.13
  1.5 0.1 broadcast_in_dim.32
  1.6 1.2 %reshape.14.block_ref = f32[2,32,1280]{2,1,0:T(8,128)S(1)} reshape(f32[2,32,2,640]{3,2,1,0:T(2,128)} %param.8) | data formatting | bytes 655360 | tf_op jit(solution)/shard_map/reshape | solution.py:467
  2.9 0.0 copy-start.1
  2.9 0.0 copy-done
  2.9 0.0 copy-start.4
  2.9 0.2 fusion.14
  3.1 0.5 copy-done.4
  3.6 0.9 %fusion.16.coef_ref = f32[2,32,256]{2,1,0:T(8,128)} fusion(f32[2,64,32]{1,2,0:T(8,128)S(1)} %fusion.14, s32[2,64]{1,0:T(2,128)S(1)} %copy-done.4), kind=kOutput, calls=%fused_computation.25 | convolution fusion | flops 12615680 | bytes 82432 | tf_op jit(solution)/shard_map/lsq,lsc->lcq/dot_general | solution.py:473
  4.5 0.0 copy-done.1
  4.5 0.3 copy.12
  4.7 0.3 reshape.15
  5.0 0.8 %maximum_maximum_fusion.pieces_ref = f32[32,24,128]{2,1,0:T(8,128)} fusion(f32[32,2,128]{2,1,0:T(2,128)S(1)} %broadcast_in_dim.32, f32[32,20,128]{2,1,0:T(8,128)S(1)} %reshape.15, f32[24]{0:T(128)S(1)} %pad.7.clone), kind=kLoop, calls=%fused_computation.3 | loop fusion | flops 196608 | bytes 753760 | tf_op jit(solution)/shard_map/concatenate | solution.py:434
  5.8 0.0 copy-start.2
  5.9 24.0 %shard_map.82 = (f32[2,32,1280]{2,1,0:T(8,128)}, f32[2,32,256]{2,1,0:T(8,128)}, f32[32,24,128]{2,1,0:T(8,128)}) custom-call(f32[2,32,1280]{2,1,0:T(8,128)} %copy-done.1, f32[2,32,256]{2,1,0:T(8,128)} %fusion.16.coef_ref, f32[32,24,128]{2,1,0:T(8,128)} %maximum_maximum_fusion.pieces_ref), custom_call_target="tpu_custom_call" | custom-call | tf_op jit(solution)/shard_map/pallas_call | solution.py:436
  29.9 0.0 copy-start.6
  29.9 0.0 copy-done.2
  29.9 0.7 copy-done.6
  30.5 1.5 %fusion = f32[32,2,1280]{2,0,1:T(8,128)S(1)} fusion(bf16[2,64,1280]{2,1,0:T(8,128)(2,1)S(1)} %copy-done, f32[2,32,1280]{2,1,0:T(8,128)} %get-tuple-element.8, f32[2,32,1280]{2,1,0:T(8,128)S(1)} %copy-done.2, f32[2,1280]{1,0:T(2,128)S(1)} %bitcast.11, pred[1280]{0:T(1024)(128)(4,1)S(1)} %get-tuple-element.11, pred[1280]{0:T(1024)(128)(4,1)S(1)} %get-tuple-element.12, ...), kind=kOutput, calls=%fused_computation.1 | convolution fusion | flops 14028800 | bytes 1394176 | tf_op jit(solution)/shard_map/lsp,lsc->lcp/dot_general | solution.py:483
  32.0 0.3 copy.14
  32.3 1.0 %reshape.16.ext_ref = f32[32,20,128]{2,1,0:T(8,128)} reshape(f32[32,2,1280]{2,1,0:T(2,128)S(1)} %copy.14) | data formatting | bytes 655360 | tf_op jit(solution)/shard_map/reshape | solution.py:310
  33.3 34.8 %shard_map.83 = f32[2,2,32,10,128]{4,3,2,1,0:T(8,128)} custom-call(f32[4]{0:T(128)} %nodes_ref.1, f32[4]{0:T(128)} %weights_ref.1, f32[32,20,128]{2,1,0:T(8,128)} %reshape.16.ext_ref, f32[32,24,128]{2,1,0:T(8,128)} %get-tuple-element.10.probe_ref), custom_call_target="tpu_custom_call" | custom-call | tf_op jit(solution)/shard_map/pallas_call | solution.py:312
  68.2 2.5 %reshape_reshape.3 = f32[2,2,32,2,640]{4,3,2,1,0:T(2,128)} reshape(f32[2,2,32,10,128]{4,3,2,1,0:T(8,128)} %shard_map.83) | data formatting | bytes 1310720 | tf_op jit(solution)/shard_map/reshape;reshape | solution.py:491
  (4 shorter events, 0.0 us)
Async XLA Ops:
  0.0 2.9 %copy-start = (bf16[2,64,1280]{2,1,0:T(8,128)(2,1)S(1)}, bf16[2,64,1280]{2,1,0:T(8,128)(2,1)}, u32[]{:S(2)}) copy-start(bf16[2,64,1280]{2,1,0:T(8,128)(2,1)} %param.10) | copy-start | bytes 983044
  0.0 0.7 %copy-start.3 = (f32[2,2,640]{2,1,0:T(2,128)S(1)}, f32[2,2,640]{2,1,0:T(2,128)}, u32[]{:S(2)}) copy-start(f32[2,2,640]{2,1,0:T(2,128)} %param.9) | copy-start | bytes 30724
  0.8 0.7 copy-start.5
  2.9 1.6 %copy-start.1 = (f32[2,32,1280]{2,1,0:T(8,128)}, f32[2,32,1280]{2,1,0:T(8,128)S(1)}, u32[]{:S(2)}) copy-start(f32[2,32,1280]{2,1,0:T(8,128)S(1)} %reshape.14.block_ref) | copy-start | bytes 983044
  2.9 0.7 %copy-start.4 = (s32[2,64]{1,0:T(2,128)S(1)}, s32[2,64]{1,0:T(2,128)}, u32[]{:S(2)}) copy-start(s32[2,64]{1,0:T(2,128)} %param.11) | copy-start | bytes 1540
  5.8 24.0 %copy-start.2 = (f32[2,32,1280]{2,1,0:T(8,128)S(1)}, f32[2,32,1280]{2,1,0:T(8,128)}, u32[]{:S(2)}) copy-start(f32[2,32,1280]{2,1,0:T(8,128)} %copy-done.1) | copy-start | bytes 983044
  29.9 0.7 copy-start.6

commit v18 on v17

--- a/solution.py
+++ b/solution.py
@@ -264,23 +264,21 @@
             )
             for m in range(2):
                 swept[source, m, layer] = state[m]
+
+        @pl.when(source != me)
+        def _():
+            pltpu.make_async_remote_copy(
+                src_ref=swept.at[source],
+                dst_ref=out_ref.at[:, :, me],
+                send_sem=back_send.at[lax.rem(source - me + count, count)],
+                recv_sem=back_recv.at[lax.rem(source - me + count, count)],
+                device_id=(source, row),
+                device_id_type=MESH,
+            ).start()
+
         return state
 
     lax.fori_loop(0, count, backward, (zero, zero))
-
-    def returning(step, carry):
-        target = lax.rem(me + step, count)
-        pltpu.make_async_remote_copy(
-            src_ref=swept.at[target],
-            dst_ref=out_ref.at[:, :, me],
-            send_sem=back_send.at[step],
-            recv_sem=back_recv.at[step],
-            device_id=(target, row),
-            device_id_type=MESH,
-        ).start()
-        return carry
-
-    lax.fori_loop(1, count, returning, 0)
     out_ref[:, :, me] = swept[me]
 
     def returned(step, carry):

time: 71 us -> 74.2 us (1.045)
  Pallas kernels: 58.8 us -> 62 us
    pallas_call x1, Pallas kernels: 34.8 us -> 38 us  [sweeps(): pl.pallas_call(functools.partial(exchange_kernel, count, layers), out_sha...]
where the time goes in v18:
time: 74.2 us; the launch traced here: 73.8 us
  Pallas kernels  62 us (84%)
  local copies, waits for them, and re-layouts  8.24 us (11%)
  matrix products  2.57 us (3%)
  other arithmetic  0.87 us (1%)
    pallas_call x1, Pallas kernels, sweeps(): pl.pallas_call(functools.partial(exchange_kernel, count, layers), out_sha...  38 us
    pallas_call x1, Pallas kernels, front_exchange(): pl.pallas_call(functools.partial(front_kernel, row_count, layer_count, de...  24 us
    unnamed x15, local copies, waits for them, and re-layouts  2.51 us
    another operation x1, local copies, waits for them, and re-layouts, shards(): return swept.reshape(2, layers, columns, rows, depth)  2.46 us
    dot_general x1, matrix products, shards(): jnp.einsum('lsp,lsc->lcp', projector, slot_back, preferred_element_type=j...  1.5 us

profile of v18, /device:TPU:32, one launch (start us, length us, event | category | flops | bytes accessed | tf_op | source)
XLA Modules:
  0.0 73.8 jit_solution(5465296019258013832)
XLA Ops:
  0.0 0.0 copy-start
  0.0 0.0 copy-start.3
  0.0 0.1 pad.7.clone
  0.1 0.6 copy-done.3
  0.8 0.0 copy-start.5
  0.8 0.7 copy-done.5
  1.4 0.1 copy.13
  1.5 0.1 broadcast_in_dim.32
  1.6 1.2 %reshape.14.block_ref = f32[2,32,1280]{2,1,0:T(8,128)S(1)} reshape(f32[2,32,2,640]{3,2,1,0:T(2,128)} %param.8) | data formatting | bytes 655360 | tf_op jit(solution)/shard_map/reshape | solution.py:465
  2.9 0.0 copy-start.1
  2.9 0.0 copy-done
  2.9 0.0 copy-start.4
  2.9 0.2 fusion.14
  3.1 0.5 copy-done.4
  3.6 0.9 %fusion.16.coef_ref = f32[2,32,256]{2,1,0:T(8,128)} fusion(f32[2,64,32]{1,2,0:T(8,128)S(1)} %fusion.14, s32[2,64]{1,0:T(2,128)S(1)} %copy-done.4), kind=kOutput, calls=%fused_computation.25 | convolution fusion | flops 12615680 | bytes 82432 | tf_op jit(solution)/shard_map/lsq,lsc->lcq/dot_general | solution.py:471
  4.5 0.0 copy-done.1
  4.5 0.3 copy.12
  4.7 0.3 reshape.15
  5.0 0.8 %maximum_maximum_fusion.pieces_ref = f32[32,24,128]{2,1,0:T(8,128)} fusion(f32[32,2,128]{2,1,0:T(2,128)S(1)} %broadcast_in_dim.32, f32[32,20,128]{2,1,0:T(8,128)S(1)} %reshape.15, f32[24]{0:T(128)S(1)} %pad.7.clone), kind=kLoop, calls=%fused_computation.3 | loop fusion | flops 196608 | bytes 753760 | tf_op jit(solution)/shard_map/concatenate | solution.py:432
  5.8 0.0 copy-start.2
  5.9 24.0 %shard_map.82 = (f32[2,32,1280]{2,1,0:T(8,128)}, f32[2,32,256]{2,1,0:T(8,128)}, f32[32,24,128]{2,1,0:T(8,128)}) custom-call(f32[2,32,1280]{2,1,0:T(8,128)} %copy-done.1, f32[2,32,256]{2,1,0:T(8,128)} %fusion.16.coef_ref, f32[32,24,128]{2,1,0:T(8,128)} %maximum_maximum_fusion.pieces_ref), custom_call_target="tpu_custom_call" | custom-call | tf_op jit(solution)/shard_map/pallas_call | solution.py:434
  29.9 0.0 copy-start.6
  29.9 0.0 copy-done.2
  29.9 0.7 copy-done.6
  30.5 1.5 %fusion = f32[32,2,1280]{2,0,1:T(8,128)S(1)} fusion(bf16[2,64,1280]{2,1,0:T(8,128)(2,1)S(1)} %copy-done, f32[2,32,1280]{2,1,0:T(8,128)} %get-tuple-element.8, f32[2,32,1280]{2,1,0:T(8,128)S(1)} %copy-done.2, f32[2,1280]{1,0:T(2,128)S(1)} %bitcast.11, pred[1280]{0:T(1024)(128)(4,1)S(1)} %get-tuple-element.11, pred[1280]{0:T(1024)(128)(4,1)S(1)} %get-tuple-element.12, ...), kind=kOutput, calls=%fused_computation.1 | convolution fusion | flops 14028800 | bytes 1394176 | tf_op jit(solution)/shard_map/lsp,lsc->lcp/dot_general | solution.py:481
  32.0 0.3 copy.14
  32.3 1.0 %reshape.16.ext_ref = f32[32,20,128]{2,1,0:T(8,128)} reshape(f32[32,2,1280]{2,1,0:T(2,128)S(1)} %copy.14) | data formatting | bytes 655360 | tf_op jit(solution)/shard_map/reshape | solution.py:308
  33.3 38.0 %shard_map.83 = f32[2,2,32,10,128]{4,3,2,1,0:T(8,128)} custom-call(f32[4]{0:T(128)} %nodes_ref.1, f32[4]{0:T(128)} %weights_ref.1, f32[32,20,128]{2,1,0:T(8,128)} %reshape.16.ext_ref, f32[32,24,128]{2,1,0:T(8,128)} %get-tuple-element.10.probe_ref), custom_call_target="tpu_custom_call" | custom-call | tf_op jit(solution)/shard_map/pallas_call | solution.py:310
  71.3 2.5 %reshape_reshape.3 = f32[2,2,32,2,640]{4,3,2,1,0:T(2,128)} reshape(f32[2,2,32,10,128]{4,3,2,1,0:T(8,128)} %shard_map.83) | data formatting | bytes 1310720 | tf_op jit(solution)/shard_map/reshape;reshape | solution.py:489
  (4 shorter events, 0.0 us)
Async XLA Ops:
  0.0 2.9 %copy-start = (bf16[2,64,1280]{2,1,0:T(8,128)(2,1)S(1)}, bf16[2,64,1280]{2,1,0:T(8,128)(2,1)}, u32[]{:S(2)}) copy-start(bf16[2,64,1280]{2,1,0:T(8,128)(2,1)} %param.10) | copy-start | bytes 983044
  0.0 0.7 %copy-start.3 = (f32[2,2,640]{2,1,0:T(2,128)S(1)}, f32[2,2,640]{2,1,0:T(2,128)}, u32[]{:S(2)}) copy-start(f32[2,2,640]{2,1,0:T(2,128)} %param.9) | copy-start | bytes 30724
  0.8 0.7 copy-start.5
  2.9 1.6 %copy-start.1 = (f32[2,32,1280]{2,1,0:T(8,128)}, f32[2,32,1280]{2,1,0:T(8,128)S(1)}, u32[]{:S(2)}) copy-start(f32[2,32,1280]{2,1,0:T(8,128)S(1)} %reshape.14.block_ref) | copy-start | bytes 983044
  2.9 0.7 copy-start.4
  5.8 24.0 %copy-start.2 = (f32[2,32,1280]{2,1,0:T(8,128)S(1)}, f32[2,32,1280]{2,1,0:T(8,128)}, u32[]{:S(2)}) copy-start(f32[2,32,1280]{2,1,0:T(8,128)} %copy-done.1) | copy-start | bytes 983044
  29.9 0.7 copy-start.6

commit v19 on v17

--- a/solution.py
+++ b/solution.py
@@ -168,11 +168,14 @@
     me = lax.axis_index("layer")
     row = lax.axis_index("xs")
     layers = layer_count
+    def offset(step):
+        return ((step + 1) // 2) * (1 - 2 * ((step + 1) % 2))
+
     barrier = pltpu.get_barrier_semaphore()
 
     def greet(step, carry):
         pl.semaphore_signal(
-            barrier, inc=1, device_id=(lax.rem(me + step, count), row), device_id_type=MESH
+            barrier, inc=1, device_id=(lax.rem(me + offset(step) + count, count), row), device_id_type=MESH
         )
         return carry
 
@@ -180,7 +183,7 @@
     pl.semaphore_wait(barrier, count - 1)
 
     def outgoing(step, carry):
-        target = lax.rem(me + step, count)
+        target = lax.rem(me + offset(step) + count, count)
         pltpu.make_async_remote_copy(
             src_ref=ext_ref.at[target],
             dst_ref=gathered.at[me],
@@ -197,10 +200,10 @@
     def arrived(step, carry):
         copy = pltpu.make_async_remote_copy(
             src_ref=ext_ref.at[me],
-            dst_ref=gathered.at[lax.rem(me + count - step, count)],
+            dst_ref=gathered.at[lax.rem(me + count - offset(step), count)],
             send_sem=send_sem.at[step],
             recv_sem=recv_sem.at[step],
-            device_id=(lax.rem(me + step, count), row),
+            device_id=(lax.rem(me + offset(step) + count, count), row),
             device_id_type=MESH,
         )
         copy.wait_send()
@@ -269,7 +272,7 @@
     lax.fori_loop(0, count, backward, (zero, zero))
 
     def returning(step, carry):
-        target = lax.rem(me + step, count)
+        target = lax.rem(me + offset(step) + count, count)
         pltpu.make_async_remote_copy(
             src_ref=swept.at[target],
             dst_ref=out_ref.at[:, :, me],
@@ -286,10 +289,10 @@
     def returned(step, carry):
         copy = pltpu.make_async_remote_copy(
             src_ref=swept.at[me],
-            dst_ref=out_ref.at[:, :, lax.rem(me + count - step, count)],
+            dst_ref=out_ref.at[:, :, lax.rem(me + count - offset(step), count)],
             send_sem=back_send.at[step],
             recv_sem=back_recv.at[step],
-            device_id=(lax.rem(me + step, count), row),
+            device_id=(lax.rem(me + offset(step) + count, count), row),
             device_id_type=MESH,
         )
         copy.wait_send()

time: 71 us -> 73 us (1.028)
  Pallas kernels: 58.8 us -> 60.7 us
    pallas_call x1, Pallas kernels: 34.8 us -> 36.7 us  [sweeps(): pl.pallas_call(functools.partial(exchange_kernel, count, layers), out_sha...]
where the time goes in v19:
time: 73 us; the launch traced here: 72.5 us
  Pallas kernels  60.7 us (83%)
  local copies, waits for them, and re-layouts  8.24 us (11%)
  matrix products  2.57 us (4%)
  other arithmetic  0.87 us (1%)
    pallas_call x1, Pallas kernels, sweeps(): pl.pallas_call(functools.partial(exchange_kernel, count, layers), out_sha...  36.7 us
    pallas_call x1, Pallas kernels, front_exchange(): pl.pallas_call(functools.partial(front_kernel, row_count, layer_count, de...  24 us
    unnamed x15, local copies, waits for them, and re-layouts  2.51 us
    another operation x1, local copies, waits for them, and re-layouts, shards(): return swept.reshape(2, layers, columns, rows, depth)  2.46 us
    dot_general x1, matrix products, shards(): jnp.einsum('lsp,lsc->lcp', projector, slot_back, preferred_element_type=j...  1.5 us

profile of v19, /device:TPU:32, one launch (start us, length us, event | category | flops | bytes accessed | tf_op | source)
XLA Modules:
  0.0 72.5 jit_solution(13685506591768938858)
XLA Ops:
  0.0 0.0 copy-start
  0.0 0.0 copy-start.3
  0.0 0.1 pad.7.clone
  0.1 0.6 copy-done.3
  0.8 0.0 copy-start.5
  0.8 0.7 copy-done.5
  1.4 0.1 copy.13
  1.5 0.1 broadcast_in_dim.32
  1.6 1.2 %reshape.14.block_ref = f32[2,32,1280]{2,1,0:T(8,128)S(1)} reshape(f32[2,32,2,640]{3,2,1,0:T(2,128)} %param.8) | data formatting | bytes 655360 | tf_op jit(solution)/shard_map/reshape | solution.py:470
  2.9 0.0 copy-start.1
  2.9 0.0 copy-done
  2.9 0.0 copy-start.4
  2.9 0.2 fusion.14
  3.1 0.5 copy-done.4
  3.6 0.9 %fusion.16.coef_ref = f32[2,32,256]{2,1,0:T(8,128)} fusion(f32[2,64,32]{1,2,0:T(8,128)S(1)} %fusion.14, s32[2,64]{1,0:T(2,128)S(1)} %copy-done.4), kind=kOutput, calls=%fused_computation.25 | convolution fusion | flops 12615680 | bytes 82432 | tf_op jit(solution)/shard_map/lsq,lsc->lcq/dot_general | solution.py:476
  4.5 0.0 copy-done.1
  4.5 0.3 copy.12
  4.7 0.3 reshape.15
  5.0 0.8 %maximum_maximum_fusion.pieces_ref = f32[32,24,128]{2,1,0:T(8,128)} fusion(f32[32,2,128]{2,1,0:T(2,128)S(1)} %broadcast_in_dim.32, f32[32,20,128]{2,1,0:T(8,128)S(1)} %reshape.15, f32[24]{0:T(128)S(1)} %pad.7.clone), kind=kLoop, calls=%fused_computation.3 | loop fusion | flops 196608 | bytes 753760 | tf_op jit(solution)/shard_map/concatenate | solution.py:437
  5.8 0.0 copy-start.2
  5.9 24.0 %shard_map.82 = (f32[2,32,1280]{2,1,0:T(8,128)}, f32[2,32,256]{2,1,0:T(8,128)}, f32[32,24,128]{2,1,0:T(8,128)}) custom-call(f32[2,32,1280]{2,1,0:T(8,128)} %copy-done.1, f32[2,32,256]{2,1,0:T(8,128)} %fusion.16.coef_ref, f32[32,24,128]{2,1,0:T(8,128)} %maximum_maximum_fusion.pieces_ref), custom_call_target="tpu_custom_call" | custom-call | tf_op jit(solution)/shard_map/pallas_call | solution.py:439
  29.9 0.0 copy-start.6
  29.9 0.0 copy-done.2
  29.9 0.7 copy-done.6
  30.5 1.5 %fusion = f32[32,2,1280]{2,0,1:T(8,128)S(1)} fusion(bf16[2,64,1280]{2,1,0:T(8,128)(2,1)S(1)} %copy-done, f32[2,32,1280]{2,1,0:T(8,128)} %get-tuple-element.8, f32[2,32,1280]{2,1,0:T(8,128)S(1)} %copy-done.2, f32[2,1280]{1,0:T(2,128)S(1)} %bitcast.11, pred[1280]{0:T(1024)(128)(4,1)S(1)} %get-tuple-element.11, pred[1280]{0:T(1024)(128)(4,1)S(1)} %get-tuple-element.12, ...), kind=kOutput, calls=%fused_computation.1 | convolution fusion | flops 14028800 | bytes 1394176 | tf_op jit(solution)/shard_map/lsp,lsc->lcp/dot_general | solution.py:486
  32.0 0.3 copy.14
  32.3 1.0 %reshape.16.ext_ref = f32[32,20,128]{2,1,0:T(8,128)} reshape(f32[32,2,1280]{2,1,0:T(2,128)S(1)} %copy.14) | data formatting | bytes 655360 | tf_op jit(solution)/shard_map/reshape | solution.py:313
  33.3 36.7 %shard_map.83 = f32[2,2,32,10,128]{4,3,2,1,0:T(8,128)} custom-call(f32[4]{0:T(128)} %nodes_ref.1, f32[4]{0:T(128)} %weights_ref.1, f32[32,20,128]{2,1,0:T(8,128)} %reshape.16.ext_ref, f32[32,24,128]{2,1,0:T(8,128)} %get-tuple-element.10.probe_ref), custom_call_target="tpu_custom_call" | custom-call | tf_op jit(solution)/shard_map/pallas_call | solution.py:315
  70.0 2.5 %reshape_reshape.3 = f32[2,2,32,2,640]{4,3,2,1,0:T(2,128)} reshape(f32[2,2,32,10,128]{4,3,2,1,0:T(8,128)} %shard_map.83) | data formatting | bytes 1310720 | tf_op jit(solution)/shard_map/reshape;reshape | solution.py:494
  (4 shorter events, 0.0 us)
Async XLA Ops:
  0.0 2.9 %copy-start = (bf16[2,64,1280]{2,1,0:T(8,128)(2,1)S(1)}, bf16[2,64,1280]{2,1,0:T(8,128)(2,1)}, u32[]{:S(2)}) copy-start(bf16[2,64,1280]{2,1,0:T(8,128)(2,1)} %param.10) | copy-start | bytes 983044
  0.0 0.7 %copy-start.3 = (f32[2,2,640]{2,1,0:T(2,128)S(1)}, f32[2,2,640]{2,1,0:T(2,128)}, u32[]{:S(2)}) copy-start(f32[2,2,640]{2,1,0:T(2,128)} %param.9) | copy-start | bytes 30724
  0.8 0.7 copy-start.5
  2.9 1.6 %copy-start.1 = (f32[2,32,1280]{2,1,0:T(8,128)}, f32[2,32,1280]{2,1,0:T(8,128)S(1)}, u32[]{:S(2)}) copy-start(f32[2,32,1280]{2,1,0:T(8,128)S(1)} %reshape.14.block_ref) | copy-start | bytes 983044
  2.9 0.7 %copy-start.4 = (s32[2,64]{1,0:T(2,128)S(1)}, s32[2,64]{1,0:T(2,128)}, u32[]{:S(2)}) copy-start(s32[2,64]{1,0:T(2,128)} %param.11) | copy-start | bytes 1540
  5.8 24.0 %copy-start.2 = (f32[2,32,1280]{2,1,0:T(8,128)S(1)}, f32[2,32,1280]{2,1,0:T(8,128)}, u32[]{:S(2)}) copy-start(f32[2,32,1280]{2,1,0:T(8,128)} %copy-done.1) | copy-start | bytes 983044
  29.9 0.7 copy-start.6
